TPU v7x, 32 devices: a whole 2x2x4 slice. The times are simulated.
32 devices in a mesh: groups: 2 (over x), ctx: 16 (over z, y, core).
Axes of the slice: x: 2, y: 2, z: 4, core: 2. Of those that a mesh axis runs over, the one named last changes fastest.
Arguments:
- raster_tokens: bfloat16 [4096, 1024], P(('groups', 'ctx')), parts along dimension 0, may hold values from -45 to 45
- hilbert_perm: int32 [4096], P(('groups', 'ctx')), parts along dimension 0, may hold values from 0 to 2047, as said below
- neighbors: int32 [32, 5], P(('groups', 'ctx')), parts along dimension 0, may hold values from 0 to 15, as said below
- neighbor_counts: int32 [32], P(('groups', 'ctx')), parts along dimension 0, may hold values from 1 to 5, as said below
- norm_gain: float32 [1024], replicated, may hold values from 0.1 to 1.9
- w_qkv: bfloat16 [1024, 3072], replicated, may hold values from -0.8125 to 0.8125
- w_out: bfloat16 [1024, 1024], replicated, may hold values from -0.5 to 0.5
- cotangent: bfloat16 [4096, 1024], P(('groups', 'ctx')), parts along dimension 0, may hold values from -6 to 6
Outputs:
- layer_out: bfloat16 [4096, 1024], P(('groups', 'ctx')), parts along dimension 0
- grad_tokens: bfloat16 [4096, 1024], P(('groups', 'ctx')), parts along dimension 0
- grad_w_out: float32 [2048, 1024], P(('groups', 'ctx')), parts along dimension 0
- grad_gain: float32 [2048], P('groups'), parts along dimension 0
There are 2 independent parts, one for each index of `groups`. A program takes and returns all parts, laid end to end along the dimension named above; an argument that names none is the same for every part. Nothing has to cross between parts.
Inputs may be any that keep to these rules, and one draw needn't show every extreme that they name: `hilbert_perm`: A permutation. Every 128 consecutive positions of the Hilbert order take exactly 8 tokens from every 128 consecutive raster tokens. `neighbors`: row b starts with b, followed by distinct blocks other than b at a distance of at most 4; entries from slot neighbor_counts[b] on equal b. `neighbor_counts`: the block itself is counted.
All inputs are finite; a program needn't handle non-finite values.
Results may differ from a plain program's by a relative error of at most 0.02.
The roundings to bfloat16 on the way count: a program that leaves them out, or rounds other values in their place, can miss the bound.
Values may be sent and summed in bfloat16 or wider, within the bound.
No kernel may reach another device: no remote copies, remote signals or barrier semaphores. Data moves between devices by JAX's collectives and lax.ppermute only.
A program may use at most 128 MiB of HBM per device.

v0:
```python
import jax
import jax.numpy as jnp
from jax import lax
from jax.sharding import PartitionSpec as P

HEADS = 16
BLOCK = 128
REACH = 4


EPS = 1e-06
FAR = -1e30


def from_behind(block, axis, distance):
    devices = range(lax.axis_size(axis))
    route = [(i - distance, i) for i in devices if i - distance in devices]
    return lax.ppermute(block, axis, route)


def softmax_probs(heads_q, heads_k, counts, score_scale):
    scores = (
        jnp.einsum("sqhd,skhd->shqk", heads_q, heads_k, preferred_element_type=jnp.float32)
        * score_scale
    )
    slot_of = jnp.arange(heads_k.shape[1]) // BLOCK
    usable = slot_of[None, :] < counts[:, None]
    scores = jnp.where(usable[:, None, None, :], scores, FAR)
    row_max = jnp.max(scores, axis=-1, keepdims=True)
    shifted = jnp.exp(scores - row_max)
    return shifted / jnp.sum(shifted, axis=-1, keepdims=True)


def per_device(
    raster_tokens, hilbert_perm, neighbors, neighbor_counts, norm_gain, w_qkv, w_out, cotangent
):
    axis_size = lax.axis_size("ctx")
    my_index = lax.axis_index("ctx")
    tok_rows, model_width = raster_tokens.shape
    per_peer = tok_rows // axis_size
    per_dev = tok_rows // BLOCK
    reach_dev = (REACH + per_dev - 1) // per_dev
    head_dim = model_width // HEADS
    score_scale = head_dim ** (-0.5)
    norm_scale = (tok_rows * axis_size) ** (-0.5)
    source_dev = hilbert_perm // tok_rows
    local_row = hilbert_perm % tok_rows
    sorted_rows = jnp.argsort(source_dev, stable=True)
    wanted = local_row[sorted_rows].reshape(axis_size, per_peer)
    requested = lax.all_to_all(wanted, "ctx", split_axis=0, concat_axis=0, tiled=True)
    requested_flat = requested.reshape(-1)
    outgoing = raster_tokens[requested_flat].reshape(axis_size, per_peer, model_width)
    arrived = lax.all_to_all(outgoing, "ctx", split_axis=0, concat_axis=0, tiled=True)
    ordered = (
        jnp.zeros_like(raster_tokens).at[sorted_rows].set(arrived.reshape(tok_rows, model_width))
    )
    ordered_f = ordered.astype(jnp.float32)
    inv_rms = lax.rsqrt(jnp.mean(ordered_f * ordered_f, axis=-1, keepdims=True) + EPS)
    normed = (ordered_f * inv_rms * norm_gain).astype(jnp.bfloat16)
    projected = jnp.dot(normed, w_qkv, preferred_element_type=jnp.float32).astype(jnp.bfloat16)
    queries = projected[:, :model_width]
    keys_vals = projected[:, model_width:]
    kv_weight = w_qkv[:, model_width:]
    from_lower = []
    from_upper = []
    carry_low = normed
    carry_high = normed
    for distance in range(reach_dev):
        carry_low = from_behind(carry_low, "ctx", 1)
        carry_high = from_behind(carry_high, "ctx", -1)
        from_lower.append(carry_low)
        from_upper.append(carry_high)
    remote_low = [
        jnp.dot(remote_piece, kv_weight, preferred_element_type=jnp.float32).astype(jnp.bfloat16)
        for remote_piece in from_lower
    ]
    remote_high = [
        jnp.dot(remote_piece, kv_weight, preferred_element_type=jnp.float32).astype(jnp.bfloat16)
        for remote_piece in from_upper
    ]
    window = jnp.concatenate(remote_low[::-1] + [keys_vals] + remote_high, axis=0)
    window_blocks = window.reshape(-1, BLOCK, 2 * model_width)
    slot_index = neighbors - (my_index - reach_dev) * per_dev
    gathered = window_blocks[slot_index].reshape(per_dev, -1, 2 * model_width)
    heads_k = gathered[:, :, :model_width].reshape(per_dev, -1, HEADS, head_dim)
    heads_v = gathered[:, :, model_width:].reshape(per_dev, -1, HEADS, head_dim)
    heads_q = queries.reshape(per_dev, BLOCK, HEADS, head_dim)
    weights_f = softmax_probs(heads_q, heads_k, neighbor_counts, score_scale)
    probs_b = weights_f.astype(jnp.bfloat16)
    attended = jnp.einsum("shqk,skhd->sqhd", probs_b, heads_v, preferred_element_type=jnp.float32)
    attended = attended.reshape(tok_rows, model_width).astype(jnp.bfloat16)
    projected_out = jnp.dot(attended, w_out, preferred_element_type=jnp.float32)
    layer_out = (ordered_f + projected_out).astype(jnp.bfloat16)
    grad_w_out = None
    d_attended = jnp.dot(cotangent, w_out.T, preferred_element_type=jnp.float32).astype(
        jnp.bfloat16
    )
    d_heads = d_attended.reshape(per_dev, BLOCK, HEADS, head_dim)
    d_probs = jnp.einsum("sqhd,skhd->shqk", d_heads, heads_v, preferred_element_type=jnp.float32)
    row_dots = jnp.sum(d_probs * weights_f, axis=-1, keepdims=True)
    d_scores = (weights_f * (d_probs - row_dots) * score_scale).astype(jnp.bfloat16)
    d_query = jnp.einsum("shqk,skhd->sqhd", d_scores, heads_k, preferred_element_type=jnp.float32)
    d_query = d_query.reshape(tok_rows, model_width).astype(jnp.bfloat16)
    d_keys = jnp.einsum("shqk,sqhd->skhd", d_scores, heads_q, preferred_element_type=jnp.float32)
    d_vals = jnp.einsum("shqk,sqhd->skhd", probs_b, d_heads, preferred_element_type=jnp.float32)
    contrib = jnp.concatenate(
        [d_keys.reshape(-1, BLOCK, model_width), d_vals.reshape(-1, BLOCK, model_width)], axis=-1
    )
    summed = jnp.zeros(window_blocks.shape, jnp.float32).at[slot_index.reshape(-1)].add(contrib)
    partials = summed.astype(jnp.bfloat16)
    accum = partials[reach_dev].astype(jnp.float32)
    for distance in range(1, reach_dev + 1):
        accum = accum + from_behind(partials[reach_dev + distance], "ctx", distance).astype(
            jnp.float32
        )
        accum = accum + from_behind(partials[reach_dev - distance], "ctx", -distance).astype(
            jnp.float32
        )
    d_kv = accum.astype(jnp.bfloat16)
    d_proj = jnp.concatenate([d_query, d_kv], axis=-1)
    d_normed = jnp.dot(d_proj, w_qkv.T, preferred_element_type=jnp.float32)
    gain_term = jnp.sum(d_normed * ordered_f * inv_rms, axis=0)
    grad_gain = lax.psum(gain_term, "ctx") * norm_scale
    scaled = d_normed * norm_gain
    d_ordered = (
        cotangent.astype(jnp.float32)
        + inv_rms * scaled
        - ordered_f * inv_rms**3 * jnp.mean(scaled * ordered_f, axis=-1, keepdims=True)
    )
    d_ordered = d_ordered.astype(jnp.bfloat16)
    leaving = d_ordered[sorted_rows].reshape(axis_size, per_peer, model_width)
    returned = lax.all_to_all(leaving, "ctx", split_axis=0, concat_axis=0, tiled=True)
    grad_tokens = (
        jnp.zeros_like(raster_tokens)
        .at[requested_flat]
        .set(returned.reshape(tok_rows, model_width))
    )
    grad_w_out = (
        lax.psum_scatter(
            lax.dot_general(
                attended, cotangent, (((0,), (0,)), ((), ())), preferred_element_type=jnp.float32
            ),
            "ctx",
            scatter_dimension=0,
            tiled=True,
        )
        * norm_scale
    )
    return (layer_out, grad_tokens, grad_w_out, grad_gain)


def solution(mesh):
    placed = (
        P(("groups", "ctx"), None),
        P(("groups", "ctx")),
        P(("groups", "ctx"), None),
        P(("groups", "ctx")),
        P(),
        P(),
        P(),
        P(("groups", "ctx"), None),
    )
    return jax.shard_map(
        per_device,
        mesh=mesh,
        in_specs=placed,
        out_specs=(
            P(("groups", "ctx"), None),
            P(("groups", "ctx"), None),
            P(("groups", "ctx"), None),
            P("groups"),
        ),
        check_vma=False,
    )
```

profile of v0, /device:TPU:0, one launch (start us, length us, event | category | flops | bytes accessed | tf_op | source)
XLA Modules:
  0.0 316.0 jit_solution(17017370256104363028)
XLA Ops:
  8.0 2.5 sort.17
  11.9 13.6 %all_to_all.19 = s32[16,1,8]{2,1,0:T(1,128)S(1)} all-to-all(s32[16,1,8]{2,1,0:T(1,128)S(1)} %bitcast.117), channel_id=1, replica_groups=mesh['groups'=2,'ctx'=16] {'ctx'}, dimensions={0} | all-to-all | bytes 1024 | tf_op jit(solution)/shard_map/all_to_all | solution.py:50
  26.9 2.0 gather_fusion.1
  28.9 12.6 %all_to_all.20 = bf16[16,8,1024]{2,1,0:T(8,128)(2,1)S(1)} all-to-all(bf16[16,8,1024]{2,1,0:T(8,128)(2,1)S(1)} %bitcast.109), channel_id=1, replica_groups=mesh['groups'=2,'ctx'=16] {'ctx'}, dimensions={0} | all-to-all | bytes 524288 | tf_op jit(solution)/shard_map/all_to_all | solution.py:53
  43.7 1.8 collective-permute-start
  46.8 4.6 %collective-permute-start.1 = (bf16[128,1024]{1,0:T(8,128)(2,1)S(1)}, bf16[128,1024]{1,0:T(8,128)(2,1)}, u32[]{:S(2)}, u32[]{:S(2)}) collective-permute-start(bf16[128,1024]{1,0:T(8,128)(2,1)S(1)} %collective-permute-done), channel_id=1, source_target_pairs={{0,1},{1,2},{2,3},{3,4},{4,5},{5,6},{6,7},{7,8},{8,9},{9,10},{10,1... | collective-permute-start | bytes 786440 | tf_op jit(solution)/shard_map/ppermute | solution.py:18
  52.7 6.4 %collective-permute-start.2 = (bf16[128,1024]{1,0:T(8,128)(2,1)}, bf16[128,1024]{1,0:T(8,128)(2,1)}, u32[]{:S(2)}, u32[]{:S(2)}) collective-permute-start(bf16[128,1024]{1,0:T(8,128)(2,1)} %collective-permute-done.1), channel_id=1, source_target_pairs={{0,1},{1,2},{2,3},{3,4},{4,5},{5,6},{6,7},{7,8},{8,9},{9,10},{10,1... | collective-permute-start | bytes 786440 | tf_op jit(solution)/shard_map/ppermute | solution.py:18
  61.1 6.1 %collective-permute-start.3 = (bf16[128,1024]{1,0:T(8,128)(2,1)}, bf16[128,1024]{1,0:T(8,128)(2,1)}, u32[]{:S(2)}, u32[]{:S(2)}) collective-permute-start(bf16[128,1024]{1,0:T(8,128)(2,1)} %collective-permute-done.2), channel_id=1, source_target_pairs={{0,1},{1,2},{2,3},{3,4},{4,5},{5,6},{6,7},{7,8},{8,9},{9,10},{10,1... | collective-permute-start | bytes 786440 | tf_op jit(solution)/shard_map/ppermute | solution.py:18
  67.2 3.8 %convolution_convert_fusion = bf16[128,3072]{1,0:T(8,128)(2,1)S(1)} fusion(bf16[128,1024]{1,0:T(8,128)(2,1)S(1)} %fusion.60, bf16[1024,3072]{1,0:T(8,128)(2,1)} %param.13), kind=kOutput, calls=%fused_computation.16 | convolution fusion | flops 805699584 | bytes 7340032 | tf_op jit(solution)/shard_map/dot_general | solution.py:60
  73.2 3.1 fusion.24
  76.3 3.1 fusion.23
  79.5 3.0 fusion.22
  84.2 1.7 fusion.19
  85.9 1.7 fusion.18
  88.4 2.1 copy-done.3
  90.5 4.7 %gather_fusion.2 = bf16[5,128,2048]{2,1,0:T(8,128)(2,1)} fusion(bf16[9,128,2048]{2,1,0:T(8,128)(2,1)} %bitcast.106, s32[1024]{0:T(1024)S(1)} %pad_clamp_fusion), kind=kCustom, calls=%fused_computation.2 | custom fusion | bytes 5242900 | tf_op jit(solution)/shard_map/gather | solution.py:84
  95.2 3.5 %fusion.89 = (bf16[1,640,1024]{2,1,0:T(8,128)(2,1)}, bf16[1,640,1024]{2,1,0:T(8,128)(2,1)}) fusion(bf16[1,640,2048]{2,1,0:T(8,128)(2,1)} %bitcast.103), kind=kLoop, calls=%fused_computation.138 | loop fusion | bytes 5242880 | tf_op jit(solution)/shard_map/slice | solution.py:85
  98.7 2.5 copy.33
  101.1 2.5 copy.32
  103.6 5.5 %fusion.90 = (f32[16,128]{1,0:T(8,128)S(1)}, f32[16,128,640]{2,1,0:T(8,128)}) fusion(pred[640]{0:T(1024)(128)(4,1)S(1)} %fusion.75, bf16[128,16,64]{0,2,1:T(8,128)(2,1)S(1)} %bitcast.114, bf16[640,16,64]{0,2,1:T(8,128)(2,1)} %bitcast.107), kind=kOutput, calls=%fused_computation.139 | convolution fusion | flops 173015680 | bytes 6824576 | tf_op jit(solution)/shard_map/sub | solution.py:30
  109.2 4.1 %fusion.31 = bf16[16,64,128]{2,1,0:T(8,128)(2,1)S(1)} fusion(bf16[640,16,64]{0,2,1:T(8,128)(2,1)} %bitcast.104, f32[16,128,640]{2,1,0:T(8,128)} %get-tuple-element.23, f32[16,128]{1,0:T(8,128)S(1)} %get-tuple-element.22), kind=kOutput, calls=%fused_computation.47 | convolution fusion | flops 170524672 | bytes 6823936 | tf_op jit(solution)/shard_map/shqk,skhd->sqhd/dot_general | solution.py:90
  113.3 2.7 fusion.92
  117.0 4.6 %convolution_bitcast_fusion = f32[1,640,16,64]{1,3,2,0:T(8,128)} fusion(bf16[128,16,64]{0,2,1:T(8,128)(2,1)S(1)} %bitcast.112, f32[16,128,640]{2,1,0:T(8,128)} %get-tuple-element.23, f32[16,128]{1,0:T(8,128)S(1)} %get-tuple-element.22), kind=kOutput, calls=%fused_computation.42 | convolution fusion | flops 170393600 | bytes 8134656 | tf_op jit(solution)/shard_map/shqk,sqhd->skhd/dot_general | solution.py:105
  121.6 4.4 %reshape.226 = f32[5,128,1024]{1,0,2:T(8,128)} reshape(f32[1,640,16,64]{1,3,2,0:T(8,128)} %convolution_bitcast_fusion) | data formatting | bytes 5242880 | tf_op jit(solution)/shard_map/reshape | solution.py:107
  126.0 4.6 %fusion.91 = f32[16,128,640]{2,1,0:T(8,128)} fusion(bf16[128,16,64]{0,2,1:T(8,128)(2,1)S(1)} %bitcast.113, bf16[640,16,64]{0,2,1:T(8,128)(2,1)} %bitcast.105), kind=kOutput, calls=%fused_computation.140 | convolution fusion | flops 167772160 | bytes 6815744 | tf_op jit(solution)/shard_map/sqhd,skhd->shqk/dot_general | solution.py:99
  130.6 19.2 %fusion.25 = f32[1,640,16,64]{1,3,2,0:T(8,128)} fusion(bf16[128,16,64]{0,2,1:T(8,128)(2,1)S(1)} %bitcast.115, f32[16,128,640]{2,1,0:T(8,128)} %fusion.91, f32[16,128,640]{2,1,0:T(8,128)} %get-tuple-element.23, f32[16,128]{1,0:T(8,128)S(1)} %get-tuple-element.22), kind=kOutput, calls=%fused_computation.41 | convolution fusion | flops 176949888 | bytes 13377536 | tf_op jit(solution)/shard_map/shqk,sqhd->skhd/dot_general | solution.py:104
  149.9 4.4 %reshape.225 = f32[5,128,1024]{1,0,2:T(8,128)} reshape(f32[1,640,16,64]{1,3,2,0:T(8,128)} %fusion.25) | data formatting | bytes 5242880 | tf_op jit(solution)/shard_map/reshape | solution.py:107
  154.3 6.7 %pad_maximum_fusion = f32[5,128,2048]{1,0,2:T(8,128)} fusion(f32[5,128,1024]{1,0,2:T(8,128)} %reshape.226, f32[5,128,1024]{1,0,2:T(8,128)} %reshape.225), kind=kLoop, calls=%fused_computation.9 | loop fusion | flops 1310720 | bytes 10485760 | tf_op jit(solution)/shard_map/concatenate | solution.py:106
  161.0 7.9 %copy.30 = f32[5,128,2048]{2,1,0:T(8,128)} copy(f32[5,128,2048]{1,0,2:T(8,128)} %pad_maximum_fusion) | data formatting | bytes 10485760 | tf_op jit(solution)/shard_map/concatenate | solution.py:106
  168.9 4.8 %broadcast_in_dim.22 = f32[9,128,2048]{2,1,0:T(8,128)} broadcast(f32[]{:T(128)} %constant.63.clone.1), dimensions={} | broadcast | bytes 9437188 | tf_op jit(solution)/shard_map/broadcast_in_dim | solution.py:109
  173.7 11.9 %scatter_fusion = f32[9,128,2048]{2,1,0:T(8,128)} fusion(f32[9,128,2048]{2,1,0:T(8,128)} %broadcast_in_dim.22, s32[5]{0:T(128)S(1)} %fusion.81, f32[5,128,2048]{2,1,0:T(8,128)} %copy.30), kind=kCustom, calls=%fused_computation.5 | custom fusion | flops 1310720 | bytes 15728660 | tf_op jit(solution)/shard_map/scatter-add | solution.py:109
  185.7 4.4 %convert_element_type.137 = bf16[9,128,2048]{2,1,0:T(8,128)(2,1)S(1)} convert(f32[9,128,2048]{2,1,0:T(8,128)} %scatter_fusion) | non-fusion elementwise | flops 2359296 | bytes 14155776 | tf_op jit(solution)/shard_map/convert_element_type | solution.py:110
  190.1 2.1 copy-done.1
  192.2 1.6 slice_bitcast_fusion.7
  193.8 5.9 %collective-permute-start.8 = (bf16[128,2048]{1,0:T(8,128)(2,1)S(1)}, bf16[128,2048]{1,0:T(8,128)(2,1)}, u32[]{:S(2)}, u32[]{:S(2)}) collective-permute-start(bf16[128,2048]{1,0:T(8,128)(2,1)S(1)} %get-tuple-element.8), channel_id=1, source_target_pairs={{0,1},{1,2},{2,3},{3,4},{4,5},{5,6},{6,7},{7,8},{8,9},{9,10},{10,1... | collective-permute-start | bytes 1572872 | tf_op jit(solution)/shard_map/ppermute | solution.py:18
  201.0 7.6 %collective-permute-start.14 = (bf16[128,2048]{1,0:T(8,128)(2,1)S(1)}, bf16[128,2048]{1,0:T(8,128)(2,1)}, u32[]{:S(2)}, u32[]{:S(2)}) collective-permute-start(bf16[128,2048]{1,0:T(8,128)(2,1)S(1)} %get-tuple-element.10), channel_id=1, source_target_pairs={{0,4},{1,5},{2,6},{3,7},{4,8},{5,9},{6,10},{7,11},{8,12},{9,13},{1... | collective-permute-start | bytes 1572872 | tf_op jit(solution)/shard_map/ppermute | solution.py:18
  210.0 6.2 %collective-permute-start.12 = (bf16[128,2048]{1,0:T(8,128)(2,1)}, bf16[128,2048]{1,0:T(8,128)(2,1)}, u32[]{:S(2)}, u32[]{:S(2)}) collective-permute-start(bf16[128,2048]{1,0:T(8,128)(2,1)} %get-tuple-element.12), channel_id=1, source_target_pairs={{0,3},{1,4},{2,5},{3,6},{4,7},{5,8},{6,9},{7,10},{8,11},{9,12},{10... | collective-permute-start | bytes 1572872 | tf_op jit(solution)/shard_map/ppermute | solution.py:18
  218.6 4.3 %collective-permute-start.10 = (bf16[128,2048]{1,0:T(8,128)(2,1)}, bf16[128,2048]{1,0:T(8,128)(2,1)}, u32[]{:S(2)}, u32[]{:S(2)}) collective-permute-start(bf16[128,2048]{1,0:T(8,128)(2,1)} %get-tuple-element.14), channel_id=1, source_target_pairs={{0,2},{1,3},{2,4},{3,5},{4,6},{5,7},{6,8},{7,9},{8,10},{9,11},{10,... | collective-permute-start | bytes 1572872 | tf_op jit(solution)/shard_map/ppermute | solution.py:18
  224.2 19.1 %fusion.34 = bf16[16,64,128]{2,1,0:T(8,128)(2,1)S(1)} fusion(bf16[640,16,64]{0,2,1:T(8,128)(2,1)} %bitcast.108, f32[16,128,640]{2,1,0:T(8,128)} %fusion.91, f32[16,128,640]{2,1,0:T(8,128)} %get-tuple-element.23, f32[16,128]{1,0:T(8,128)S(1)} %get-tuple-element.22), kind=kOutput, calls=%fused_computation.48 | convolution fusion | flops 177080960 | bytes 12066816 | tf_op jit(solution)/shard_map/shqk,skhd->sqhd/dot_general | solution.py:102
  243.5 2.2 collective-permute-done.12
  245.7 9.1 %collective-permute-done.10 = bf16[128,2048]{1,0:T(8,128)(2,1)} collective-permute-done((bf16[128,2048]{1,0:T(8,128)(2,1)}, bf16[128,2048]{1,0:T(8,128)(2,1)}, u32[]{:S(2)}, u32[]{:S(2)}) %collective-permute-start.10) | collective-permute-done | bytes 524320 | tf_op jit(solution)/shard_map/ppermute | solution.py:18
  254.8 3.1 fusion.45
  257.9 5.1 %fusion.66 = (f32[1024]{0:T(1024)S(1)}, f32[128]{0:T(128)S(1)}, f32[128,1024]{1,0:T(8,128)S(1)}) fusion(bf16[128,1024]{1,0:T(8,128)(2,1)S(1)} %scatter_custom_fusion, f32[128]{0:T(128)S(1)} %get-tuple-element.19, f32[1024]{0:T(1024)S(1)} %copy-done.6, bf16[1024,3072]{1,0:T(8,128)(2,1)} %param.13, bf16[128,2048]{1,0:T(8,128)(2,1)S(1)} %fusion.45, ...), kind=kOutput, calls=%fused_computation.85 | convolution fusion | flops 807795584 | bytes 7873536 | tf_op jit(solution)/shard_map/dot_general | solution.py:121
  263.3 1.6 gather_fusion.3
  264.9 5.2 %all-to-all-start.2 = ((bf16[16,8,1024]{2,1,0:T(8,128)(2,1)}), bf16[16,8,1024]{2,1,0:T(8,128)(2,1)S(1)}, u32[]{:S(2)}, u32[]{:S(2)}) async-start(bf16[16,8,1024]{2,1,0:T(8,128)(2,1)} %bitcast.33), calls=%async_computation.2 | async-start | bytes 524288 | tf_op jit(solution)/shard_map/all_to_all | solution.py:132
  271.3 33.8 %psum.7 = f32[1024]{0:T(1024)S(1)} all-reduce(f32[1024]{0:T(1024)S(1)} %get-tuple-element.6), channel_id=1, replica_groups=mesh['groups'=2,'ctx'=16] {'ctx'}, use_global_device_ids=true, to_apply=%region_11.12 | all-reduce | flops 1024 | bytes 8192 | tf_op jit(solution)/shard_map/psum | solution.py:123
  305.7 1.8 scatter_custom_fusion.2
  307.5 1.7 broadcast_multiply_fusion
  (85 shorter events, 23.8 us)
Async XLA Ops:
  7.2 108.8 %copy-start = (bf16[1024,1024]{1,0:T(8,128)(2,1)S(1)}, bf16[1024,1024]{1,0:T(8,128)(2,1)}, u32[]{:S(2)}) copy-start(bf16[1024,1024]{1,0:T(8,128)(2,1)} %param.14) | copy-start | bytes 6291460
  7.2 51.9 %copy-start.11 = (s32[1,5]{1,0:T(1,128)S(1)}, s32[1,5]{1,0:T(1,128)}, u32[]{:S(2)}) copy-start(s32[1,5]{1,0:T(1,128)} %param.10) | copy-start | bytes 64
  7.2 300.3 %reduce-scatter.2.cloned.1.call-start = ((), (), s32[]{:S(2)}) async-start(), calls=%async_computation.4 | async-start | bytes 4456448 | tf_op jit(solution)/shard_map/reduce_scatter | solution.py:139
  43.7 3.1 collective-permute-start
  45.5 5.9 %collective-permute-start.4 = (bf16[128,1024]{1,0:T(8,128)(2,1)S(1)}, bf16[128,1024]{1,0:T(8,128)(2,1)S(1)}, u32[]{:S(2)}, u32[]{:S(2)}) collective-permute-start(bf16[128,1024]{1,0:T(8,128)(2,1)S(1)} %fusion.60), channel_id=1, source_target_pairs={{1,0},{2,1},{3,2},{4,3},{5,4},{6,5},{7,6},{8,7},{9,8},{10,9},{11,1... | collective-permute-start | bytes 786440 | tf_op jit(solution)/shard_map/ppermute | solution.py:18
  46.8 14.3 %copy-start.9 = (bf16[128,1024]{1,0:T(8,128)(2,1)}, bf16[128,1024]{1,0:T(8,128)(2,1)S(1)}, u32[]{:S(2)}) copy-start(bf16[128,1024]{1,0:T(8,128)(2,1)S(1)} %collective-permute-done) | copy-start | bytes 786436
  46.8 5.9 %collective-permute-start.1 = (bf16[128,1024]{1,0:T(8,128)(2,1)S(1)}, bf16[128,1024]{1,0:T(8,128)(2,1)}, u32[]{:S(2)}, u32[]{:S(2)}) collective-permute-start(bf16[128,1024]{1,0:T(8,128)(2,1)S(1)} %collective-permute-done), channel_id=1, source_target_pairs={{0,1},{1,2},{2,3},{3,4},{4,5},{5,6},{6,7},{7,8},{8,9},{9,10},{10,1... | collective-permute-start | bytes 786440 | tf_op jit(solution)/shard_map/ppermute | solution.py:18
  51.4 9.7 %copy-start.7 = (bf16[128,1024]{1,0:T(8,128)(2,1)}, bf16[128,1024]{1,0:T(8,128)(2,1)S(1)}, u32[]{:S(2)}) copy-start(bf16[128,1024]{1,0:T(8,128)(2,1)S(1)} %collective-permute-done.4) | copy-start | bytes 786436
  51.4 8.4 %collective-permute-start.5 = (bf16[128,1024]{1,0:T(8,128)(2,1)S(1)}, bf16[128,1024]{1,0:T(8,128)(2,1)}, u32[]{:S(2)}, u32[]{:S(2)}) collective-permute-start(bf16[128,1024]{1,0:T(8,128)(2,1)S(1)} %collective-permute-done.4), channel_id=1, source_target_pairs={{1,0},{2,1},{3,2},{4,3},{5,4},{6,5},{7,6},{8,7},{9,8},{10,9},{11,1... | collective-permute-start | bytes 786440 | tf_op jit(solution)/shard_map/ppermute | solution.py:18
  52.7 8.4 %collective-permute-start.2 = (bf16[128,1024]{1,0:T(8,128)(2,1)}, bf16[128,1024]{1,0:T(8,128)(2,1)}, u32[]{:S(2)}, u32[]{:S(2)}) collective-permute-start(bf16[128,1024]{1,0:T(8,128)(2,1)} %collective-permute-done.1), channel_id=1, source_target_pairs={{0,1},{1,2},{2,3},{3,4},{4,5},{5,6},{6,7},{7,8},{8,9},{9,10},{10,1... | collective-permute-start | bytes 786440 | tf_op jit(solution)/shard_map/ppermute | solution.py:18
  59.8 12.1 %collective-permute-start.6 = (bf16[128,1024]{1,0:T(8,128)(2,1)}, bf16[128,1024]{1,0:T(8,128)(2,1)}, u32[]{:S(2)}, u32[]{:S(2)}) collective-permute-start(bf16[128,1024]{1,0:T(8,128)(2,1)} %collective-permute-done.5), channel_id=1, source_target_pairs={{1,0},{2,1},{3,2},{4,3},{5,4},{6,5},{7,6},{8,7},{9,8},{10,9},{11,1... | collective-permute-start | bytes 786440 | tf_op jit(solution)/shard_map/ppermute | solution.py:18
  61.1 12.0 %collective-permute-start.3 = (bf16[128,1024]{1,0:T(8,128)(2,1)}, bf16[128,1024]{1,0:T(8,128)(2,1)}, u32[]{:S(2)}, u32[]{:S(2)}) collective-permute-start(bf16[128,1024]{1,0:T(8,128)(2,1)} %collective-permute-done.2), channel_id=1, source_target_pairs={{0,1},{1,2},{2,3},{3,4},{4,5},{5,6},{6,7},{7,8},{8,9},{9,10},{10,1... | collective-permute-start | bytes 786440 | tf_op jit(solution)/shard_map/ppermute | solution.py:18
  71.9 15.8 %collective-permute-start.7 = (bf16[128,1024]{1,0:T(8,128)(2,1)}, bf16[128,1024]{1,0:T(8,128)(2,1)S(1)}, u32[]{:S(2)}, u32[]{:S(2)}) collective-permute-start(bf16[128,1024]{1,0:T(8,128)(2,1)} %collective-permute-done.6), channel_id=1, source_target_pairs={{1,0},{2,1},{3,2},{4,3},{5,4},{6,5},{7,6},{8,7},{9,8},{10,9},{11,1... | collective-permute-start | bytes 786440 | tf_op jit(solution)/shard_map/ppermute | solution.py:18
  73.2 9.4 %slice-start = ((s8[6291456]{0:T(1024)(128)(4,1)}), s8[4194304]{0:T(1024)(128)(4,1)S(1)}, s32[]{:S(2)}) async-start(s8[6291456]{0:T(1024)(128)(4,1)} %bitcast.101), calls=%async_computation.5 | async-start | bytes 8388608
  76.3 6.2 %slice-start.1 = ((s8[6291456]{0:T(1024)(128)(4,1)}), s8[2097152]{0:T(1024)(128)(4,1)S(1)}, s32[]{:S(2)}) async-start(s8[6291456]{0:T(1024)(128)(4,1)} %bitcast.101), calls=%async_computation.6 | async-start | bytes 4194304
  76.3 6.2 %copy-start.10 = (bf16[128,1024]{1,0:T(8,128)(2,1)S(1)}, bf16[128,1024]{1,0:T(8,128)(2,1)}, u32[]{:S(2)}) copy-start(bf16[128,1024]{1,0:T(8,128)(2,1)} %copy-done.9) | copy-start | bytes 786436
  82.5 1.0 copy-start.8
  88.4 2.1 copy-start.3
  95.2 8.4 %copy-start.4 = (bf16[128,1024]{0,1:T(8,128)(2,1)S(1)}, bf16[128,1024]{0,1:T(8,128)(2,1)}, u32[]{:S(2)}) copy-start(bf16[128,1024]{0,1:T(8,128)(2,1)} %copy.27) | copy-start | bytes 786436
  109.1 4.2 %copy-start.2 = (bf16[128,1024]{1,0:T(8,128)(2,1)S(1)}, bf16[128,1024]{1,0:T(8,128)(2,1)}, u32[]{:S(2)}) copy-start(bf16[128,1024]{1,0:T(8,128)(2,1)} %param.15) | copy-start | bytes 786436
  126.0 4.6 %copy-start.5 = (bf16[128,1024]{0,1:T(8,128)(2,1)S(1)}, bf16[128,1024]{0,1:T(8,128)(2,1)}, u32[]{:S(2)}) copy-start(bf16[128,1024]{0,1:T(8,128)(2,1)} %copy.27) | copy-start | bytes 786436
  190.1 2.1 copy-start.1
  193.8 22.4 %collective-permute-start.8 = (bf16[128,2048]{1,0:T(8,128)(2,1)S(1)}, bf16[128,2048]{1,0:T(8,128)(2,1)}, u32[]{:S(2)}, u32[]{:S(2)}) collective-permute-start(bf16[128,2048]{1,0:T(8,128)(2,1)S(1)} %get-tuple-element.8), channel_id=1, source_target_pairs={{0,1},{1,2},{2,3},{3,4},{4,5},{5,6},{6,7},{7,8},{8,9},{9,10},{10,1... | collective-permute-start | bytes 1572872 | tf_op jit(solution)/shard_map/ppermute | solution.py:18
  199.7 18.9 %collective-permute-start.15 = (bf16[128,2048]{1,0:T(8,128)(2,1)S(1)}, bf16[128,2048]{1,0:T(8,128)(2,1)}, u32[]{:S(2)}, u32[]{:S(2)}) collective-permute-start(bf16[128,2048]{1,0:T(8,128)(2,1)S(1)} %get-tuple-element.9), channel_id=1, source_target_pairs={{4,0},{5,1},{6,2},{7,3},{8,4},{9,5},{10,6},{11,7},{12,8},{13,9},{1... | collective-permute-start | bytes 1572872 | tf_op jit(solution)/shard_map/ppermute | solution.py:18
  201.0 21.9 %collective-permute-start.14 = (bf16[128,2048]{1,0:T(8,128)(2,1)S(1)}, bf16[128,2048]{1,0:T(8,128)(2,1)}, u32[]{:S(2)}, u32[]{:S(2)}) collective-permute-start(bf16[128,2048]{1,0:T(8,128)(2,1)S(1)} %get-tuple-element.10), channel_id=1, source_target_pairs={{0,4},{1,5},{2,6},{3,7},{4,8},{5,9},{6,10},{7,11},{8,12},{9,13},{1... | collective-permute-start | bytes 1572872 | tf_op jit(solution)/shard_map/ppermute | solution.py:18
  208.5 35.0 %collective-permute-start.13 = (bf16[128,2048]{1,0:T(8,128)(2,1)}, bf16[128,2048]{1,0:T(8,128)(2,1)}, u32[]{:S(2)}, u32[]{:S(2)}) collective-permute-start(bf16[128,2048]{1,0:T(8,128)(2,1)} %get-tuple-element.11), channel_id=1, source_target_pairs={{3,0},{4,1},{5,2},{6,3},{7,4},{8,5},{9,6},{10,7},{11,8},{12,9},{13... | collective-permute-start | bytes 1572872 | tf_op jit(solution)/shard_map/ppermute | solution.py:18
  210.0 35.7 %collective-permute-start.12 = (bf16[128,2048]{1,0:T(8,128)(2,1)}, bf16[128,2048]{1,0:T(8,128)(2,1)}, u32[]{:S(2)}, u32[]{:S(2)}) collective-permute-start(bf16[128,2048]{1,0:T(8,128)(2,1)} %get-tuple-element.12), channel_id=1, source_target_pairs={{0,3},{1,4},{2,5},{3,6},{4,7},{5,8},{6,9},{7,10},{8,11},{9,12},{10... | collective-permute-start | bytes 1572872 | tf_op jit(solution)/shard_map/ppermute | solution.py:18
  216.2 29.5 %collective-permute-start.11 = (bf16[128,2048]{1,0:T(8,128)(2,1)}, bf16[128,2048]{1,0:T(8,128)(2,1)}, u32[]{:S(2)}, u32[]{:S(2)}) collective-permute-start(bf16[128,2048]{1,0:T(8,128)(2,1)} %get-tuple-element.13), channel_id=1, source_target_pairs={{2,0},{3,1},{4,2},{5,3},{6,4},{7,5},{8,6},{9,7},{10,8},{11,9},{12,... | collective-permute-start | bytes 1572872 | tf_op jit(solution)/shard_map/ppermute | solution.py:18
  218.6 36.2 %collective-permute-start.10 = (bf16[128,2048]{1,0:T(8,128)(2,1)}, bf16[128,2048]{1,0:T(8,128)(2,1)}, u32[]{:S(2)}, u32[]{:S(2)}) collective-permute-start(bf16[128,2048]{1,0:T(8,128)(2,1)} %get-tuple-element.14), channel_id=1, source_target_pairs={{0,2},{1,3},{2,4},{3,5},{4,6},{5,7},{6,8},{7,9},{8,10},{9,11},{10,... | collective-permute-start | bytes 1572872 | tf_op jit(solution)/shard_map/ppermute | solution.py:18
  222.9 31.9 %collective-permute-start.9 = (bf16[128,2048]{1,0:T(8,128)(2,1)}, bf16[128,2048]{1,0:T(8,128)(2,1)}, u32[]{:S(2)}, u32[]{:S(2)}) collective-permute-start(bf16[128,2048]{1,0:T(8,128)(2,1)} %get-tuple-element.15), channel_id=1, source_target_pairs={{1,0},{2,1},{3,2},{4,3},{5,4},{6,5},{7,6},{8,7},{9,8},{10,9},{11,1... | collective-permute-start | bytes 1572872 | tf_op jit(solution)/shard_map/ppermute | solution.py:18
  243.3 14.6 %copy-start.6 = (f32[1024]{0:T(1024)S(1)}, f32[1024]{0:T(1024)}, u32[]{:S(2)}) copy-start(f32[1024]{0:T(1024)} %param.12) | copy-start | bytes 12292
  264.9 40.8 %all-to-all-start.2 = ((bf16[16,8,1024]{2,1,0:T(8,128)(2,1)}), bf16[16,8,1024]{2,1,0:T(8,128)(2,1)S(1)}, u32[]{:S(2)}, u32[]{:S(2)}) async-start(bf16[16,8,1024]{2,1,0:T(8,128)(2,1)} %bitcast.33), calls=%async_computation.2 | async-start | bytes 524288 | tf_op jit(solution)/shard_map/all_to_all | solution.py:132
Sparse Core Ops, SparseCore 0:
  116.1 78.6 reduce-scatter.1
where the time goes:
time: 318 us; the launch traced here: 316 us
  matrix products  85.6 us (27%)
  blocking collectives  60.1 us (19%)
  starting transfers between devices  58.5 us (18%)
  local copies, waits for them, and re-layouts  50.4 us (16%)
  other arithmetic  33.8 us (11%)
  between operations  15.2 us (5%)
  waiting for transfers between devices  12.5 us (4%)
    ppermute x16, starting transfers between devices, from_behind(): return lax.ppermute(block, axis, route)  53.3 us
    psum x1, blocking collectives, per_device(): grad_gain = lax.psum(gain_term, 'ctx') * norm_scale  33.8 us
    dot_general x1, matrix products, per_device(): jnp.einsum('shqk,sqhd->skhd', d_scores, heads_q, preferred_element_type=j...  19.2 us
    dot_general x1, matrix products, per_device(): jnp.einsum('shqk,skhd->sqhd', d_scores, heads_k, preferred_element_type=j...  19.1 us
    dot_general x8, matrix products, per_device(): jnp.dot(remote_piece, kv_weight, preferred_element_type=jnp.float32)  14.8 us
    all_to_all x1, blocking collectives, per_device(): lax.all_to_all(wanted, 'ctx', split_axis=0, concat_axis=0, tiled=True)  13.6 us
    all_to_all x1, blocking collectives, per_device(): lax.all_to_all(outgoing, 'ctx', split_axis=0, concat_axis=0, tiled=True)  12.6 us
    ppermute x16, waiting for transfers between devices, from_behind(): return lax.ppermute(block, axis, route)  12.5 us
  transfers between devices with their start and end apart: 18, of which 3 were waited for; matrix products, arithmetic and copies ran while one was open for 40% of the time, Pallas kernels for 0%

commit v1 on v0

v1 whole, which is shorter than its diff:
```python
import functools

import jax
import jax.numpy as jnp
from jax import lax
from jax.experimental import pallas as pl
from jax.experimental.pallas import tpu as pltpu
from jax.sharding import PartitionSpec as P

HEADS = 16
BLOCK = 128
LANES = 128
EPS = 1e-06
FAR = -1e30
F32 = jnp.float32
BF16 = jnp.bfloat16


def iota(shape, dim):
    return lax.broadcasted_iota(jnp.int32, shape, dim)


def nn(a, b):
    return jnp.dot(a, b, preferred_element_type=F32)


def nt(a, b):
    return lax.dot_general(a, b, (((1,), (1,)), ((), ())), preferred_element_type=F32)


def tn(a, b):
    return lax.dot_general(a, b, (((0,), (0,)), ((), ())), preferred_element_type=F32)


def ranks(key_col, key_row, dim):
    if dim == 0:
        return jnp.sum((key_col < key_row).astype(F32), axis=0, keepdims=True).astype(jnp.int32)
    return jnp.sum((key_row < key_col).astype(F32), axis=1, keepdims=True).astype(jnp.int32)


def column_of(row):
    n = row.shape[1]
    wide = jnp.broadcast_to(row.astype(F32), (n, n))
    return jnp.transpose(wide)[:, :1].astype(jnp.int32)


def row_of(col):
    n = col.shape[0]
    wide = jnp.broadcast_to(col.astype(F32), (n, n))
    return jnp.transpose(wide)[:1, :].astype(jnp.int32)


def pack_kernel(n_dev, slots, per_peer, owners_ref, table_ref, perm_ref, raster_ref, msg_ref, one_ref, sorted_ref):
    rows = raster_ref.shape[1]
    for part in range(raster_ref.shape[0]):
        target = owners_ref[part] * rows + iota((rows, 1), 0)

        def hit(block, acc):
            line = perm_ref[pl.ds(block, 1), :]
            return acc + jnp.where(line == target, block, 0)

        found = lax.fori_loop(0, n_dev, hit, jnp.zeros((rows, rows), jnp.int32), unroll=4)
        home = jnp.sum(found.astype(F32), axis=1, keepdims=True).astype(jnp.int32)
        key_col = home * rows + iota((rows, 1), 0)
        key_row = row_of(key_col)
        slot_row = ranks(key_col, key_row, 0)
        slot_col = ranks(key_col, key_row, 1)
        pick = (slot_row == iota((rows, rows), 0)).astype(BF16)
        one_ref[part] = (slot_col == iota((rows, rows), 1)).astype(BF16)
        ordered = nn(pick, raster_ref[part]).astype(BF16)
        if per_peer % 8 == 0:
            sorted_ref[part] = ordered.astype(F32).reshape(n_dev, per_peer, -1)
        else:
            sorted_ref[part] = ordered
    if per_peer % 8 == 0:
        n_dest = msg_ref.shape[0]
        for part in range(raster_ref.shape[0]):

            def place(dest, carry):
                for slot in range(slots):
                    block = table_ref[dest, slot]
                    msg_ref[dest, part, slot] = sorted_ref[part, block].astype(BF16)
                return carry

            lax.fori_loop(0, n_dest, place, 0, unroll=2)


def main_kernel(
    count_ref, arrived_ref, perm_ref, gain_ref, cot_ref, wqkv_ref, wout_ref,
    layer_ref, ret_ref, gain_out_ref, att_ref, cots_ref,
    x_ref, inv_ref, nrm_ref, q_ref, kv_ref, do_ref, attf_ref, dq_ref, dkv_ref,
):
    n_rows, width = x_ref.shape
    slots = n_rows // BLOCK
    head_dim = width // HEADS
    gain = gain_ref[...]
    key_row = perm_ref[...]
    key_col = column_of(key_row)
    slot_row = ranks(key_col, key_row, 0)
    slot_col = ranks(key_col, key_row, 1)
    to_arrival = (slot_row == iota((BLOCK, BLOCK), 0)).astype(BF16)
    to_order = (slot_col == iota((BLOCK, BLOCK), 1)).astype(BF16)
    cots_ref[...] = nn(to_arrival, cot_ref[...]).astype(BF16)
    for j in range(slots):
        x = arrived_ref[:, j].astype(F32).reshape(BLOCK, width)
        x_ref[pl.ds(j * BLOCK, BLOCK), :] = x
        inv = lax.rsqrt(jnp.mean(x * x, axis=1, keepdims=True) + EPS)
        inv_ref[pl.ds(j * BLOCK, BLOCK), :] = jnp.broadcast_to(inv, (BLOCK, LANES))
        nrm_ref[pl.ds(j * BLOCK, BLOCK), :] = (x * inv * gain).astype(BF16)
    scale = head_dim ** (-0.5)
    q_ref[...] = nn(nrm_ref[pl.ds(0, BLOCK), :], wqkv_ref[:, :width]).astype(BF16)
    kv_ref[...] = nn(nrm_ref[...], wqkv_ref[:, width:]).astype(BF16)
    do_ref[...] = nt(cots_ref[...], wout_ref[...]).astype(BF16)
    count = count_ref[0]
    first = iota((BLOCK, LANES), 1) < head_dim

    def both(pair):
        zero = jnp.zeros_like(pair)
        return jnp.concatenate([jnp.where(first, pair, zero), jnp.where(first, zero, pair)], axis=0)

    def own(out):
        return jnp.concatenate([out[:head_dim, :BLOCK], out[head_dim:, BLOCK:]], axis=0)

    def pair_step(pair, carry):
        lane = pl.multiple_of(pair * LANES, LANES)
        cols = pl.ds(lane, LANES)
        vcols = pl.ds(pl.multiple_of(width + pair * LANES, LANES), LANES)
        qm = both(q_ref[:, cols])
        dom = both(do_ref[:, cols])
        k = kv_ref[:, cols]
        v = kv_ref[:, vcols]
        s = nt(k, qm) * scale
        s = jnp.concatenate(
            [jnp.where(j < count, s[j * BLOCK:(j + 1) * BLOCK], FAR) for j in range(slots)], axis=0
        )
        e = jnp.exp(s - jnp.max(s, axis=0, keepdims=True))
        p = e / jnp.sum(e, axis=0, keepdims=True)
        pb = p.astype(BF16)
        dp = nt(v, dom)
        dots = jnp.sum(dp * p, axis=0, keepdims=True)
        ds = (p * (dp - dots) * scale).astype(BF16)
        attf_ref[:, cols] = jnp.transpose(own(tn(v, pb)))
        dq_ref[:, cols] = jnp.transpose(own(tn(k, ds))).astype(BF16)
        dkv_ref[:, cols] = nn(ds, qm).astype(BF16)
        dkv_ref[:, vcols] = nn(pb, dom).astype(BF16)
        return carry

    lax.fori_loop(0, width // LANES, pair_step, 0)
    att = attf_ref[...].astype(BF16)
    att_ref[...] = att
    layer = (x_ref[pl.ds(0, BLOCK), :] + nn(att, wout_ref[...])).astype(BF16)
    layer_ref[...] = nn(to_order, layer).astype(BF16)
    gains = jnp.zeros((1, width), F32)
    for j in range(slots):
        rows = pl.ds(j * BLOCK, BLOCK)
        dn = nt(dkv_ref[rows, :], wqkv_ref[:, width:])
        if j == 0:
            dn = dn + nt(dq_ref[...], wqkv_ref[:, :width])
        x = x_ref[rows, :]
        inv = inv_ref[rows, :][:, :1]
        gains = gains + jnp.sum(dn * (x * inv), axis=0, keepdims=True)
        scaled = dn * gain
        out = inv * scaled - x * (inv * inv * inv * jnp.mean(scaled * x, axis=1, keepdims=True))
        if j == 0:
            out = out + cots_ref[...].astype(F32)
        ret_ref[:, j] = out.reshape(ret_ref.shape[0], ret_ref.shape[2], width).astype(BF16)
    gain_out_ref[...] = gains


def sum_kernel(n_dev, slots, table_ref, back_ref, one_ref, out_ref, acc_ref):
    acc_ref[...] = jnp.zeros_like(acc_ref)

    def add(dest, carry):
        for slot in range(slots):
            block = table_ref[dest, slot]
            acc_ref[block] += back_ref[dest, slot].astype(F32)
        return carry

    lax.fori_loop(0, n_dev, add, 0, unroll=2)
    total = acc_ref[...].reshape(out_ref.shape).astype(BF16)
    out_ref[...] = nn(one_ref[0], total).astype(BF16)


VM = pl.BlockSpec(memory_space=pltpu.VMEM)
SM = pl.BlockSpec(memory_space=pltpu.SMEM)


def per_device(
    raster_tokens, hilbert_perm, neighbors, neighbor_counts, norm_gain, w_qkv, w_out, cotangent
):
    n_dev = lax.axis_size("ctx")
    me = lax.axis_index("ctx")
    rows, width = raster_tokens.shape
    slots = neighbors.shape[1]
    per_peer = rows // n_dev
    norm_scale = (rows * n_dev) ** (-0.5)
    n_rows = slots * BLOCK
    fits = per_peer % 8 == 0
    note = jnp.concatenate([hilbert_perm, jnp.pad(neighbors[0], (0, rows - slots))])
    note = jnp.broadcast_to(note[None, None], (n_dev, 1, 2 * rows))
    note = lax.all_to_all(note, "ctx", 0, 0, tiled=True)[:, 0]
    perm_all = note[:, :rows]
    table = note[:, rows:rows + slots]

    msg_shape = (n_dev, 1, slots, per_peer, width)
    if not fits:
        msg_shape = (1, 1, 1, 8, LANES)
    sort_shape = (1, n_dev, per_peer, width) if fits else (1, rows, width)
    msg, one, in_order = pl.pallas_call(
        functools.partial(pack_kernel, n_dev, slots, per_peer),
        out_shape=(
            jax.ShapeDtypeStruct(msg_shape, BF16),
            jax.ShapeDtypeStruct((1, rows, rows), BF16),
            jax.ShapeDtypeStruct(sort_shape, F32 if fits else BF16),
        ),
        in_specs=[SM, SM, VM, VM],
        out_specs=(VM, VM, VM),
    )(me[None], table, perm_all, raster_tokens[None])
    if not fits:
        msg = in_order.reshape(n_dev, per_peer, width)[table][:, None]
    msg = msg[:, 0]
    arrived = lax.all_to_all(msg, "ctx", 0, 0, tiled=True)
    if not fits:
        arrived = arrived.transpose(1, 0, 2, 3).reshape(1, slots, rows, width).transpose(0, 1, 2, 3)
        ret_shape = (1, slots, rows, width)
    else:
        ret_shape = (n_dev, slots, per_peer, width)

    layer_out, ret, gains, att, cots = pl.pallas_call(
        main_kernel,
        out_shape=(
            jax.ShapeDtypeStruct((rows, width), BF16),
            jax.ShapeDtypeStruct(ret_shape, BF16),
            jax.ShapeDtypeStruct((1, width), F32),
            jax.ShapeDtypeStruct((rows, width), BF16),
            jax.ShapeDtypeStruct((rows, width), BF16),
        ),
        in_specs=[SM] + [VM] * 6,
        out_specs=(VM,) * 5,
        scratch_shapes=[
            pltpu.VMEM((n_rows, width), F32),
            pltpu.VMEM((n_rows, LANES), F32),
            pltpu.VMEM((n_rows, width), BF16),
            pltpu.VMEM((rows, width), BF16),
            pltpu.VMEM((n_rows, 2 * width), BF16),
            pltpu.VMEM((rows, width), BF16),
            pltpu.VMEM((rows, width), F32),
            pltpu.VMEM((rows, width), BF16),
            pltpu.VMEM((n_rows, 2 * width), BF16),
        ],
    )(neighbor_counts, arrived, hilbert_perm[None], norm_gain[None], cotangent, w_qkv, w_out)

    grad_w_out = (
        lax.psum_scatter(tn(att, cots), "ctx", scatter_dimension=0, tiled=True) * norm_scale
    )
    high = gains.astype(BF16)
    low = (gains - high.astype(F32)).astype(BF16)
    extra = jnp.concatenate([high, low, jnp.zeros((6, width), BF16)])
    if fits:
        extra = jnp.broadcast_to(extra.reshape(1, 1, 8, width), (n_dev, 1, 8, width))
        back = lax.all_to_all(jnp.concatenate([ret, extra], axis=1), "ctx", 0, 0, tiled=True)
        parts = back[:, slots, :2].astype(F32)
        grad_tokens = pl.pallas_call(
            functools.partial(sum_kernel, n_dev, slots),
            out_shape=jax.ShapeDtypeStruct((rows, width), BF16),
            in_specs=[SM, VM, VM],
            out_specs=VM,
            scratch_shapes=[pltpu.VMEM((n_dev, per_peer, width), F32)],
        )(table, back, one)
    else:
        ret = ret.reshape(slots, n_dev, per_peer, width).transpose(1, 0, 2, 3)
        ret = ret.reshape(n_dev, slots * per_peer, width)
        extra = jnp.broadcast_to(extra[None, :2], (n_dev, 2, width))
        back = lax.all_to_all(jnp.concatenate([ret, extra], axis=1), "ctx", 0, 0, tiled=True)
        parts = back[:, slots * per_peer:].astype(F32)
        rest = back[:, :slots * per_peer].reshape(n_dev * slots, per_peer, width).astype(F32)
        total = jnp.zeros((n_dev, per_peer, width), F32).at[table.reshape(-1)].add(rest)
        grad_tokens = nn(one[0], total.reshape(rows, width).astype(BF16)).astype(BF16)
    grad_gain = jnp.sum(parts, axis=(0, 1)) * norm_scale
    return (layer_out, grad_tokens, grad_w_out, grad_gain)


def solution(mesh):
    placed = (
        P(("groups", "ctx"), None),
        P(("groups", "ctx")),
        P(("groups", "ctx"), None),
        P(("groups", "ctx")),
        P(),
        P(),
        P(),
        P(("groups", "ctx"), None),
    )
    return jax.shard_map(
        per_device,
        mesh=mesh,
        in_specs=placed,
        out_specs=(
            P(("groups", "ctx"), None),
            P(("groups", "ctx"), None),
            P(("groups", "ctx"), None),
            P("groups"),
        ),
        check_vma=False,
    )
```

time: 318 us -> 181 us (0.57)
  matrix products: 85.6 us -> 3.7 us
  starting transfers between devices: 58.5 us -> 11.2 us
  local copies, waits for them, and re-layouts: 50.4 us -> 4.11 us
  waiting for transfers between devices: 12.5 us -> 52.4 us
  Pallas kernels: 0 us -> 32 us
  other arithmetic: 33.8 us -> 4.2 us
    dot_general x18 -> x1, matrix products: 80.1 us -> 3.7 us  [tn(): lax.dot_general(a, b, (((0,), (0,)), ((), ())), preferred_element_type=F32)]
    ppermute x16 -> x0, starting transfers between devices: 53.3 us -> none  [from_behind(): return lax.ppermute(block, axis, route)]
    psum x1 -> x0, blocking collectives: 33.8 us -> none  [per_device(): grad_gain = lax.psum(gain_term, 'ctx') * norm_scale]
    all_to_all x1 -> x2, waiting for transfers between devices: 0.01 us -> 33 us  [the longest x1 26.5 us: per_device(): arrived = lax.all_to_all(msg, 'ctx', 0, 0, tiled=True)]
    pallas_call x0 -> x3, Pallas kernels: none -> 32 us  [the longest x1 26.2 us: per_device(): pl.pallas_call(main_kernel, out_shape=(jax.ShapeDtypeStruct((rows, width)...]
    all_to_all x2 -> x1, blocking collectives: 26.3 us -> 58.1 us  [per_device(): lax.all_to_all(jnp.concatenate([ret, extra], axis=1), 'ctx', 0, 0, tiled=...]
    reduce_scatter x1, waiting for transfers between devices: 0.01 us -> 19.4 us  [per_device(): lax.psum_scatter(tn(att, cots), 'ctx', scatter_dimension=0, tiled=True)]
    ppermute x16 -> x0, waiting for transfers between devices: 12.5 us -> none  [from_behind(): return lax.ppermute(block, axis, route)]
  transfers between devices with their start and end apart: 18 -> 3, of which waited for: 3 -> 3; matrix products, arithmetic and copies ran while one was open for 40% -> 1% of each run, Pallas kernels for 0% -> 2%
where the time goes in v1:
time: 181 us; the launch traced here: 180 us
  blocking collectives  58.1 us (32%)
  waiting for transfers between devices  52.4 us (29%)
  Pallas kernels  32 us (18%)
  between operations  14.7 us (8%)
  starting transfers between devices  11.2 us (6%)
  other arithmetic  4.2 us (2%)
  local copies, waits for them, and re-layouts  4.11 us (2%)
  matrix products  3.7 us (2%)
    all_to_all x1, blocking collectives, per_device(): lax.all_to_all(jnp.concatenate([ret, extra], axis=1), 'ctx', 0, 0, tiled=...  58.1 us
    all_to_all x1, waiting for transfers between devices, per_device(): arrived = lax.all_to_all(msg, 'ctx', 0, 0, tiled=True)  26.5 us
    pallas_call x1, Pallas kernels, per_device(): pl.pallas_call(main_kernel, out_shape=(jax.ShapeDtypeStruct((rows, width)...  26.2 us
    reduce_scatter x1, waiting for transfers between devices, per_device(): lax.psum_scatter(tn(att, cots), 'ctx', scatter_dimension=0, tiled=True)  19.4 us
    all_to_all x1, starting transfers between devices, per_device(): note = lax.all_to_all(note, 'ctx', 0, 0, tiled=True)[:, 0]  7.41 us
    all_to_all x1, waiting for transfers between devices, per_device(): note = lax.all_to_all(note, 'ctx', 0, 0, tiled=True)[:, 0]  6.5 us
    all_to_all x1, starting transfers between devices, per_device(): arrived = lax.all_to_all(msg, 'ctx', 0, 0, tiled=True)  3.7 us
    dot_general x1, matrix products, tn(): lax.dot_general(a, b, (((0,), (0,)), ((), ())), preferred_element_type=F32)  3.7 us
  transfers between devices with their start and end apart: 3, of which 3 were waited for; matrix products, arithmetic and copies ran while one was open for 1% of the time, Pallas kernels for 2%

profile of v1, /device:TPU:0, one launch (start us, length us, event | category | flops | bytes accessed | tf_op | source)
XLA Modules:
  0.0 180.3 jit_solution(14283255455618924061)
XLA Ops:
  7.2 0.7 pad_add_fusion
  7.8 0.6 broadcast_in_dim.27
  8.5 7.4 %all-to-all-start = ((s32[16,1,256]{2,1,0:T(1,128)}), s32[16,1,256]{2,1,0:T(1,128)S(1)}, u32[]{:S(2)}, u32[]{:S(2)}) async-start(s32[16,1,256]{2,1,0:T(1,128)} %broadcast_in_dim.27), calls=%async_computation | async-start | bytes 32768 | tf_op jit(solution)/shard_map/all_to_all | solution.py:201
  15.9 6.5 %all-to-all-done = s32[16,1,256]{2,1,0:T(1,128)S(1)} async-done(((s32[16,1,256]{2,1,0:T(1,128)}), s32[16,1,256]{2,1,0:T(1,128)S(1)}, u32[]{:S(2)}, u32[]{:S(2)}) %all-to-all-start) | async-done | bytes 16416 | tf_op jit(solution)/shard_map/all_to_all | solution.py:201
  22.4 0.6 slice.12.table_ref
  23.0 0.6 slice.13.perm_ref
  23.6 2.9 %shard_map.111 = (bf16[16,1,5,8,1024]{4,3,2,1,0:T(8,128)(2,1)}, bf16[1,128,128]{2,1,0:T(8,128)(2,1)}, f32[1,16,8,1024]{3,2,1,0:T(8,128)}) custom-call(s32[1]{0:T(128)} %bitcast.owners_ref, s32[16,5]{1,0:T(8,128)} %slice.12.table_ref, s32[16,128]{1,0:T(8,128)} %slice.13.perm_ref, bf16[1,128,1024]{2,1,0:T(8,128)(2,1)} %bitcast.12), custom_call_target="tpu_custom_call" | custom-call | tf_op jit(solution)/shard_map/pallas_call | solution.py:209
  26.5 3.7 %all-to-all-start.1 = ((bf16[16,5,8,1024]{3,2,1,0:T(8,128)(2,1)}), bf16[16,5,8,1024]{3,2,1,0:T(8,128)(2,1)S(1)}, u32[]{:S(2)}, u32[]{:S(2)}) async-start(bf16[16,5,8,1024]{3,2,1,0:T(8,128)(2,1)} %bitcast.11), calls=%async_computation.1 | async-start | bytes 2621440 | tf_op jit(solution)/shard_map/all_to_all | solution.py:222
  30.2 0.0 reduce-scatter.2.cloned.1.call-start
  30.9 26.5 %all-to-all-done.1.arrived_ref = bf16[16,5,8,1024]{3,2,1,0:T(8,128)(2,1)S(1)} async-done(((bf16[16,5,8,1024]{3,2,1,0:T(8,128)(2,1)}), bf16[16,5,8,1024]{3,2,1,0:T(8,128)(2,1)S(1)}, u32[]{:S(2)}, u32[]{:S(2)}) %all-to-all-start.1) | async-done | bytes 1310752 | tf_op jit(solution)/shard_map/all_to_all | solution.py:222
  57.4 0.0 copy-start
  57.4 1.1 copy-done
  58.5 26.2 %shard_map.112 = (bf16[128,1024]{1,0:T(8,128)(2,1)}, bf16[16,5,8,1024]{3,2,1,0:T(8,128)(2,1)}, f32[1,1024]{1,0:T(1,128)}, bf16[128,1024]{1,0:T(8,128)(2,1)}, bf16[128,1024]{1,0:T(8,128)(2,1)}) custom-call(s32[1]{0:T(128)S(6)} %copy.15.count_ref, bf16[16,5,8,1024]{3,2,1,0:T(8,128)(2,1)} %copy-done, s32[1,128]{1,0:T(1,128)} %bitcast.16, f32[1,1024]{1,0:T(1,128)} %bitcast.15, ...), custom_call_target="tpu_custom_call" | custom-call | tf_op jit(solution)/shard_map/pallas_call | solution.py:229
  84.7 3.7 %fusion.1 = f32[1024,1024]{1,0:T(8,128)} fusion(bf16[128,1024]{1,0:T(8,128)(2,1)} %get-tuple-element.16, bf16[128,1024]{1,0:T(8,128)(2,1)} %get-tuple-element.17), kind=kOutput, calls=%fused_computation.9 | convolution fusion | flops 268435456 | bytes 4718592 | tf_op jit(solution)/shard_map/dot_general | solution.py:32
  88.4 0.0 copy-start.2
  88.5 0.0 copy-start.1
  88.5 0.0 reduce-scatter.2.cloned.1.call-update
  88.5 0.1 pad.9.clone
  88.6 0.6 copy-done.2
  89.1 0.1 maximum_maximum_fusion
  89.2 0.5 copy-done.1
  89.8 0.1 pad_maximum_fusion
  89.9 58.1 %all_to_all.15.back_ref = bf16[16,6,8,1024]{3,2,1,0:T(8,128)(2,1)} all-to-all(bf16[16,6,8,1024]{3,2,1,0:T(8,128)(2,1)S(1)} %pad_maximum_fusion), channel_id=1, replica_groups=mesh['groups'=2,'ctx'=16] {'ctx'}, dimensions={0} | all-to-all | bytes 3145728 | tf_op jit(solution)/shard_map/all_to_all | solution.py:261
  148.0 2.8 %shard_map.113 = bf16[128,1024]{1,0:T(8,128)(2,1)} custom-call(s32[16,5]{1,0:T(8,128)} %slice.12.table_ref, bf16[16,6,8,1024]{3,2,1,0:T(8,128)(2,1)} %all_to_all.15.back_ref, bf16[1,128,128]{2,1,0:T(8,128)(2,1)} %get-tuple-element.15.one_ref), custom_call_target="tpu_custom_call" | custom-call | tf_op jit(solution)/shard_map/pallas_call | solution.py:263
  150.8 1.0 convert_reduce_fusion
  151.9 0.6 broadcast_multiply_fusion.1
  152.5 19.4 %reduce-scatter.2.cloned.1.call-done = f32[64,1024]{1,0:T(8,128)} async-done(((f32[1024,1024]{1,0:T(8,128)}), f32[64,1024]{1,0:T(8,128)}) %reduce-scatter.2.cloned.1.call-update) | async-done | bytes 262160 | tf_op jit(solution)/shard_map/reduce_scatter | solution.py:254
  171.8 1.7 broadcast_multiply_fusion
  (4 shorter events, 0.0 us)
Async XLA Ops:
  8.5 13.9 %all-to-all-start = ((s32[16,1,256]{2,1,0:T(1,128)}), s32[16,1,256]{2,1,0:T(1,128)S(1)}, u32[]{:S(2)}, u32[]{:S(2)}) async-start(s32[16,1,256]{2,1,0:T(1,128)} %broadcast_in_dim.27), calls=%async_computation | async-start | bytes 32768 | tf_op jit(solution)/shard_map/all_to_all | solution.py:201
  26.5 30.9 %all-to-all-start.1 = ((bf16[16,5,8,1024]{3,2,1,0:T(8,128)(2,1)}), bf16[16,5,8,1024]{3,2,1,0:T(8,128)(2,1)S(1)}, u32[]{:S(2)}, u32[]{:S(2)}) async-start(bf16[16,5,8,1024]{3,2,1,0:T(8,128)(2,1)} %bitcast.11), calls=%async_computation.1 | async-start | bytes 2621440 | tf_op jit(solution)/shard_map/all_to_all | solution.py:222
  30.2 141.6 %reduce-scatter.2.cloned.1.call-start = ((), (), s32[]{:S(2)}) async-start(), calls=%async_computation.4 | async-start | bytes 4456448 | tf_op jit(solution)/shard_map/reduce_scatter | solution.py:254
  57.4 1.1 copy-start
  88.4 0.7 copy-start.2
  88.5 1.3 copy-start.1
Sparse Core Ops, SparseCore 0:
  88.6 83.1 reduce-scatter.1

commit v2 on v1

v2 whole, which is shorter than its diff:
```python
import functools

import jax
import jax.numpy as jnp
from jax import lax
from jax.experimental import pallas as pl
from jax.experimental.pallas import tpu as pltpu
from jax.sharding import PartitionSpec as P

HEADS = 16
BLOCK = 128
LANES = 128
EPS = 1e-06
FAR = -1e30
F32 = jnp.float32
BF16 = jnp.bfloat16


def iota(shape, dim):
    return lax.broadcasted_iota(jnp.int32, shape, dim)


def nn(a, b):
    return jnp.dot(a, b, preferred_element_type=F32)


def nt(a, b):
    return lax.dot_general(a, b, (((1,), (1,)), ((), ())), preferred_element_type=F32)


def tn(a, b):
    return lax.dot_general(a, b, (((0,), (0,)), ((), ())), preferred_element_type=F32)


def ranks(key_col, key_row, dim):
    if dim == 0:
        return jnp.sum((key_col < key_row).astype(F32), axis=0, keepdims=True).astype(jnp.int32)
    return jnp.sum((key_row < key_col).astype(F32), axis=1, keepdims=True).astype(jnp.int32)


def column_of(row):
    n = row.shape[1]
    wide = jnp.broadcast_to(row.astype(F32), (n, n))
    return jnp.transpose(wide)[:, :1].astype(jnp.int32)


def row_of(col):
    n = col.shape[0]
    wide = jnp.broadcast_to(col.astype(F32), (n, n))
    return jnp.transpose(wide)[:1, :].astype(jnp.int32)


def pack_kernel(n_dev, slots, per_peer, place_ref, table_ref, note_ref, own_ref, mirror_ref, msg_ref, one_ref, sorted_ref):
    rows, width = own_ref.shape
    half = n_dev // 2
    upper, seat = place_ref[0], place_ref[1]
    for part in range(2):
        target = (part * half + seat) * rows + iota((rows, 1), 0)

        def hit(block, acc):
            line = note_ref[block][:, :rows]
            return acc + jnp.where(line == target, block, 0)

        found = lax.fori_loop(0, n_dev, hit, jnp.zeros((rows, rows), jnp.int32), unroll=4)
        home = jnp.sum(found.astype(F32), axis=1, keepdims=True).astype(jnp.int32)
        key_col = home * rows + iota((rows, 1), 0)
        key_row = row_of(key_col)
        slot_row = ranks(key_col, key_row, 0)
        slot_col = ranks(key_col, key_row, 1)
        pick = (slot_row == iota((rows, rows), 0)).astype(BF16)
        one_ref[part] = (slot_col == iota((rows, rows), 1)).astype(BF16)
        chunk = jnp.where(upper == part, own_ref[...], mirror_ref[...])
        ordered = nn(pick, chunk)
        if per_peer % 8 == 0:
            sorted_ref[part] = ordered.reshape(n_dev, per_peer, width).astype(BF16)
        else:
            sorted_ref[part] = ordered.astype(BF16)
    if per_peer % 8 == 0:

        def place(dest, carry):
            for slot in range(slots):
                block = table_ref[upper * half + dest, 0, rows + slot]
                for part in range(2):
                    msg_ref[dest, part, slot] = sorted_ref[part, block]
            return carry

        lax.fori_loop(0, half, place, 0, unroll=2)


def main_kernel(
    fits, count_ref, arrived_ref, perm_ref, gain_ref, cot_ref, wqkv_ref, wout_ref,
    layer_ref, ret_ref, *rest
):
    if fits:
        x_ref, inv_ref, nrm_ref, q_ref, kv_ref, do_ref, attt_ref, cots_ref, dq_ref, dkv_ref = rest
    else:
        gain_out_ref, att_out_ref, x_ref, inv_ref, nrm_ref, q_ref, kv_ref, do_ref, attt_ref, cots_ref, dq_ref, dkv_ref = rest
    n_rows, width = x_ref.shape
    slots = n_rows // BLOCK
    head_dim = width // HEADS
    gain = gain_ref[...]
    key_row = perm_ref[...]
    key_col = column_of(key_row)
    slot_row = ranks(key_col, key_row, 0)
    slot_col = ranks(key_col, key_row, 1)
    to_arrival = (slot_row == iota((BLOCK, BLOCK), 0)).astype(BF16)
    to_order = (slot_col == iota((BLOCK, BLOCK), 1)).astype(BF16)
    cots_ref[...] = nn(to_arrival, cot_ref[...]).astype(BF16)
    for j in range(slots):
        if fits:
            part_rows = BLOCK // 2
            for part in range(2):
                x = arrived_ref[:, part, j].astype(F32).reshape(part_rows, width)
                x_ref[pl.ds(j * BLOCK + part * part_rows, part_rows), :] = x
        else:
            x_ref[pl.ds(j * BLOCK, BLOCK), :] = arrived_ref[j].astype(F32)
        x = x_ref[pl.ds(j * BLOCK, BLOCK), :]
        inv = lax.rsqrt(jnp.mean(x * x, axis=1, keepdims=True) + EPS)
        inv_ref[pl.ds(j * BLOCK, BLOCK), :] = jnp.broadcast_to(inv, (BLOCK, LANES))
        nrm_ref[pl.ds(j * BLOCK, BLOCK), :] = (x * inv * gain).astype(BF16)
    scale = head_dim ** (-0.5)
    q_ref[...] = nn(nrm_ref[pl.ds(0, BLOCK), :], wqkv_ref[:, :width]).astype(BF16)
    kv_ref[...] = nn(nrm_ref[...], wqkv_ref[:, width:]).astype(BF16)
    do_ref[...] = nt(cots_ref[...], wout_ref[...]).astype(BF16)
    count = count_ref[0]
    first = iota((BLOCK, LANES), 1) < head_dim

    def both(pair):
        zero = jnp.zeros_like(pair)
        return jnp.concatenate([jnp.where(first, pair, zero), jnp.where(first, zero, pair)], axis=0)

    def own(out):
        return jnp.concatenate([out[:head_dim, :BLOCK], out[head_dim:, BLOCK:]], axis=0)

    def pair_step(pair, carry):
        lane = pl.multiple_of(pair * LANES, LANES)
        cols = pl.ds(lane, LANES)
        vcols = pl.ds(pl.multiple_of(width + pair * LANES, LANES), LANES)
        qm = both(q_ref[:, cols])
        dom = both(do_ref[:, cols])
        k = kv_ref[:, cols]
        v = kv_ref[:, vcols]
        s = nt(k, qm) * scale
        s = jnp.concatenate(
            [jnp.where(j < count, s[j * BLOCK:(j + 1) * BLOCK], FAR) for j in range(slots)], axis=0
        )
        e = jnp.exp(s - jnp.max(s, axis=0, keepdims=True))
        p = e / jnp.sum(e, axis=0, keepdims=True)
        pb = p.astype(BF16)
        dp = nt(v, dom)
        dots = jnp.sum(dp * p, axis=0, keepdims=True)
        ds = (p * (dp - dots) * scale).astype(BF16)
        attt_ref[cols, :] = own(tn(v, pb)).astype(BF16)
        dq_ref[:, cols] = jnp.transpose(own(tn(k, ds))).astype(BF16)
        dkv_ref[:, cols] = nn(ds, qm).astype(BF16)
        dkv_ref[:, vcols] = nn(pb, dom).astype(BF16)
        return carry

    lax.fori_loop(0, width // LANES, pair_step, 0)
    layer = (x_ref[pl.ds(0, BLOCK), :] + tn(attt_ref[...], wout_ref[...])).astype(BF16)
    layer_ref[...] = nn(to_order, layer).astype(BF16)
    att = nt(attt_ref[...], to_order).astype(BF16)
    lane_blocks = width // LANES
    gains = jnp.zeros((1, width), F32)
    for j in range(slots):
        rows = pl.ds(j * BLOCK, BLOCK)
        dn = nt(dkv_ref[rows, :], wqkv_ref[:, width:])
        if j == 0:
            dn = dn + nt(dq_ref[...], wqkv_ref[:, :width])
        x = x_ref[rows, :]
        inv = inv_ref[rows, :][:, :1]
        gains = gains + jnp.sum(dn * (x * inv), axis=0, keepdims=True)
        scaled = dn * gain
        out = inv * scaled - x * (inv * inv * inv * jnp.mean(scaled * x, axis=1, keepdims=True))
        if j == 0:
            out = out + cots_ref[...].astype(F32)
        if fits:
            n_dev = ret_ref.shape[0]
            for lb in range(lane_blocks):
                piece = out[:, lb * LANES:(lb + 1) * LANES].reshape(n_dev, 8, LANES)
                ret_ref[:, pl.ds((j * lane_blocks + lb) * 8, 8), :] = piece.astype(BF16)
        else:
            ret_ref[j] = out.astype(BF16)
    if not fits:
        gain_out_ref[...] = gains
        att_out_ref[...] = att
        return
    base = slots * lane_blocks * 8
    feats = width // n_dev
    ret_ref[:, pl.ds(base, feats), :] = att.reshape(n_dev, feats, LANES)
    high = gains.astype(BF16).astype(F32)
    low = gains - high
    row = iota((8, LANES), 0)
    for part, value in enumerate((high, low)):
        tile = jnp.zeros((8, LANES), F32)
        for lb in range(lane_blocks):
            tile = jnp.where(row == lb, value[:, lb * LANES:(lb + 1) * LANES], tile)
        tile = jnp.broadcast_to(tile.astype(BF16)[None], (n_dev, 8, LANES))
        ret_ref[:, pl.ds(base + feats + part * 8, 8), :] = tile


def finish_kernel(
    n_dev, slots, masks, norm_scale, place_ref, table_ref, back_ref, one_ref, *rest
):
    cots = rest[:len(masks)]
    out_ref, gw_ref, gain_ref, acc_ref = rest[len(masks):]
    rows, width = out_ref.shape
    lane_blocks = width // LANES
    size = lane_blocks * 8
    acc_ref[...] = jnp.zeros_like(acc_ref)

    def add(dest, carry):
        for slot in range(slots):
            block = table_ref[dest, 0, rows + slot]
            acc_ref[block] += back_ref[dest, pl.ds(slot * size, size), :].astype(F32)
        return carry

    lax.fori_loop(0, n_dev, add, 0, unroll=2)
    upper, seat = place_ref[0], place_ref[1]
    me = upper * (n_dev // 2) + seat
    one = one_ref[upper]
    for lb in range(lane_blocks):
        total = acc_ref[:, pl.ds(lb * 8, 8), :].reshape(rows, LANES).astype(BF16)
        out_ref[:, pl.ds(lb * LANES, LANES)] = nn(one, total).astype(BF16)
    base = slots * size
    feats = width // n_dev
    acc = jnp.zeros((feats, width), F32)
    for group, ref in zip(masks, cots):
        for at, mask in enumerate(group):
            att = back_ref[me ^ mask, pl.ds(base, feats), :]
            acc = acc + nn(att, ref[pl.ds(at * rows, rows), :])
    gw_ref[...] = acc * norm_scale
    tile = jnp.zeros((8, LANES), F32)
    for dest in range(n_dev):
        for part in range(2):
            tile = tile + back_ref[dest, pl.ds(base + feats + part * 8, 8), :].astype(F32)
    gain_ref[...] = tile * norm_scale


VM = pl.BlockSpec(memory_space=pltpu.VMEM)
SM = pl.BlockSpec(memory_space=pltpu.SMEM)


def swap(block, mask):
    n_dev = lax.axis_size("ctx")
    return lax.ppermute(block, "ctx", [(i, i ^ mask) for i in range(n_dev)])


def gather_cotangent(cotangent, n_dev):
    masks = [2, n_dev // 2]
    masks += [m for m in (1 << b for b in range(n_dev.bit_length() - 1)) if m not in masks + [1]]
    held, names = cotangent, [0]
    for mask in masks[:-1]:
        other = swap(held, mask)
        held = jnp.concatenate([held, other])
        names = names + [m ^ mask for m in names]
    other = swap(held, masks[-1])
    others = [m ^ masks[-1] for m in names]
    pieces = [(names, held), (others, other)]
    return pieces + [([m ^ 1 for m in group], swap(piece, 1)) for group, piece in pieces]


def per_device(
    raster_tokens, hilbert_perm, neighbors, neighbor_counts, norm_gain, w_qkv, w_out, cotangent
):
    n_dev = lax.axis_size("ctx")
    half = n_dev // 2
    me = lax.axis_index("ctx")
    rows, width = raster_tokens.shape
    slots = neighbors.shape[1]
    per_peer = rows // n_dev
    norm_scale = (rows * n_dev) ** (-0.5)
    n_rows = slots * BLOCK
    fits = per_peer % 8 == 0
    lane_blocks = width // LANES
    feats = width // n_dev
    place = jnp.stack([me // half, me % half]).astype(jnp.int32)
    note = jnp.concatenate([hilbert_perm, jnp.pad(neighbors[0], (0, rows - slots))])
    note = jnp.broadcast_to(note[None, None], (n_dev, 1, 2 * rows))
    mirror = swap(raster_tokens, half)
    pieces = gather_cotangent(cotangent, n_dev)
    note = lax.all_to_all(note, "ctx", 0, 0, tiled=True)

    msg_shape = (half, 2, slots, per_peer, width) if fits else (8, LANES)
    sort_shape = (2, n_dev, per_peer, width) if fits else (2, rows, width)
    msg, one, in_order = pl.pallas_call(
        functools.partial(pack_kernel, n_dev, slots, per_peer),
        out_shape=(
            jax.ShapeDtypeStruct(msg_shape, BF16),
            jax.ShapeDtypeStruct((2, rows, rows), BF16),
            jax.ShapeDtypeStruct(sort_shape, BF16),
        ),
        in_specs=[SM, SM, VM, VM, VM],
        out_specs=(VM, VM, VM),
    )(place, note, note, raster_tokens, mirror)
    table = note[:, 0, rows:rows + slots]
    if not fits:
        mine = lax.dynamic_slice_in_dim(table, place[0] * half, half, 0)
        msg = in_order.reshape(2, n_dev, per_peer, width)[:, mine].transpose(1, 0, 2, 3, 4)
    halves = [list(range(half)), list(range(half, n_dev))]
    arrived = lax.all_to_all(msg, "ctx", 0, 0, tiled=True, axis_index_groups=halves)
    if fits:
        ret_shape = (n_dev, slots * lane_blocks * 8 + feats + 16, LANES)
        extra_shapes = ()
    else:
        arrived = arrived.transpose(2, 1, 0, 3, 4).reshape(slots, rows, width)
        ret_shape = (slots, rows, width)
        extra_shapes = (
            jax.ShapeDtypeStruct((1, width), F32),
            jax.ShapeDtypeStruct((width, rows), BF16),
        )

    layer_out, ret, *extra = pl.pallas_call(
        functools.partial(main_kernel, fits),
        out_shape=(
            jax.ShapeDtypeStruct((rows, width), BF16),
            jax.ShapeDtypeStruct(ret_shape, BF16),
        ) + extra_shapes,
        in_specs=[SM] + [VM] * 6,
        out_specs=(VM,) * (2 + len(extra_shapes)),
        scratch_shapes=[
            pltpu.VMEM((n_rows, width), F32),
            pltpu.VMEM((n_rows, LANES), F32),
            pltpu.VMEM((n_rows, width), BF16),
            pltpu.VMEM((rows, width), BF16),
            pltpu.VMEM((n_rows, 2 * width), BF16),
            pltpu.VMEM((rows, width), BF16),
            pltpu.VMEM((width, rows), BF16),
            pltpu.VMEM((rows, width), BF16),
            pltpu.VMEM((rows, width), BF16),
            pltpu.VMEM((n_rows, 2 * width), BF16),
        ],
        cost_estimate=pl.CostEstimate(
            flops=14 * n_rows * width * width, bytes_accessed=16 * width * width, transcendentals=0
        ),
    )(neighbor_counts, arrived, hilbert_perm[None], norm_gain[None], cotangent, w_qkv, w_out)

    if fits:
        back = lax.all_to_all(ret, "ctx", 0, 0, tiled=True)
        masks = [group for group, piece in pieces]
        grad_tokens, grad_w_out, grad_gain = pl.pallas_call(
            functools.partial(finish_kernel, n_dev, slots, masks, norm_scale),
            out_shape=(
                jax.ShapeDtypeStruct((rows, width), BF16),
                jax.ShapeDtypeStruct((feats, width), F32),
                jax.ShapeDtypeStruct((lane_blocks, LANES), F32),
            ),
            in_specs=[SM, SM, VM, VM] + [VM] * len(pieces),
            out_specs=(VM, VM, VM),
            scratch_shapes=[pltpu.VMEM((n_dev, lane_blocks * 8, LANES), F32)],
        )(place, note, back, one, *[piece for group, piece in pieces])
        return (layer_out, grad_tokens, grad_w_out, grad_gain.reshape(width))
    gains, att = extra
    high = gains.astype(BF16)
    low = (gains - high.astype(F32)).astype(BF16)
    ret = ret.reshape(slots, n_dev, per_peer, width).transpose(1, 0, 2, 3).reshape(n_dev, -1)
    both = jnp.broadcast_to(jnp.concatenate([high, low]).reshape(1, -1), (n_dev, 2 * width))
    sizes = (ret.shape[1], feats * rows)
    ret = jnp.concatenate([ret, att.reshape(n_dev, -1), both], axis=1).reshape(n_dev, -1, LANES)
    back = lax.all_to_all(ret, "ctx", 0, 0, tiled=True).reshape(n_dev, -1)
    rest = back[:, :sizes[0]].reshape(n_dev * slots, per_peer, width).astype(F32)
    total = jnp.zeros((n_dev, per_peer, width), F32).at[table.reshape(-1)].add(rest)
    grad_tokens = nn(one[place[0]], total.reshape(rows, width).astype(BF16)).astype(BF16)
    att = back[:, sizes[0]:sizes[0] + sizes[1]].reshape(n_dev, feats, rows)
    order = me ^ jnp.array(sum([group for group, piece in pieces], []))
    cots = jnp.concatenate([piece for group, piece in pieces]).reshape(n_dev, rows, width)
    grad_w_out = jnp.einsum("sft,stw->fw", att[order], cots, preferred_element_type=F32) * norm_scale
    parts = back[:, sizes[0] + sizes[1]:].reshape(n_dev, 2, width).astype(F32)
    grad_gain = jnp.sum(parts, axis=(0, 1)) * norm_scale
    return (layer_out, grad_tokens, grad_w_out, grad_gain)


def solution(mesh):
    placed = (
        P(("groups", "ctx"), None),
        P(("groups", "ctx")),
        P(("groups", "ctx"), None),
        P(("groups", "ctx")),
        P(),
        P(),
        P(),
        P(("groups", "ctx"), None),
    )
    return jax.shard_map(
        per_device,
        mesh=mesh,
        in_specs=placed,
        out_specs=(
            P(("groups", "ctx"), None),
            P(("groups", "ctx"), None),
            P(("groups", "ctx"), None),
            P("groups"),
        ),
        check_vma=False,
    )
```

time: 181 us -> 172 us (0.950)
  blocking collectives: 58.1 us -> 0 us
  waiting for transfers between devices: 52.4 us -> 105 us
  between operations: 14.7 us -> 1.4 us
  starting transfers between devices: 11.2 us -> 21.5 us
  matrix products: 3.7 us -> 0 us
  local copies, waits for them, and re-layouts: 4.11 us -> 7.13 us
  Pallas kernels: 32 us -> 34.6 us
  other arithmetic: 4.2 us -> 2.31 us
    ppermute x0 -> x6, waiting for transfers between devices: none -> 82.1 us  [swap(): return lax.ppermute(block, 'ctx', [(i, i ^ mask) for i in range(n_dev)])]
    all_to_all x1 -> x0, blocking collectives: 58.1 us -> none  [per_device(): lax.all_to_all(jnp.concatenate([ret, extra], axis=1), 'ctx', 0, 0, tiled=...]
    reduce_scatter x1 -> x0, waiting for transfers between devices: 19.4 us -> none  [per_device(): lax.psum_scatter(tn(att, cots), 'ctx', scatter_dimension=0, tiled=True)]
    all_to_all x2 -> x3, waiting for transfers between devices: 33 us -> 22.7 us  [the longest x1 15.1 us: per_device(): lax.all_to_all(msg, 'ctx', 0, 0, tiled=True, axis_index_groups=halves)]
    ppermute x0 -> x6, starting transfers between devices: none -> 9.09 us  [swap(): return lax.ppermute(block, 'ctx', [(i, i ^ mask) for i in range(n_dev)])]
    unnamed x7 -> x16, local copies, waits for them, and re-layouts: 2.18 us -> 6.48 us
    dot_general x1 -> x0, matrix products: 3.7 us -> none  [tn(): lax.dot_general(a, b, (((0,), (0,)), ((), ())), preferred_element_type=F32)]
    mul x2 -> x0, other arithmetic: 2.27 us -> none  [the longest x1 1.68 us: per_device(): lax.psum_scatter(tn(att, cots), 'ctx', scatter_dimension=0, tiled=True)]
  transfers between devices with their start and end apart: 3 -> 9, of which waited for: 3 -> 5; matrix products, arithmetic and copies ran while one was open for 1% -> 2% of each run, Pallas kernels for 2% -> 15%
where the time goes in v2:
time: 172 us
  waiting for transfers between devices  105 us (61%)
  Pallas kernels  34.6 us (20%)
  starting transfers between devices  21.5 us (12%)
  local copies, waits for them, and re-layouts  7.13 us (4%)
  other arithmetic  2.31 us (1%)
    ppermute x6, waiting for transfers between devices, swap(): return lax.ppermute(block, 'ctx', [(i, i ^ mask) for i in range(n_dev)])  82.1 us
    pallas_call x1, Pallas kernels, per_device(): pl.pallas_call(functools.partial(main_kernel, fits), out_shape=(jax.Shape...  26.5 us
    all_to_all x1, waiting for transfers between devices, per_device(): lax.all_to_all(msg, 'ctx', 0, 0, tiled=True, axis_index_groups=halves)  15.1 us
    ppermute x6, starting transfers between devices, swap(): return lax.ppermute(block, 'ctx', [(i, i ^ mask) for i in range(n_dev)])  9.09 us
    all_to_all x1, waiting for transfers between devices, per_device(): note = lax.all_to_all(note, 'ctx', 0, 0, tiled=True)  7.56 us
    unnamed x16, local copies, waits for them, and re-layouts  6.48 us
    all_to_all x1, starting transfers between devices, per_device(): back = lax.all_to_all(ret, 'ctx', 0, 0, tiled=True)  4.93 us
    pallas_call x1, Pallas kernels, per_device(): pl.pallas_call(functools.partial(finish_kernel, n_dev, slots, masks, norm...  4.7 us
  transfers between devices with their start and end apart: 9, of which 5 were waited for; matrix products, arithmetic and copies ran while one was open for 2% of the time, Pallas kernels for 15%

profile of v2, /device:TPU:0, one launch (start us, length us, event | category | flops | bytes accessed | tf_op | source)
XLA Modules:
  0.0 171.8 jit_solution(14188542786204492102)
XLA Ops:
  0.6 4.1 %collective-permute-start = (bf16[128,1024]{1,0:T(8,128)(2,1)}, bf16[128,1024]{1,0:T(8,128)(2,1)S(1)}, u32[]{:S(2)}, u32[]{:S(2)}) collective-permute-start(bf16[128,1024]{1,0:T(8,128)(2,1)} %own_ref.1), channel_id=1, source_target_pairs={{0,8},{1,9},{2,10},{3,11},{4,12},{5,13},{6,14},{7,15},{8,0},{9,1},... | collective-permute-start | bytes 786440 | tf_op jit(solution)/shard_map/ppermute | solution.py:246
  4.8 0.7 pad_add_fusion
  5.4 0.6 broadcast_in_dim.12
  6.1 3.9 %all-to-all-start = ((s32[16,1,256]{2,1,0:T(1,128)}), s32[16,1,256]{2,1,0:T(1,128)S(1)}, u32[]{:S(2)}, u32[]{:S(2)}) async-start(s32[16,1,256]{2,1,0:T(1,128)} %broadcast_in_dim.12), calls=%async_computation | async-start | bytes 32768 | tf_op jit(solution)/shard_map/all_to_all | solution.py:282
  10.0 0.6 pad_add_fusion.1.place_ref
  10.6 7.6 %all-to-all-done.table_ref.note_ref = s32[16,1,256]{2,1,0:T(1,128)S(1)} async-done(((s32[16,1,256]{2,1,0:T(1,128)}), s32[16,1,256]{2,1,0:T(1,128)S(1)}, u32[]{:S(2)}, u32[]{:S(2)}) %all-to-all-start) | async-done | bytes 16416 | tf_op jit(solution)/shard_map/all_to_all | solution.py:282
  18.2 0.0 copy-start.5
  18.2 0.0 collective-permute-done.mirror_ref
  18.2 0.6 copy-done.5
  18.8 0.0 copy-start.6
  18.8 0.7 copy-done.6
  19.5 3.5 %shard_map.111 = (bf16[8,2,5,8,1024]{4,3,2,1,0:T(8,128)(2,1)}, bf16[2,128,128]{2,1,0:T(8,128)(2,1)}, bf16[2,16,8,1024]{3,2,1,0:T(8,128)(2,1)}) custom-call(s32[2]{0:T(128)} %pad_add_fusion.1.place_ref, s32[16,1,256]{2,1,0:T(1,128)} %copy-done.5, s32[16,1,256]{2,1,0:T(1,128)} %copy-done.5, bf16[128,1024]{1,0:T(8,128)(2,1)} %own_ref.1, bf16[128,1024]{1,0:T(8,128)(2,1)} %copy-done.6), custom_call_target="tpu_custom_call" | custom-call | tf_op jit(solution)/shard_map/pallas_call | solution.py:286
  23.0 3.6 %all-to-all-start.1 = ((bf16[8,2,5,8,1024]{4,3,2,1,0:T(8,128)(2,1)}), bf16[8,2,5,8,1024]{4,3,2,1,0:T(8,128)(2,1)S(1)}, u32[]{:S(2)}, u32[]{:S(2)}) async-start(bf16[8,2,5,8,1024]{4,3,2,1,0:T(8,128)(2,1)} %get-tuple-element.11), calls=%async_computation.1 | async-start | bytes 2621440 | tf_op jit(solution)/shard_map/all_to_all | solution.py:301
  26.6 1.9 %collective-permute-start.1 = (bf16[128,1024]{1,0:T(8,128)(2,1)}, bf16[128,1024]{1,0:T(8,128)(2,1)S(1)}, u32[]{:S(2)}, u32[]{:S(2)}) collective-permute-start(bf16[128,1024]{1,0:T(8,128)(2,1)} %cot_ref.1), channel_id=1, source_target_pairs={{0,2},{1,3},{2,0},{3,1},{4,6},{5,7},{6,4},{7,5},{8,10},{9,11},{10,... | collective-permute-start | bytes 786440 | tf_op jit(solution)/shard_map/ppermute | solution.py:246
  29.1 15.1 %all-to-all-done.1.arrived_ref = bf16[8,2,5,8,1024]{4,3,2,1,0:T(8,128)(2,1)S(1)} async-done(((bf16[8,2,5,8,1024]{4,3,2,1,0:T(8,128)(2,1)}), bf16[8,2,5,8,1024]{4,3,2,1,0:T(8,128)(2,1)S(1)}, u32[]{:S(2)}, u32[]{:S(2)}) %all-to-all-start.1) | async-done | bytes 1310752 | tf_op jit(solution)/shard_map/all_to_all | solution.py:301
  44.3 0.0 copy-start.2
  44.3 1.1 copy-done.2
  45.3 26.5 %shard_map.112 = (bf16[128,1024]{1,0:T(8,128)(2,1)}, bf16[16,400,128]{2,1,0:T(8,128)(2,1)}) custom-call(s32[1]{0:T(128)S(6)} %copy.14.count_ref, bf16[8,2,5,8,1024]{4,3,2,1,0:T(8,128)(2,1)} %copy-done.2, s32[1,128]{1,0:T(1,128)} %bitcast.7, f32[1,1024]{1,0:T(1,128)} %bitcast.8, bf16[128,1024]{1,0:T(8,128)(2,1)} %cot_ref.1, bf16[1024,3072]{1,0:T(8,128)(2,1)} %wqkv_ref.1, ...), custom_call_target="tpu_custom_call" | custom-call | flops 9395240960 | bytes 16777216 | tf_op jit(solution)/shard_map/pallas_call | solution.py:313
  71.8 4.9 %all-to-all-start.2 = ((bf16[16,400,128]{2,1,0:T(8,128)(2,1)}), bf16[16,400,128]{2,1,0:T(8,128)(2,1)S(1)}, u32[]{:S(2)}, u32[]{:S(2)}) async-start(bf16[16,400,128]{2,1,0:T(8,128)(2,1)} %get-tuple-element.13), calls=%async_computation.2 | async-start | bytes 3276800 | tf_op jit(solution)/shard_map/all_to_all | solution.py:339
  76.8 0.0 collective-permute-done.1
  76.8 1.0 pad_maximum_fusion
  77.8 2.9 %collective-permute-start.2 = (bf16[256,1024]{1,0:T(8,128)(2,1)S(1)}, bf16[256,1024]{1,0:T(8,128)(2,1)S(1)}, u32[]{:S(2)}, u32[]{:S(2)}) collective-permute-start(bf16[256,1024]{1,0:T(8,128)(2,1)S(1)} %pad_maximum_fusion), channel_id=1, source_target_pairs={{0,8},{1,9},{2,10},{3,11},{4,12},{5,13},{6,14},{7,15},{8,0},{9,1},... | collective-permute-start | bytes 1572872 | tf_op jit(solution)/shard_map/ppermute | solution.py:246
  80.6 1.0 constant_dynamic-update-slice_fusion.2
  81.6 56.8 %collective-permute-done.2 = bf16[256,1024]{1,0:T(8,128)(2,1)S(1)} collective-permute-done((bf16[256,1024]{1,0:T(8,128)(2,1)S(1)}, bf16[256,1024]{1,0:T(8,128)(2,1)S(1)}, u32[]{:S(2)}, u32[]{:S(2)}) %collective-permute-start.2) | collective-permute-done | bytes 524320 | tf_op jit(solution)/shard_map/ppermute | solution.py:246
  138.5 0.0 copy-start.1
  138.5 0.1 collective-permute-start.3
  138.6 0.1 collective-permute-start.4
  138.6 24.5 %collective-permute-done.3.rest_1_ = bf16[512,1024]{1,0:T(8,128)(2,1)S(1)} collective-permute-done((bf16[512,1024]{1,0:T(8,128)(2,1)S(1)}, bf16[512,1024]{1,0:T(8,128)(2,1)S(1)}, u32[]{:S(2)}, u32[]{:S(2)}) %collective-permute-start.3) | collective-permute-done | bytes 1048608 | tf_op jit(solution)/shard_map/ppermute | solution.py:246
  163.1 0.0 copy-start.3
  163.1 0.0 collective-permute-start.5
  163.2 0.0 collective-permute-done.4.rest_2_
  163.2 1.0 copy-done.3
  164.1 0.0 copy-start.4
  164.1 1.0 copy-done.4
  165.1 0.8 collective-permute-done.5.rest_3_
  165.9 0.0 all-to-all-done.2.back_ref
  165.9 0.0 copy-start
  165.9 0.0 copy-done.1
  166.0 1.2 copy-done
  167.1 4.7 %shard_map.113 = (bf16[128,1024]{1,0:T(8,128)(2,1)}, f32[64,1024]{1,0:T(8,128)}, f32[8,128]{1,0:T(8,128)}) custom-call(s32[2]{0:T(128)} %pad_add_fusion.1.place_ref, s32[16,1,256]{2,1,0:T(1,128)} %copy-done.5, bf16[16,400,128]{2,1,0:T(8,128)(2,1)} %copy-done, bf16[2,128,128]{2,1,0:T(8,128)(2,1)} %get-tuple-element.14.one_ref, bf16[512,1024]{1,0:T(8,128)(2,1)} %copy-done.1, ...), custom_call_target="tpu_custom_call" | custom-call | tf_op jit(solution)/shard_map/pallas_call | solution.py:341
  (2 shorter events, 0.1 us)
Async XLA Ops:
  0.6 17.6 %collective-permute-start = (bf16[128,1024]{1,0:T(8,128)(2,1)}, bf16[128,1024]{1,0:T(8,128)(2,1)S(1)}, u32[]{:S(2)}, u32[]{:S(2)}) collective-permute-start(bf16[128,1024]{1,0:T(8,128)(2,1)} %own_ref.1), channel_id=1, source_target_pairs={{0,8},{1,9},{2,10},{3,11},{4,12},{5,13},{6,14},{7,15},{8,0},{9,1},... | collective-permute-start | bytes 786440 | tf_op jit(solution)/shard_map/ppermute | solution.py:246
  6.1 12.2 %all-to-all-start = ((s32[16,1,256]{2,1,0:T(1,128)}), s32[16,1,256]{2,1,0:T(1,128)S(1)}, u32[]{:S(2)}, u32[]{:S(2)}) async-start(s32[16,1,256]{2,1,0:T(1,128)} %broadcast_in_dim.12), calls=%async_computation | async-start | bytes 32768 | tf_op jit(solution)/shard_map/all_to_all | solution.py:282
  18.2 0.6 copy-start.5
  18.8 0.7 copy-start.6
  23.0 21.3 %all-to-all-start.1 = ((bf16[8,2,5,8,1024]{4,3,2,1,0:T(8,128)(2,1)}), bf16[8,2,5,8,1024]{4,3,2,1,0:T(8,128)(2,1)S(1)}, u32[]{:S(2)}, u32[]{:S(2)}) async-start(bf16[8,2,5,8,1024]{4,3,2,1,0:T(8,128)(2,1)} %get-tuple-element.11), calls=%async_computation.1 | async-start | bytes 2621440 | tf_op jit(solution)/shard_map/all_to_all | solution.py:301
  26.6 50.2 %collective-permute-start.1 = (bf16[128,1024]{1,0:T(8,128)(2,1)}, bf16[128,1024]{1,0:T(8,128)(2,1)S(1)}, u32[]{:S(2)}, u32[]{:S(2)}) collective-permute-start(bf16[128,1024]{1,0:T(8,128)(2,1)} %cot_ref.1), channel_id=1, source_target_pairs={{0,2},{1,3},{2,0},{3,1},{4,6},{5,7},{6,4},{7,5},{8,10},{9,11},{10,... | collective-permute-start | bytes 786440 | tf_op jit(solution)/shard_map/ppermute | solution.py:246
  44.3 1.1 copy-start.2
  71.8 94.1 %all-to-all-start.2 = ((bf16[16,400,128]{2,1,0:T(8,128)(2,1)}), bf16[16,400,128]{2,1,0:T(8,128)(2,1)S(1)}, u32[]{:S(2)}, u32[]{:S(2)}) async-start(bf16[16,400,128]{2,1,0:T(8,128)(2,1)} %get-tuple-element.13), calls=%async_computation.2 | async-start | bytes 3276800 | tf_op jit(solution)/shard_map/all_to_all | solution.py:339
  77.8 60.7 %collective-permute-start.2 = (bf16[256,1024]{1,0:T(8,128)(2,1)S(1)}, bf16[256,1024]{1,0:T(8,128)(2,1)S(1)}, u32[]{:S(2)}, u32[]{:S(2)}) collective-permute-start(bf16[256,1024]{1,0:T(8,128)(2,1)S(1)} %pad_maximum_fusion), channel_id=1, source_target_pairs={{0,8},{1,9},{2,10},{3,11},{4,12},{5,13},{6,14},{7,15},{8,0},{9,1},... | collective-permute-start | bytes 1572872 | tf_op jit(solution)/shard_map/ppermute | solution.py:246
  138.5 27.5 %copy-start.1 = (bf16[512,1024]{1,0:T(8,128)(2,1)}, bf16[512,1024]{1,0:T(8,128)(2,1)S(1)}, u32[]{:S(2)}) copy-start(bf16[512,1024]{1,0:T(8,128)(2,1)S(1)} %constant_dynamic-update-slice_fusion.rest_0_) | copy-start | bytes 3145732
  138.5 24.7 %collective-permute-start.3 = (bf16[512,1024]{1,0:T(8,128)(2,1)S(1)}, bf16[512,1024]{1,0:T(8,128)(2,1)S(1)}, u32[]{:S(2)}, u32[]{:S(2)}) collective-permute-start(bf16[512,1024]{1,0:T(8,128)(2,1)S(1)} %constant_dynamic-update-slice_fusion.rest_0_), channel_id=1, source_target_pairs={{0,4},{1,5},{2,6},{3,7},{4,0},{5,1},{6,2},{7,3},{8,12},{9,13},{10,... | collective-permute-start | bytes 3145736 | tf_op jit(solution)/shard_map/ppermute | solution.py:246
  138.6 24.6 %collective-permute-start.4 = (bf16[512,1024]{1,0:T(8,128)(2,1)S(1)}, bf16[512,1024]{1,0:T(8,128)(2,1)S(1)}, u32[]{:S(2)}, u32[]{:S(2)}) collective-permute-start(bf16[512,1024]{1,0:T(8,128)(2,1)S(1)} %constant_dynamic-update-slice_fusion.rest_0_), channel_id=1, source_target_pairs={{0,1},{1,0},{2,3},{3,2},{4,5},{5,4},{6,7},{7,6},{8,9},{9,8},{10,11... | collective-permute-start | bytes 3145736 | tf_op jit(solution)/shard_map/ppermute | solution.py:246
  163.1 1.0 copy-start.3
  163.1 2.8 %collective-permute-start.5 = (bf16[512,1024]{1,0:T(8,128)(2,1)S(1)}, bf16[512,1024]{1,0:T(8,128)(2,1)}, u32[]{:S(2)}, u32[]{:S(2)}) collective-permute-start(bf16[512,1024]{1,0:T(8,128)(2,1)S(1)} %collective-permute-done.3.rest_1_), channel_id=1, source_target_pairs={{0,1},{1,0},{2,3},{3,2},{4,5},{5,4},{6,7},{7,6},{8,9},{9,8},{10,11... | collective-permute-start | bytes 3145736 | tf_op jit(solution)/shard_map/ppermute | solution.py:246
  164.1 1.0 copy-start.4
  165.9 1.2 copy-start

commit v3 on v2

--- a/solution.py
+++ b/solution.py
@@ -6,6 +6,7 @@
 from jax.experimental import pallas as pl
 from jax.experimental.pallas import tpu as pltpu
 from jax.sharding import PartitionSpec as P
+
 
 HEADS = 16
 BLOCK = 128
@@ -50,7 +51,9 @@
     return jnp.transpose(wide)[:1, :].astype(jnp.int32)
 
 
-def pack_kernel(n_dev, slots, per_peer, place_ref, table_ref, note_ref, own_ref, mirror_ref, msg_ref, one_ref, sorted_ref):
+def pack_kernel(n_dev, slots, per_peer, place_ref, table_ref, note_ref, own_ref, mirror_ref, cot_ref, other_ref, msg_ref, one_ref, sorted_ref, held_ref):
+    held_ref[pl.ds(0, cot_ref.shape[0]), :] = cot_ref[...]
+    held_ref[pl.ds(cot_ref.shape[0], cot_ref.shape[0]), :] = other_ref[...]
     rows, width = own_ref.shape
     half = n_dev // 2
     upper, seat = place_ref[0], place_ref[1]
@@ -246,20 +249,6 @@
     return lax.ppermute(block, "ctx", [(i, i ^ mask) for i in range(n_dev)])
 
 
-def gather_cotangent(cotangent, n_dev):
-    masks = [2, n_dev // 2]
-    masks += [m for m in (1 << b for b in range(n_dev.bit_length() - 1)) if m not in masks + [1]]
-    held, names = cotangent, [0]
-    for mask in masks[:-1]:
-        other = swap(held, mask)
-        held = jnp.concatenate([held, other])
-        names = names + [m ^ mask for m in names]
-    other = swap(held, masks[-1])
-    others = [m ^ masks[-1] for m in names]
-    pieces = [(names, held), (others, other)]
-    return pieces + [([m ^ 1 for m in group], swap(piece, 1)) for group, piece in pieces]
-
-
 def per_device(
     raster_tokens, hilbert_perm, neighbors, neighbor_counts, norm_gain, w_qkv, w_out, cotangent
 ):
@@ -278,27 +267,37 @@
     note = jnp.concatenate([hilbert_perm, jnp.pad(neighbors[0], (0, rows - slots))])
     note = jnp.broadcast_to(note[None, None], (n_dev, 1, 2 * rows))
     mirror = swap(raster_tokens, half)
-    pieces = gather_cotangent(cotangent, n_dev)
+    other = swap(cotangent, half // 2)
     note = lax.all_to_all(note, "ctx", 0, 0, tiled=True)
+    note, other = lax.optimization_barrier((note, other))
 
     msg_shape = (half, 2, slots, per_peer, width) if fits else (8, LANES)
     sort_shape = (2, n_dev, per_peer, width) if fits else (2, rows, width)
-    msg, one, in_order = pl.pallas_call(
+    msg, one, in_order, held = pl.pallas_call(
         functools.partial(pack_kernel, n_dev, slots, per_peer),
         out_shape=(
             jax.ShapeDtypeStruct(msg_shape, BF16),
             jax.ShapeDtypeStruct((2, rows, rows), BF16),
             jax.ShapeDtypeStruct(sort_shape, BF16),
+            jax.ShapeDtypeStruct((2 * rows, width), BF16),
         ),
-        in_specs=[SM, SM, VM, VM, VM],
-        out_specs=(VM, VM, VM),
-    )(place, note, note, raster_tokens, mirror)
+        in_specs=[SM, SM] + [VM] * 5,
+        out_specs=(VM,) * 4,
+    )(place, note, note, raster_tokens, mirror, cotangent, other)
     table = note[:, 0, rows:rows + slots]
     if not fits:
         mine = lax.dynamic_slice_in_dim(table, place[0] * half, half, 0)
         msg = in_order.reshape(2, n_dev, per_peer, width)[:, mine].transpose(1, 0, 2, 3, 4)
     halves = [list(range(half)), list(range(half, n_dev))]
     arrived = lax.all_to_all(msg, "ctx", 0, 0, tiled=True, axis_index_groups=halves)
+    arrived, held = lax.optimization_barrier((arrived, held))
+    names = [0, half // 2]
+    bits = [1 << b for b in range(n_dev.bit_length() - 1)]
+    for mask in [m for m in bits if m not in (1, 2, half, half // 2)]:
+        held = jnp.concatenate([held, swap(held, mask)])
+        names = names + [m ^ mask for m in names]
+    across = swap(held, half)
+    beside = swap(held, 2)
     if fits:
         ret_shape = (n_dev, slots * lane_blocks * 8 + feats + 16, LANES)
         extra_shapes = ()
@@ -336,7 +335,18 @@
     )(neighbor_counts, arrived, hilbert_perm[None], norm_gain[None], cotangent, w_qkv, w_out)
 
     if fits:
+        ret, across, beside = lax.optimization_barrier((ret, across, beside))
         back = lax.all_to_all(ret, "ctx", 0, 0, tiled=True)
+    corner = swap(across, 2)
+    pieces = [
+        (names, held),
+        ([m ^ half for m in names], across),
+        ([m ^ 2 for m in names], beside),
+        ([m ^ 2 ^ half for m in names], corner),
+    ]
+    for group, piece in list(pieces):
+        pieces.append(([m ^ 1 for m in group], swap(piece, 1)))
+    if fits:
         masks = [group for group, piece in pieces]
         grad_tokens, grad_w_out, grad_gain = pl.pallas_call(
             functools.partial(finish_kernel, n_dev, slots, masks, norm_scale),
@@ -381,6 +391,7 @@
         P(),
         P(("groups", "ctx"), None),
     )
+
     return jax.shard_map(
         per_device,
         mesh=mesh,

time: 172 us -> 122 us (0.71)
  the two profiles are of different devices: /device:TPU:0 before, /device:TPU:15 now
where the time goes in v3:
time: 122 us
  waiting for transfers between devices  52.5 us (43%)
  Pallas kernels  35 us (29%)
  starting transfers between devices  26.5 us (22%)
  local copies, waits for them, and re-layouts  4.95 us (4%)
  between operations  1.35 us (1%)
  other arithmetic  1.3 us (1%)
    pallas_call x1, Pallas kernels, per_device(): pl.pallas_call(functools.partial(main_kernel, fits), out_shape=(jax.Shape...  26.5 us
    ppermute x9, waiting for transfers between devices, swap(): return lax.ppermute(block, 'ctx', [(i, i ^ mask) for i in range(n_dev)])  22.8 us
    all_to_all x1, waiting for transfers between devices, per_device(): lax.all_to_all(msg, 'ctx', 0, 0, tiled=True, axis_index_groups=halves)  14.6 us
    all_to_all x1, waiting for transfers between devices, per_device(): back = lax.all_to_all(ret, 'ctx', 0, 0, tiled=True)  9.51 us
    ppermute x9, starting transfers between devices, swap(): return lax.ppermute(block, 'ctx', [(i, i ^ mask) for i in range(n_dev)])  7.91 us
    all_to_all x1, starting transfers between devices, per_device(): back = lax.all_to_all(ret, 'ctx', 0, 0, tiled=True)  6.92 us
    all_to_all x1, starting transfers between devices, per_device(): lax.all_to_all(msg, 'ctx', 0, 0, tiled=True, axis_index_groups=halves)  5.97 us
    all_to_all x1, starting transfers between devices, per_device(): note = lax.all_to_all(note, 'ctx', 0, 0, tiled=True)  5.68 us
  transfers between devices with their start and end apart: 12, of which 4 were waited for; matrix products, arithmetic and copies ran while one was open for 2% of the time, Pallas kernels for 22%

profile of v3, /device:TPU:15, one launch (start us, length us, event | category | flops | bytes accessed | tf_op | source)
XLA Modules:
  0.0 121.6 jit_solution(3465647401968204954)
XLA Ops:
  0.6 0.2 collective-permute-start
  0.9 2.3 %collective-permute-start.1 = (bf16[128,1024]{1,0:T(8,128)(2,1)}, bf16[128,1024]{1,0:T(8,128)(2,1)S(1)}, u32[]{:S(2)}, u32[]{:S(2)}) collective-permute-start(bf16[128,1024]{1,0:T(8,128)(2,1)} %own_ref.1), channel_id=1, source_target_pairs={{0,8},{1,9},{2,10},{3,11},{4,12},{5,13},{6,14},{7,15},{8,0},{9,1},... | collective-permute-start | bytes 786440 | tf_op jit(solution)/shard_map/ppermute | solution.py:249
  3.2 0.7 pad_add_fusion
  3.9 0.6 broadcast_in_dim.12
  4.5 5.7 %all-to-all-start = ((s32[16,1,256]{2,1,0:T(1,128)}), s32[16,1,256]{2,1,0:T(1,128)S(1)}, u32[]{:S(2)}, u32[]{:S(2)}) async-start(s32[16,1,256]{2,1,0:T(1,128)} %broadcast_in_dim.12), calls=%async_computation | async-start | bytes 32768 | tf_op jit(solution)/shard_map/all_to_all | solution.py:271
  10.2 0.6 pad_add_fusion.1.place_ref
  10.8 5.6 %all-to-all-done.table_ref.note_ref = s32[16,1,256]{2,1,0:T(1,128)S(1)} async-done(((s32[16,1,256]{2,1,0:T(1,128)}), s32[16,1,256]{2,1,0:T(1,128)S(1)}, u32[]{:S(2)}, u32[]{:S(2)}) %all-to-all-start) | async-done | bytes 16416 | tf_op jit(solution)/shard_map/all_to_all | solution.py:271
  16.4 0.0 copy-start.9
  16.4 0.0 collective-permute-done.other_ref
  16.4 0.0 copy-start.10
  16.4 0.0 collective-permute-done.1.mirror_ref
  16.4 0.6 copy-done.9
  17.0 0.1 copy-done.10
  17.1 0.0 copy-start.11
  17.1 0.7 copy-done.11
  17.8 3.8 %shard_map.111 = (bf16[8,2,5,8,1024]{4,3,2,1,0:T(8,128)(2,1)}, bf16[2,128,128]{2,1,0:T(8,128)(2,1)}, bf16[2,16,8,1024]{3,2,1,0:T(8,128)(2,1)}, bf16[256,1024]{1,0:T(8,128)(2,1)}) custom-call(s32[2]{0:T(128)} %pad_add_fusion.1.place_ref, s32[16,1,256]{2,1,0:T(1,128)} %copy-done.9, s32[16,1,256]{2,1,0:T(1,128)} %copy-done.9, bf16[128,1024]{1,0:T(8,128)(2,1)} %own_ref.1, ...), custom_call_target="tpu_custom_call" | custom-call | tf_op jit(solution)/shard_map/pallas_call | solution.py:276
  21.6 0.0 copy-start.2
  21.6 6.0 %all-to-all-start.1 = ((bf16[8,2,5,8,1024]{4,3,2,1,0:T(8,128)(2,1)}), bf16[8,2,5,8,1024]{4,3,2,1,0:T(8,128)(2,1)S(1)}, u32[]{:S(2)}, u32[]{:S(2)}) async-start(bf16[8,2,5,8,1024]{4,3,2,1,0:T(8,128)(2,1)} %get-tuple-element.21), calls=%async_computation.1 | async-start | bytes 2621440 | tf_op jit(solution)/shard_map/all_to_all | solution.py:292
  28.2 14.6 %all-to-all-done.1.arrived_ref = bf16[8,2,5,8,1024]{4,3,2,1,0:T(8,128)(2,1)S(1)} async-done(((bf16[8,2,5,8,1024]{4,3,2,1,0:T(8,128)(2,1)}), bf16[8,2,5,8,1024]{4,3,2,1,0:T(8,128)(2,1)S(1)}, u32[]{:S(2)}, u32[]{:S(2)}) %all-to-all-start.1) | async-done | bytes 1310752 | tf_op jit(solution)/shard_map/all_to_all | solution.py:292
  42.8 0.0 copy-done.2
  42.8 0.4 collective-permute-start.3
  43.2 1.4 %collective-permute-start.2 = (bf16[256,1024]{1,0:T(8,128)(2,1)S(1)}, bf16[256,1024]{1,0:T(8,128)(2,1)S(1)}, u32[]{:S(2)}, u32[]{:S(2)}) collective-permute-start(bf16[256,1024]{1,0:T(8,128)(2,1)S(1)} %copy-done.2), channel_id=1, source_target_pairs={{0,8},{1,9},{2,10},{3,11},{4,12},{5,13},{6,14},{7,15},{8,0},{9,1},... | collective-permute-start | bytes 1572872 | tf_op jit(solution)/shard_map/ppermute | solution.py:249
  44.6 0.0 copy-done.1
  44.6 26.5 %shard_map.112 = (bf16[128,1024]{1,0:T(8,128)(2,1)}, bf16[16,400,128]{2,1,0:T(8,128)(2,1)}) custom-call(s32[1]{0:T(128)S(6)} %copy.12.count_ref, bf16[8,2,5,8,1024]{4,3,2,1,0:T(8,128)(2,1)} %copy-done.1, s32[1,128]{1,0:T(1,128)} %bitcast.7, f32[1,1024]{1,0:T(1,128)} %bitcast.8, bf16[128,1024]{1,0:T(8,128)(2,1)} %cot_ref.3, bf16[1024,3072]{1,0:T(8,128)(2,1)} %wqkv_ref.1, ...), custom_call_target="tpu_custom_call" | custom-call | flops 9395240960 | bytes 16777216 | tf_op jit(solution)/shard_map/pallas_call | solution.py:312
  71.1 0.0 collective-permute-done.3.rest_2_
  71.1 0.0 collective-permute-done.2.rest_1_
  71.1 0.0 copy-start.4
  71.1 6.9 %all-to-all-start.2 = ((bf16[16,400,128]{2,1,0:T(8,128)(2,1)}), bf16[16,400,128]{2,1,0:T(8,128)(2,1)S(1)}, u32[]{:S(2)}, u32[]{:S(2)}) async-start(bf16[16,400,128]{2,1,0:T(8,128)(2,1)} %get-tuple-element.27), calls=%async_computation.2 | async-start | bytes 3276800 | tf_op jit(solution)/shard_map/all_to_all | solution.py:339
  78.1 0.3 collective-permute-start.4
  78.3 0.7 collective-permute-start.5
  79.0 0.0 copy-done.4
  79.0 0.0 collective-permute-start.6
  79.0 0.0 copy-done.3
  79.0 0.5 collective-permute-start.7
  79.5 22.8 %collective-permute-done.4.rest_3_ = bf16[256,1024]{1,0:T(8,128)(2,1)S(1)} collective-permute-done((bf16[256,1024]{1,0:T(8,128)(2,1)S(1)}, bf16[256,1024]{1,0:T(8,128)(2,1)S(1)}, u32[]{:S(2)}, u32[]{:S(2)}) %collective-permute-start.4) | collective-permute-done | bytes 524320 | tf_op jit(solution)/shard_map/ppermute | solution.py:249
  102.3 2.1 %collective-permute-start.8 = (bf16[256,1024]{1,0:T(8,128)(2,1)S(1)}, bf16[256,1024]{1,0:T(8,128)(2,1)}, u32[]{:S(2)}, u32[]{:S(2)}) collective-permute-start(bf16[256,1024]{1,0:T(8,128)(2,1)S(1)} %collective-permute-done.4.rest_3_), channel_id=1, source_target_pairs={{0,1},{1,0},{2,3},{3,2},{4,5},{5,4},{6,7},{7,6},{8,9},{9,8},{10,11... | collective-permute-start | bytes 1572872 | tf_op jit(solution)/shard_map/ppermute | solution.py:249
  104.4 0.0 collective-permute-done.5.rest_4_
  104.4 0.0 collective-permute-done.7.rest_6_
  104.4 0.0 copy-start.8
  104.5 0.0 collective-permute-done.6.rest_5_
  104.5 0.0 copy-done.5
  104.5 0.8 copy-done.6
  105.2 0.2 copy-done.8
  105.4 0.8 copy-done.7
  106.2 0.0 collective-permute-done.8.rest_7_
  106.2 9.5 %all-to-all-done.2.back_ref = bf16[16,400,128]{2,1,0:T(8,128)(2,1)S(1)} async-done(((bf16[16,400,128]{2,1,0:T(8,128)(2,1)}), bf16[16,400,128]{2,1,0:T(8,128)(2,1)S(1)}, u32[]{:S(2)}, u32[]{:S(2)}) %all-to-all-start.2) | async-done | bytes 1638432 | tf_op jit(solution)/shard_map/all_to_all | solution.py:339
  115.7 1.2 copy-done
  116.9 4.7 %shard_map.113 = (bf16[128,1024]{1,0:T(8,128)(2,1)}, f32[64,1024]{1,0:T(8,128)}, f32[8,128]{1,0:T(8,128)}) custom-call(s32[2]{0:T(128)} %pad_add_fusion.1.place_ref, s32[16,1,256]{2,1,0:T(1,128)} %copy-done.9, bf16[16,400,128]{2,1,0:T(8,128)(2,1)} %copy-done, bf16[2,128,128]{2,1,0:T(8,128)(2,1)} %get-tuple-element.28.one_ref, ...), custom_call_target="tpu_custom_call" | custom-call | tf_op jit(solution)/shard_map/pallas_call | solution.py:351
  (6 shorter events, 0.0 us)
Async XLA Ops:
  0.6 15.8 %collective-permute-start = (bf16[128,1024]{1,0:T(8,128)(2,1)}, bf16[128,1024]{1,0:T(8,128)(2,1)S(1)}, u32[]{:S(2)}, u32[]{:S(2)}) collective-permute-start(bf16[128,1024]{1,0:T(8,128)(2,1)} %cot_ref.3), channel_id=1, source_target_pairs={{0,4},{1,5},{2,6},{3,7},{4,0},{5,1},{6,2},{7,3},{8,12},{9,13},{10,... | collective-permute-start | bytes 786440 | tf_op jit(solution)/shard_map/ppermute | solution.py:249
  0.9 15.5 %collective-permute-start.1 = (bf16[128,1024]{1,0:T(8,128)(2,1)}, bf16[128,1024]{1,0:T(8,128)(2,1)S(1)}, u32[]{:S(2)}, u32[]{:S(2)}) collective-permute-start(bf16[128,1024]{1,0:T(8,128)(2,1)} %own_ref.1), channel_id=1, source_target_pairs={{0,8},{1,9},{2,10},{3,11},{4,12},{5,13},{6,14},{7,15},{8,0},{9,1},... | collective-permute-start | bytes 786440 | tf_op jit(solution)/shard_map/ppermute | solution.py:249
  4.5 11.9 %all-to-all-start = ((s32[16,1,256]{2,1,0:T(1,128)}), s32[16,1,256]{2,1,0:T(1,128)S(1)}, u32[]{:S(2)}, u32[]{:S(2)}) async-start(s32[16,1,256]{2,1,0:T(1,128)} %broadcast_in_dim.12), calls=%async_computation | async-start | bytes 32768 | tf_op jit(solution)/shard_map/all_to_all | solution.py:271
  16.4 0.6 copy-start.9
  16.4 0.7 copy-start.10
  17.1 0.7 copy-start.11
  21.6 21.2 %copy-start.2 = (bf16[256,1024]{1,0:T(8,128)(2,1)S(1)}, bf16[256,1024]{1,0:T(8,128)(2,1)}, u32[]{:S(2)}) copy-start(bf16[256,1024]{1,0:T(8,128)(2,1)} %get-tuple-element.26.rest_0_) | copy-start | bytes 1572868
  21.6 21.2 %all-to-all-start.1 = ((bf16[8,2,5,8,1024]{4,3,2,1,0:T(8,128)(2,1)}), bf16[8,2,5,8,1024]{4,3,2,1,0:T(8,128)(2,1)S(1)}, u32[]{:S(2)}, u32[]{:S(2)}) async-start(bf16[8,2,5,8,1024]{4,3,2,1,0:T(8,128)(2,1)} %get-tuple-element.21), calls=%async_computation.1 | async-start | bytes 2621440 | tf_op jit(solution)/shard_map/all_to_all | solution.py:292
  42.8 1.8 %copy-start.1 = (bf16[8,2,5,8,1024]{4,3,2,1,0:T(8,128)(2,1)}, bf16[8,2,5,8,1024]{4,3,2,1,0:T(8,128)(2,1)S(1)}, u32[]{:S(2)}) copy-start(bf16[8,2,5,8,1024]{4,3,2,1,0:T(8,128)(2,1)S(1)} %all-to-all-done.1.arrived_ref) | copy-start | bytes 3932164
  42.8 28.3 %collective-permute-start.3 = (bf16[256,1024]{1,0:T(8,128)(2,1)S(1)}, bf16[256,1024]{1,0:T(8,128)(2,1)S(1)}, u32[]{:S(2)}, u32[]{:S(2)}) collective-permute-start(bf16[256,1024]{1,0:T(8,128)(2,1)S(1)} %copy-done.2), channel_id=1, source_target_pairs={{0,2},{1,3},{2,0},{3,1},{4,6},{5,7},{6,4},{7,5},{8,10},{9,11},{10,... | collective-permute-start | bytes 1572872 | tf_op jit(solution)/shard_map/ppermute | solution.py:249
  43.2 27.9 %collective-permute-start.2 = (bf16[256,1024]{1,0:T(8,128)(2,1)S(1)}, bf16[256,1024]{1,0:T(8,128)(2,1)S(1)}, u32[]{:S(2)}, u32[]{:S(2)}) collective-permute-start(bf16[256,1024]{1,0:T(8,128)(2,1)S(1)} %copy-done.2), channel_id=1, source_target_pairs={{0,8},{1,9},{2,10},{3,11},{4,12},{5,13},{6,14},{7,15},{8,0},{9,1},... | collective-permute-start | bytes 1572872 | tf_op jit(solution)/shard_map/ppermute | solution.py:249
  71.1 7.9 %copy-start.3 = (bf16[256,1024]{1,0:T(8,128)(2,1)}, bf16[256,1024]{1,0:T(8,128)(2,1)S(1)}, u32[]{:S(2)}) copy-start(bf16[256,1024]{1,0:T(8,128)(2,1)S(1)} %collective-permute-done.3.rest_2_) | copy-start | bytes 1572868
  71.1 7.9 %copy-start.4 = (bf16[256,1024]{1,0:T(8,128)(2,1)}, bf16[256,1024]{1,0:T(8,128)(2,1)S(1)}, u32[]{:S(2)}) copy-start(bf16[256,1024]{1,0:T(8,128)(2,1)S(1)} %collective-permute-done.2.rest_1_) | copy-start | bytes 1572868
  71.1 44.6 %all-to-all-start.2 = ((bf16[16,400,128]{2,1,0:T(8,128)(2,1)}), bf16[16,400,128]{2,1,0:T(8,128)(2,1)S(1)}, u32[]{:S(2)}, u32[]{:S(2)}) async-start(bf16[16,400,128]{2,1,0:T(8,128)(2,1)} %get-tuple-element.27), calls=%async_computation.2 | async-start | bytes 3276800 | tf_op jit(solution)/shard_map/all_to_all | solution.py:339
  78.1 24.3 %collective-permute-start.4 = (bf16[256,1024]{1,0:T(8,128)(2,1)S(1)}, bf16[256,1024]{1,0:T(8,128)(2,1)S(1)}, u32[]{:S(2)}, u32[]{:S(2)}) collective-permute-start(bf16[256,1024]{1,0:T(8,128)(2,1)S(1)} %collective-permute-done.2.rest_1_), channel_id=1, source_target_pairs={{0,2},{1,3},{2,0},{3,1},{4,6},{5,7},{6,4},{7,5},{8,10},{9,11},{10,... | collective-permute-start | bytes 1572872 | tf_op jit(solution)/shard_map/ppermute | solution.py:249
  78.3 26.1 %collective-permute-start.5 = (bf16[256,1024]{1,0:T(8,128)(2,1)S(1)}, bf16[256,1024]{1,0:T(8,128)(2,1)S(1)}, u32[]{:S(2)}, u32[]{:S(2)}) collective-permute-start(bf16[256,1024]{1,0:T(8,128)(2,1)S(1)} %copy-done.2), channel_id=1, source_target_pairs={{0,1},{1,0},{2,3},{3,2},{4,5},{5,4},{6,7},{7,6},{8,9},{9,8},{10,11... | collective-permute-start | bytes 1572872 | tf_op jit(solution)/shard_map/ppermute | solution.py:249
  79.0 25.5 %collective-permute-start.6 = (bf16[256,1024]{1,0:T(8,128)(2,1)S(1)}, bf16[256,1024]{1,0:T(8,128)(2,1)S(1)}, u32[]{:S(2)}, u32[]{:S(2)}) collective-permute-start(bf16[256,1024]{1,0:T(8,128)(2,1)S(1)} %collective-permute-done.2.rest_1_), channel_id=1, source_target_pairs={{0,1},{1,0},{2,3},{3,2},{4,5},{5,4},{6,7},{7,6},{8,9},{9,8},{10,11... | collective-permute-start | bytes 1572872 | tf_op jit(solution)/shard_map/ppermute | solution.py:249
  79.0 25.4 %collective-permute-start.7 = (bf16[256,1024]{1,0:T(8,128)(2,1)S(1)}, bf16[256,1024]{1,0:T(8,128)(2,1)S(1)}, u32[]{:S(2)}, u32[]{:S(2)}) collective-permute-start(bf16[256,1024]{1,0:T(8,128)(2,1)S(1)} %collective-permute-done.3.rest_2_), channel_id=1, source_target_pairs={{0,1},{1,0},{2,3},{3,2},{4,5},{5,4},{6,7},{7,6},{8,9},{9,8},{10,11... | collective-permute-start | bytes 1572872 | tf_op jit(solution)/shard_map/ppermute | solution.py:249
  102.3 2.1 %copy-start.5 = (bf16[256,1024]{1,0:T(8,128)(2,1)}, bf16[256,1024]{1,0:T(8,128)(2,1)S(1)}, u32[]{:S(2)}) copy-start(bf16[256,1024]{1,0:T(8,128)(2,1)S(1)} %collective-permute-done.4.rest_3_) | copy-start | bytes 1572868
  102.3 3.9 %collective-permute-start.8 = (bf16[256,1024]{1,0:T(8,128)(2,1)S(1)}, bf16[256,1024]{1,0:T(8,128)(2,1)}, u32[]{:S(2)}, u32[]{:S(2)}) collective-permute-start(bf16[256,1024]{1,0:T(8,128)(2,1)S(1)} %collective-permute-done.4.rest_3_), channel_id=1, source_target_pairs={{0,1},{1,0},{2,3},{3,2},{4,5},{5,4},{6,7},{7,6},{8,9},{9,8},{10,11... | collective-permute-start | bytes 1572872 | tf_op jit(solution)/shard_map/ppermute | solution.py:249
  104.4 0.8 copy-start.6
  104.4 1.0 copy-start.8
  105.4 0.8 copy-start.7
  115.7 1.2 copy-start

commit v4 on v3

--- a/solution.py
+++ b/solution.py
@@ -51,9 +51,7 @@
     return jnp.transpose(wide)[:1, :].astype(jnp.int32)
 
 
-def pack_kernel(n_dev, slots, per_peer, place_ref, table_ref, note_ref, own_ref, mirror_ref, cot_ref, other_ref, msg_ref, one_ref, sorted_ref, held_ref):
-    held_ref[pl.ds(0, cot_ref.shape[0]), :] = cot_ref[...]
-    held_ref[pl.ds(cot_ref.shape[0], cot_ref.shape[0]), :] = other_ref[...]
+def pack_kernel(n_dev, slots, per_peer, place_ref, table_ref, note_ref, own_ref, mirror_ref, msg_ref, one_ref, sorted_ref):
     rows, width = own_ref.shape
     half = n_dev // 2
     upper, seat = place_ref[0], place_ref[1]
@@ -90,25 +88,42 @@
         lax.fori_loop(0, half, place, 0, unroll=2)
 
 
-def main_kernel(
-    fits, count_ref, arrived_ref, perm_ref, gain_ref, cot_ref, wqkv_ref, wout_ref,
-    layer_ref, ret_ref, *rest
+def ready_kernel(
+    cot_ref, other_ref, perm_ref, wout_ref, held_ref, cots_ref, do_ref, order_ref
 ):
-    if fits:
-        x_ref, inv_ref, nrm_ref, q_ref, kv_ref, do_ref, attt_ref, cots_ref, dq_ref, dkv_ref = rest
-    else:
-        gain_out_ref, att_out_ref, x_ref, inv_ref, nrm_ref, q_ref, kv_ref, do_ref, attt_ref, cots_ref, dq_ref, dkv_ref = rest
-    n_rows, width = x_ref.shape
-    slots = n_rows // BLOCK
-    head_dim = width // HEADS
-    gain = gain_ref[...]
+    rows = cot_ref.shape[0]
+    held_ref[pl.ds(0, rows), :] = cot_ref[...]
+    held_ref[pl.ds(rows, rows), :] = other_ref[...]
     key_row = perm_ref[...]
     key_col = column_of(key_row)
     slot_row = ranks(key_col, key_row, 0)
     slot_col = ranks(key_col, key_row, 1)
     to_arrival = (slot_row == iota((BLOCK, BLOCK), 0)).astype(BF16)
-    to_order = (slot_col == iota((BLOCK, BLOCK), 1)).astype(BF16)
+    order_ref[...] = (slot_col == iota((BLOCK, BLOCK), 1)).astype(BF16)
     cots_ref[...] = nn(to_arrival, cot_ref[...]).astype(BF16)
+    do_ref[...] = nt(cots_ref[...], wout_ref[...]).astype(BF16)
+
+
+def main_kernel(
+    fits, count_ref, arrived_ref, order_ref, gain_ref, cots_ref, do_ref, wqkv_hbm, wout_hbm,
+    layer_ref, ret_ref, *rest
+):
+    if fits:
+        x_ref, inv_ref, nrm_ref, q_ref, kv_ref, attt_ref, dq_ref, dkv_ref, dn_ref, wqkv_ref, wout_ref, sems = rest
+    else:
+        gain_out_ref, att_out_ref, x_ref, inv_ref, nrm_ref, q_ref, kv_ref, attt_ref, dq_ref, dkv_ref, dn_ref, wqkv_ref, wout_ref, sems = rest
+    n_rows, width = x_ref.shape
+    slots = n_rows // BLOCK
+    head_dim = width // HEADS
+    gain = gain_ref[...]
+    to_order = order_ref[...]
+    loads = []
+    for at, (start, size) in enumerate(((width, width), (2 * width, width), (0, width))):
+        part = pl.ds(start, size)
+        loads.append(pltpu.make_async_copy(wqkv_hbm.at[:, part], wqkv_ref.at[:, part], sems.at[at]))
+    loads.append(pltpu.make_async_copy(wout_hbm, wout_ref, sems.at[3]))
+    for load in loads:
+        load.start()
     for j in range(slots):
         if fits:
             part_rows = BLOCK // 2
@@ -122,9 +137,13 @@
         inv_ref[pl.ds(j * BLOCK, BLOCK), :] = jnp.broadcast_to(inv, (BLOCK, LANES))
         nrm_ref[pl.ds(j * BLOCK, BLOCK), :] = (x * inv * gain).astype(BF16)
     scale = head_dim ** (-0.5)
+    for at in range(2):
+        loads[at].wait()
+        weight = wqkv_ref[:, (at + 1) * width:(at + 2) * width]
+        kv_ref[:, pl.ds(at * width, width)] = nn(nrm_ref[...], weight).astype(BF16)
+    loads[2].wait()
     q_ref[...] = nn(nrm_ref[pl.ds(0, BLOCK), :], wqkv_ref[:, :width]).astype(BF16)
-    kv_ref[...] = nn(nrm_ref[...], wqkv_ref[:, width:]).astype(BF16)
-    do_ref[...] = nt(cots_ref[...], wout_ref[...]).astype(BF16)
+    loads[-1].wait()
     count = count_ref[0]
     first = iota((BLOCK, LANES), 1) < head_dim
 
@@ -159,15 +178,16 @@
         dkv_ref[:, vcols] = nn(pb, dom).astype(BF16)
         return carry
 
-    lax.fori_loop(0, width // LANES, pair_step, 0)
+    lax.fori_loop(0, width // LANES, pair_step, 0, unroll=2)
     layer = (x_ref[pl.ds(0, BLOCK), :] + tn(attt_ref[...], wout_ref[...])).astype(BF16)
     layer_ref[...] = nn(to_order, layer).astype(BF16)
     att = nt(attt_ref[...], to_order).astype(BF16)
     lane_blocks = width // LANES
     gains = jnp.zeros((1, width), F32)
+    dn_ref[...] = nt(dkv_ref[...], wqkv_ref[:, width:])
     for j in range(slots):
         rows = pl.ds(j * BLOCK, BLOCK)
-        dn = nt(dkv_ref[rows, :], wqkv_ref[:, width:])
+        dn = dn_ref[rows, :]
         if j == 0:
             dn = dn + nt(dq_ref[...], wqkv_ref[:, :width])
         x = x_ref[rows, :]
@@ -205,8 +225,15 @@
 def finish_kernel(
     n_dev, slots, masks, norm_scale, place_ref, table_ref, back_ref, one_ref, *rest
 ):
-    cots = rest[:len(masks)]
-    out_ref, gw_ref, gain_ref, acc_ref = rest[len(masks):]
+    sources = rest[:len(masks)]
+    out_ref, gw_ref, gain_ref, acc_ref, sems = rest[len(masks):len(masks) + 5]
+    cots = rest[len(masks) + 5:]
+    loads = [
+        pltpu.make_async_copy(source, target, sems.at[at])
+        for at, (source, target) in enumerate(zip(sources, cots))
+    ]
+    for load in loads:
+        load.start()
     rows, width = out_ref.shape
     lane_blocks = width // LANES
     size = lane_blocks * 8
@@ -228,7 +255,8 @@
     base = slots * size
     feats = width // n_dev
     acc = jnp.zeros((feats, width), F32)
-    for group, ref in zip(masks, cots):
+    for group, ref, load in zip(masks, cots, loads):
+        load.wait()
         for at, mask in enumerate(group):
             att = back_ref[me ^ mask, pl.ds(base, feats), :]
             acc = acc + nn(att, ref[pl.ds(at * rows, rows), :])
@@ -242,6 +270,11 @@
 
 VM = pl.BlockSpec(memory_space=pltpu.VMEM)
 SM = pl.BlockSpec(memory_space=pltpu.SMEM)
+HB = pl.BlockSpec(memory_space=pltpu.HBM)
+
+
+def near_core(x):
+    return pltpu.with_memory_space_constraint(x, pltpu.VMEM)
 
 
 def swap(block, mask):
@@ -269,27 +302,35 @@
     mirror = swap(raster_tokens, half)
     other = swap(cotangent, half // 2)
     note = lax.all_to_all(note, "ctx", 0, 0, tiled=True)
-    note, other = lax.optimization_barrier((note, other))
-
     msg_shape = (half, 2, slots, per_peer, width) if fits else (8, LANES)
     sort_shape = (2, n_dev, per_peer, width) if fits else (2, rows, width)
-    msg, one, in_order, held = pl.pallas_call(
+    msg, one, in_order = pl.pallas_call(
         functools.partial(pack_kernel, n_dev, slots, per_peer),
         out_shape=(
             jax.ShapeDtypeStruct(msg_shape, BF16),
             jax.ShapeDtypeStruct((2, rows, rows), BF16),
             jax.ShapeDtypeStruct(sort_shape, BF16),
-            jax.ShapeDtypeStruct((2 * rows, width), BF16),
         ),
-        in_specs=[SM, SM] + [VM] * 5,
-        out_specs=(VM,) * 4,
-    )(place, note, note, raster_tokens, mirror, cotangent, other)
+        in_specs=[SM, SM] + [VM] * 3,
+        out_specs=(VM,) * 3,
+    )(place, note, near_core(note), raster_tokens, near_core(mirror))
     table = note[:, 0, rows:rows + slots]
     if not fits:
         mine = lax.dynamic_slice_in_dim(table, place[0] * half, half, 0)
         msg = in_order.reshape(2, n_dev, per_peer, width)[:, mine].transpose(1, 0, 2, 3, 4)
     halves = [list(range(half)), list(range(half, n_dev))]
     arrived = lax.all_to_all(msg, "ctx", 0, 0, tiled=True, axis_index_groups=halves)
+    held, cots, d_att, order = pl.pallas_call(
+        ready_kernel,
+        out_shape=(
+            jax.ShapeDtypeStruct((2 * rows, width), BF16),
+            jax.ShapeDtypeStruct((rows, width), BF16),
+            jax.ShapeDtypeStruct((rows, width), BF16),
+            jax.ShapeDtypeStruct((rows, rows), BF16),
+        ),
+        in_specs=[VM] * 4,
+        out_specs=(VM,) * 4,
+    )(cotangent, near_core(other), hilbert_perm[None], w_out)
     arrived, held = lax.optimization_barrier((arrived, held))
     names = [0, half // 2]
     bits = [1 << b for b in range(n_dev.bit_length() - 1)]
@@ -315,7 +356,7 @@
             jax.ShapeDtypeStruct((rows, width), BF16),
             jax.ShapeDtypeStruct(ret_shape, BF16),
         ) + extra_shapes,
-        in_specs=[SM] + [VM] * 6,
+        in_specs=[SM] + [VM] * 5 + [HB] * 2,
         out_specs=(VM,) * (2 + len(extra_shapes)),
         scratch_shapes=[
             pltpu.VMEM((n_rows, width), F32),
@@ -323,19 +364,22 @@
             pltpu.VMEM((n_rows, width), BF16),
             pltpu.VMEM((rows, width), BF16),
             pltpu.VMEM((n_rows, 2 * width), BF16),
-            pltpu.VMEM((rows, width), BF16),
             pltpu.VMEM((width, rows), BF16),
             pltpu.VMEM((rows, width), BF16),
-            pltpu.VMEM((rows, width), BF16),
             pltpu.VMEM((n_rows, 2 * width), BF16),
+            pltpu.VMEM((n_rows, width), F32),
+            pltpu.VMEM(w_qkv.shape, BF16),
+            pltpu.VMEM(w_out.shape, BF16),
+            pltpu.SemaphoreType.DMA((4,)),
         ],
         cost_estimate=pl.CostEstimate(
             flops=14 * n_rows * width * width, bytes_accessed=16 * width * width, transcendentals=0
         ),
-    )(neighbor_counts, arrived, hilbert_perm[None], norm_gain[None], cotangent, w_qkv, w_out)
+    )(
+        neighbor_counts, near_core(arrived), order, norm_gain[None], cots, d_att, w_qkv, w_out,
+    )
 
     if fits:
-        ret, across, beside = lax.optimization_barrier((ret, across, beside))
         back = lax.all_to_all(ret, "ctx", 0, 0, tiled=True)
     corner = swap(across, 2)
     pieces = [
@@ -355,10 +399,13 @@
                 jax.ShapeDtypeStruct((feats, width), F32),
                 jax.ShapeDtypeStruct((lane_blocks, LANES), F32),
             ),
-            in_specs=[SM, SM, VM, VM] + [VM] * len(pieces),
+            in_specs=[SM, SM, VM, VM] + [HB] * len(pieces),
             out_specs=(VM, VM, VM),
-            scratch_shapes=[pltpu.VMEM((n_dev, lane_blocks * 8, LANES), F32)],
-        )(place, note, back, one, *[piece for group, piece in pieces])
+            scratch_shapes=[
+                pltpu.VMEM((n_dev, lane_blocks * 8, LANES), F32),
+                pltpu.SemaphoreType.DMA((len(pieces),)),
+            ] + [pltpu.VMEM(piece.shape, BF16) for group, piece in pieces],
+        )(place, note, near_core(back), one, *[piece for group, piece in pieces])
         return (layer_out, grad_tokens, grad_w_out, grad_gain.reshape(width))
     gains, att = extra
     high = gains.astype(BF16)

time: 122 us -> 158 us (1.30)
  the two profiles are of different devices: /device:TPU:15 before, /device:TPU:0 now
where the time goes in v4:
time: 158 us
  waiting for transfers between devices  96.3 us (61%)
  Pallas kernels  30.8 us (19%)
  starting transfers between devices  25.2 us (16%)
  local copies, waits for them, and re-layouts  2.52 us (2%)
    ppermute x9, waiting for transfers between devices, swap(): return lax.ppermute(block, 'ctx', [(i, i ^ mask) for i in range(n_dev)])  88.8 us
    pallas_call x1, Pallas kernels, per_device(): pl.pallas_call(functools.partial(main_kernel, fits), out_shape=(jax.Shape...  19.9 us
    ppermute x9, starting transfers between devices, swap(): return lax.ppermute(block, 'ctx', [(i, i ^ mask) for i in range(n_dev)])  12.6 us
    all_to_all x1, waiting for transfers between devices, per_device(): note = lax.all_to_all(note, 'ctx', 0, 0, tiled=True)  7.55 us
    all_to_all x1, starting transfers between devices, per_device(): back = lax.all_to_all(ret, 'ctx', 0, 0, tiled=True)  5.07 us
    pallas_call x1, Pallas kernels, per_device(): pl.pallas_call(functools.partial(finish_kernel, n_dev, slots, masks, norm...  4.08 us
    all_to_all x1, starting transfers between devices, per_device(): note = lax.all_to_all(note, 'ctx', 0, 0, tiled=True)  3.91 us
    all_to_all x1, starting transfers between devices, per_device(): lax.all_to_all(msg, 'ctx', 0, 0, tiled=True, axis_index_groups=halves)  3.57 us
  transfers between devices with their start and end apart: 12, of which 5 were waited for; matrix products, arithmetic and copies ran while one was open for 1% of the time, Pallas kernels for 2%

profile of v4, /device:TPU:0, one launch (start us, length us, event | category | flops | bytes accessed | tf_op | source)
XLA Modules:
  0.0 157.6 jit_solution(3928372046900957823)
XLA Ops:
  0.6 4.1 %collective-permute-start = (bf16[128,1024]{1,0:T(8,128)(2,1)}, bf16[128,1024]{1,0:T(8,128)(2,1)S(1)}, u32[]{:S(2)}, u32[]{:S(2)}) collective-permute-start(bf16[128,1024]{1,0:T(8,128)(2,1)} %own_ref.1), channel_id=1, source_target_pairs={{0,8},{1,9},{2,10},{3,11},{4,12},{5,13},{6,14},{7,15},{8,0},{9,1},... | collective-permute-start | bytes 786440 | tf_op jit(solution)/shard_map/ppermute | solution.py:282
  4.8 0.7 pad_add_fusion
  5.4 0.0 copy-start.8
  5.4 0.6 broadcast_in_dim.12
  6.1 3.9 %all-to-all-start = ((s32[16,1,256]{2,1,0:T(1,128)}), s32[16,1,256]{2,1,0:T(1,128)S(1)}, u32[]{:S(2)}, u32[]{:S(2)}) async-start(s32[16,1,256]{2,1,0:T(1,128)} %broadcast_in_dim.12), calls=%async_computation | async-start | bytes 32768 | tf_op jit(solution)/shard_map/all_to_all | solution.py:304
  10.0 0.7 pad_add_fusion.1.place_ref
  10.7 7.5 %all-to-all-done.table_ref.note_ref = s32[16,1,256]{2,1,0:T(1,128)S(1)} async-done(((s32[16,1,256]{2,1,0:T(1,128)}), s32[16,1,256]{2,1,0:T(1,128)S(1)}, u32[]{:S(2)}, u32[]{:S(2)}) %all-to-all-start) | async-done | bytes 16416 | tf_op jit(solution)/shard_map/all_to_all | solution.py:304
  18.2 0.0 copy-start
  18.2 0.0 collective-permute-done.mirror_ref
  18.2 3.4 %shard_map.111 = (bf16[8,2,5,8,1024]{4,3,2,1,0:T(8,128)(2,1)}, bf16[2,128,128]{2,1,0:T(8,128)(2,1)}, bf16[2,16,8,1024]{3,2,1,0:T(8,128)(2,1)}) custom-call(s32[2]{0:T(128)} %pad_add_fusion.1.place_ref, s32[16,1,256]{2,1,0:T(1,128)S(1)} %all-to-all-done.table_ref.note_ref, s32[16,1,256]{2,1,0:T(1,128)S(1)} %all-to-all-done.table_ref.note_ref, ...), custom_call_target="tpu_custom_call" | custom-call | tf_op jit(solution)/shard_map/pallas_call | solution.py:307
  21.6 3.6 %all-to-all-start.1 = ((bf16[8,2,5,8,1024]{4,3,2,1,0:T(8,128)(2,1)}), bf16[8,2,5,8,1024]{4,3,2,1,0:T(8,128)(2,1)S(1)}, u32[]{:S(2)}, u32[]{:S(2)}) async-start(bf16[8,2,5,8,1024]{4,3,2,1,0:T(8,128)(2,1)} %get-tuple-element.17), calls=%async_computation.1 | async-start | bytes 2621440 | tf_op jit(solution)/shard_map/all_to_all | solution.py:322
  25.1 0.0 copy-done.8
  25.2 1.9 %collective-permute-start.1 = (bf16[128,1024]{1,0:T(8,128)(2,1)S(1)}, bf16[128,1024]{1,0:T(8,128)(2,1)S(1)}, u32[]{:S(2)}, u32[]{:S(2)}) collective-permute-start(bf16[128,1024]{1,0:T(8,128)(2,1)S(1)} %copy-done.8), channel_id=1, source_target_pairs={{0,4},{1,5},{2,6},{3,7},{4,0},{5,1},{6,2},{7,3},{8,12},{9,13},{10,... | collective-permute-start | bytes 786440 | tf_op jit(solution)/shard_map/ppermute | solution.py:282
  27.7 20.2 %collective-permute-done.1.other_ref = bf16[128,1024]{1,0:T(8,128)(2,1)S(1)} collective-permute-done((bf16[128,1024]{1,0:T(8,128)(2,1)S(1)}, bf16[128,1024]{1,0:T(8,128)(2,1)S(1)}, u32[]{:S(2)}, u32[]{:S(2)}) %collective-permute-start.1) | collective-permute-done | bytes 262176 | tf_op jit(solution)/shard_map/ppermute | solution.py:282
  48.0 3.5 %shard_map.112 = (bf16[256,1024]{1,0:T(8,128)(2,1)}, bf16[128,1024]{1,0:T(8,128)(2,1)}, bf16[128,1024]{1,0:T(8,128)(2,1)}, bf16[128,128]{1,0:T(8,128)(2,1)}) custom-call(bf16[128,1024]{1,0:T(8,128)(2,1)} %cot_ref.1, bf16[128,1024]{1,0:T(8,128)(2,1)S(1)} %collective-permute-done.1.other_ref, s32[1,128]{1,0:T(1,128)} %bitcast.6, bf16[1024,1024]{1,0:T(8,128)(2,1)} %wout_hbm.1), custom_call_target="tpu_custom_call" | custom-call | tf_op jit(solution)/shard_map/pallas_call | solution.py:323
  51.5 0.0 copy-done
  51.5 0.0 all-to-all-done.1.arrived_ref
  51.5 19.9 %shard_map.113 = (bf16[128,1024]{1,0:T(8,128)(2,1)}, bf16[16,400,128]{2,1,0:T(8,128)(2,1)}) custom-call(s32[1]{0:T(128)S(6)} %copy.12.count_ref, bf16[8,2,5,8,1024]{4,3,2,1,0:T(8,128)(2,1)S(1)} %all-to-all-done.1.arrived_ref, bf16[128,128]{1,0:T(8,128)(2,1)} %get-tuple-element.20.order_ref, f32[1,1024]{1,0:T(1,128)} %bitcast.8, ...), custom_call_target="tpu_custom_call" | custom-call | flops 9395240960 | bytes 16777216 | tf_op jit(solution)/shard_map/pallas_call | solution.py:353
  71.4 0.0 copy-start.1
  71.4 5.1 %all-to-all-start.2 = ((bf16[16,400,128]{2,1,0:T(8,128)(2,1)}), bf16[16,400,128]{2,1,0:T(8,128)(2,1)S(1)}, u32[]{:S(2)}, u32[]{:S(2)}) async-start(bf16[16,400,128]{2,1,0:T(8,128)(2,1)} %get-tuple-element.24), calls=%async_computation.2 | async-start | bytes 3276800 | tf_op jit(solution)/shard_map/all_to_all | solution.py:383
  76.5 0.0 copy-done.1
  76.5 2.9 %collective-permute-start.2 = (bf16[256,1024]{1,0:T(8,128)(2,1)S(1)}, bf16[256,1024]{1,0:T(8,128)(2,1)S(1)}, u32[]{:S(2)}, u32[]{:S(2)}) collective-permute-start(bf16[256,1024]{1,0:T(8,128)(2,1)S(1)} %copy-done.1), channel_id=1, source_target_pairs={{0,8},{1,9},{2,10},{3,11},{4,12},{5,13},{6,14},{7,15},{8,0},{9,1},... | collective-permute-start | bytes 1572872 | tf_op jit(solution)/shard_map/ppermute | solution.py:282
  79.4 1.5 collective-permute-start.3
  80.8 57.3 %collective-permute-done.2.rest_1_ = bf16[256,1024]{1,0:T(8,128)(2,1)S(1)} collective-permute-done((bf16[256,1024]{1,0:T(8,128)(2,1)S(1)}, bf16[256,1024]{1,0:T(8,128)(2,1)S(1)}, u32[]{:S(2)}, u32[]{:S(2)}) %collective-permute-start.2) | collective-permute-done | bytes 524320 | tf_op jit(solution)/shard_map/ppermute | solution.py:282
  138.1 1.6 %collective-permute-start.4 = (bf16[256,1024]{1,0:T(8,128)(2,1)S(1)}, bf16[256,1024]{1,0:T(8,128)(2,1)S(1)}, u32[]{:S(2)}, u32[]{:S(2)}) collective-permute-start(bf16[256,1024]{1,0:T(8,128)(2,1)S(1)} %collective-permute-done.2.rest_1_), channel_id=1, source_target_pairs={{0,2},{1,3},{2,0},{3,1},{4,6},{5,7},{6,4},{7,5},{8,10},{9,11},{10,... | collective-permute-start | bytes 1572872 | tf_op jit(solution)/shard_map/ppermute | solution.py:282
  139.7 0.0 collective-permute-start.5
  139.7 0.5 collective-permute-start.6
  140.2 0.0 collective-permute-done.3.rest_2_
  140.2 0.0 copy-start.3
  140.2 0.1 collective-permute-start.7
  140.3 11.2 %collective-permute-done.4.rest_3_ = bf16[256,1024]{1,0:T(8,128)(2,1)S(1)} collective-permute-done((bf16[256,1024]{1,0:T(8,128)(2,1)S(1)}, bf16[256,1024]{1,0:T(8,128)(2,1)S(1)}, u32[]{:S(2)}, u32[]{:S(2)}) %collective-permute-start.4) | collective-permute-done | bytes 524320 | tf_op jit(solution)/shard_map/ppermute | solution.py:282
  151.5 0.0 copy-start.4
  151.5 0.0 collective-permute-start.8
  151.5 0.0 collective-permute-done.5.rest_4_
  151.5 0.0 copy-start.5
  151.5 0.0 collective-permute-done.7.rest_6_
  151.5 0.0 copy-start.7
  151.5 0.0 collective-permute-done.6.rest_5_
  151.5 0.8 copy-done.4
  152.3 0.1 copy-done.5
  152.4 0.2 copy-done.7
  152.6 0.0 copy-start.6
  152.6 0.8 copy-done.6
  153.4 0.1 collective-permute-done.8.rest_7_
  153.5 0.0 all-to-all-done.2.back_ref
  153.5 0.0 copy-done.2
  153.5 0.0 copy-done.3
  153.5 4.1 %shard_map.114 = (bf16[128,1024]{1,0:T(8,128)(2,1)}, f32[64,1024]{1,0:T(8,128)}, f32[8,128]{1,0:T(8,128)}) custom-call(s32[2]{0:T(128)} %pad_add_fusion.1.place_ref, s32[16,1,256]{2,1,0:T(1,128)} %copy-done, bf16[16,400,128]{2,1,0:T(8,128)(2,1)S(1)} %all-to-all-done.2.back_ref, bf16[2,128,128]{2,1,0:T(8,128)(2,1)} %get-tuple-element.25.one_ref, ...), custom_call_target="tpu_custom_call" | custom-call | tf_op jit(solution)/shard_map/pallas_call | solution.py:395
  (1 shorter events, 0.0 us)
Async XLA Ops:
  0.6 17.6 %collective-permute-start = (bf16[128,1024]{1,0:T(8,128)(2,1)}, bf16[128,1024]{1,0:T(8,128)(2,1)S(1)}, u32[]{:S(2)}, u32[]{:S(2)}) collective-permute-start(bf16[128,1024]{1,0:T(8,128)(2,1)} %own_ref.1), channel_id=1, source_target_pairs={{0,8},{1,9},{2,10},{3,11},{4,12},{5,13},{6,14},{7,15},{8,0},{9,1},... | collective-permute-start | bytes 786440 | tf_op jit(solution)/shard_map/ppermute | solution.py:282
  5.4 19.7 %copy-start.8 = (bf16[128,1024]{1,0:T(8,128)(2,1)S(1)}, bf16[128,1024]{1,0:T(8,128)(2,1)}, u32[]{:S(2)}) copy-start(bf16[128,1024]{1,0:T(8,128)(2,1)} %cot_ref.1) | copy-start | bytes 786436
  6.1 12.2 %all-to-all-start = ((s32[16,1,256]{2,1,0:T(1,128)}), s32[16,1,256]{2,1,0:T(1,128)S(1)}, u32[]{:S(2)}, u32[]{:S(2)}) async-start(s32[16,1,256]{2,1,0:T(1,128)} %broadcast_in_dim.12), calls=%async_computation | async-start | bytes 32768 | tf_op jit(solution)/shard_map/all_to_all | solution.py:304
  18.2 33.3 %copy-start = (s32[16,1,256]{2,1,0:T(1,128)}, s32[16,1,256]{2,1,0:T(1,128)S(1)}, u32[]{:S(2)}) copy-start(s32[16,1,256]{2,1,0:T(1,128)S(1)} %all-to-all-done.table_ref.note_ref) | copy-start | bytes 49156
  21.6 29.9 %all-to-all-start.1 = ((bf16[8,2,5,8,1024]{4,3,2,1,0:T(8,128)(2,1)}), bf16[8,2,5,8,1024]{4,3,2,1,0:T(8,128)(2,1)S(1)}, u32[]{:S(2)}, u32[]{:S(2)}) async-start(bf16[8,2,5,8,1024]{4,3,2,1,0:T(8,128)(2,1)} %get-tuple-element.17), calls=%async_computation.1 | async-start | bytes 2621440 | tf_op jit(solution)/shard_map/all_to_all | solution.py:322
  25.2 22.8 %collective-permute-start.1 = (bf16[128,1024]{1,0:T(8,128)(2,1)S(1)}, bf16[128,1024]{1,0:T(8,128)(2,1)S(1)}, u32[]{:S(2)}, u32[]{:S(2)}) collective-permute-start(bf16[128,1024]{1,0:T(8,128)(2,1)S(1)} %copy-done.8), channel_id=1, source_target_pairs={{0,4},{1,5},{2,6},{3,7},{4,0},{5,1},{6,2},{7,3},{8,12},{9,13},{10,... | collective-permute-start | bytes 786440 | tf_op jit(solution)/shard_map/ppermute | solution.py:282
  71.4 5.1 %copy-start.1 = (bf16[256,1024]{1,0:T(8,128)(2,1)S(1)}, bf16[256,1024]{1,0:T(8,128)(2,1)}, u32[]{:S(2)}) copy-start(bf16[256,1024]{1,0:T(8,128)(2,1)} %get-tuple-element.26.rest_0_) | copy-start | bytes 1572868
  71.4 82.1 %all-to-all-start.2 = ((bf16[16,400,128]{2,1,0:T(8,128)(2,1)}), bf16[16,400,128]{2,1,0:T(8,128)(2,1)S(1)}, u32[]{:S(2)}, u32[]{:S(2)}) async-start(bf16[16,400,128]{2,1,0:T(8,128)(2,1)} %get-tuple-element.24), calls=%async_computation.2 | async-start | bytes 3276800 | tf_op jit(solution)/shard_map/all_to_all | solution.py:383
  76.5 61.6 %collective-permute-start.2 = (bf16[256,1024]{1,0:T(8,128)(2,1)S(1)}, bf16[256,1024]{1,0:T(8,128)(2,1)S(1)}, u32[]{:S(2)}, u32[]{:S(2)}) collective-permute-start(bf16[256,1024]{1,0:T(8,128)(2,1)S(1)} %copy-done.1), channel_id=1, source_target_pairs={{0,8},{1,9},{2,10},{3,11},{4,12},{5,13},{6,14},{7,15},{8,0},{9,1},... | collective-permute-start | bytes 1572872 | tf_op jit(solution)/shard_map/ppermute | solution.py:282
  79.4 60.8 %collective-permute-start.3 = (bf16[256,1024]{1,0:T(8,128)(2,1)S(1)}, bf16[256,1024]{1,0:T(8,128)(2,1)S(1)}, u32[]{:S(2)}, u32[]{:S(2)}) collective-permute-start(bf16[256,1024]{1,0:T(8,128)(2,1)S(1)} %copy-done.1), channel_id=1, source_target_pairs={{0,2},{1,3},{2,0},{3,1},{4,6},{5,7},{6,4},{7,5},{8,10},{9,11},{10,... | collective-permute-start | bytes 1572872 | tf_op jit(solution)/shard_map/ppermute | solution.py:282
  138.1 15.4 %copy-start.2 = (bf16[256,1024]{1,0:T(8,128)(2,1)}, bf16[256,1024]{1,0:T(8,128)(2,1)S(1)}, u32[]{:S(2)}) copy-start(bf16[256,1024]{1,0:T(8,128)(2,1)S(1)} %collective-permute-done.2.rest_1_) | copy-start | bytes 1572868
  138.1 13.4 %collective-permute-start.4 = (bf16[256,1024]{1,0:T(8,128)(2,1)S(1)}, bf16[256,1024]{1,0:T(8,128)(2,1)S(1)}, u32[]{:S(2)}, u32[]{:S(2)}) collective-permute-start(bf16[256,1024]{1,0:T(8,128)(2,1)S(1)} %collective-permute-done.2.rest_1_), channel_id=1, source_target_pairs={{0,2},{1,3},{2,0},{3,1},{4,6},{5,7},{6,4},{7,5},{8,10},{9,11},{10,... | collective-permute-start | bytes 1572872 | tf_op jit(solution)/shard_map/ppermute | solution.py:282
  139.7 11.8 %collective-permute-start.5 = (bf16[256,1024]{1,0:T(8,128)(2,1)S(1)}, bf16[256,1024]{1,0:T(8,128)(2,1)S(1)}, u32[]{:S(2)}, u32[]{:S(2)}) collective-permute-start(bf16[256,1024]{1,0:T(8,128)(2,1)S(1)} %copy-done.1), channel_id=1, source_target_pairs={{0,1},{1,0},{2,3},{3,2},{4,5},{5,4},{6,7},{7,6},{8,9},{9,8},{10,11... | collective-permute-start | bytes 1572872 | tf_op jit(solution)/shard_map/ppermute | solution.py:282
  139.7 11.8 %collective-permute-start.6 = (bf16[256,1024]{1,0:T(8,128)(2,1)S(1)}, bf16[256,1024]{1,0:T(8,128)(2,1)S(1)}, u32[]{:S(2)}, u32[]{:S(2)}) collective-permute-start(bf16[256,1024]{1,0:T(8,128)(2,1)S(1)} %collective-permute-done.2.rest_1_), channel_id=1, source_target_pairs={{0,1},{1,0},{2,3},{3,2},{4,5},{5,4},{6,7},{7,6},{8,9},{9,8},{10,11... | collective-permute-start | bytes 1572872 | tf_op jit(solution)/shard_map/ppermute | solution.py:282
  140.2 13.3 %copy-start.3 = (bf16[256,1024]{1,0:T(8,128)(2,1)}, bf16[256,1024]{1,0:T(8,128)(2,1)S(1)}, u32[]{:S(2)}) copy-start(bf16[256,1024]{1,0:T(8,128)(2,1)S(1)} %collective-permute-done.3.rest_2_) | copy-start | bytes 1572868
  140.2 11.3 %collective-permute-start.7 = (bf16[256,1024]{1,0:T(8,128)(2,1)S(1)}, bf16[256,1024]{1,0:T(8,128)(2,1)S(1)}, u32[]{:S(2)}, u32[]{:S(2)}) collective-permute-start(bf16[256,1024]{1,0:T(8,128)(2,1)S(1)} %collective-permute-done.3.rest_2_), channel_id=1, source_target_pairs={{0,1},{1,0},{2,3},{3,2},{4,5},{5,4},{6,7},{7,6},{8,9},{9,8},{10,11... | collective-permute-start | bytes 1572872 | tf_op jit(solution)/shard_map/ppermute | solution.py:282
  151.5 0.8 copy-start.4
  151.5 2.0 %collective-permute-start.8 = (bf16[256,1024]{1,0:T(8,128)(2,1)S(1)}, bf16[256,1024]{1,0:T(8,128)(2,1)}, u32[]{:S(2)}, u32[]{:S(2)}) collective-permute-start(bf16[256,1024]{1,0:T(8,128)(2,1)S(1)} %collective-permute-done.4.rest_3_), channel_id=1, source_target_pairs={{0,1},{1,0},{2,3},{3,2},{4,5},{5,4},{6,7},{7,6},{8,9},{9,8},{10,11... | collective-permute-start | bytes 1572872 | tf_op jit(solution)/shard_map/ppermute | solution.py:282
  151.5 0.9 copy-start.5
  151.5 1.1 copy-start.7
  152.6 0.8 copy-start.6

commit v5 on v4

--- a/solution.py
+++ b/solution.py
@@ -1,4 +1,5 @@
 import functools
+import math
 
 import jax
 import jax.numpy as jnp
@@ -109,9 +110,9 @@
     layer_ref, ret_ref, *rest
 ):
     if fits:
-        x_ref, inv_ref, nrm_ref, q_ref, kv_ref, attt_ref, dq_ref, dkv_ref, dn_ref, wqkv_ref, wout_ref, sems = rest
+        x_ref, inv_ref, nrm_ref, q_ref, kv_ref, attt_ref, dq_ref, dkv_ref, dn_ref, wqkv_ref, wout_ref, sems, ret_v = rest
     else:
-        gain_out_ref, att_out_ref, x_ref, inv_ref, nrm_ref, q_ref, kv_ref, attt_ref, dq_ref, dkv_ref, dn_ref, wqkv_ref, wout_ref, sems = rest
+        gain_out_ref, att_out_ref, x_ref, inv_ref, nrm_ref, q_ref, kv_ref, attt_ref, dq_ref, dkv_ref, dn_ref, wqkv_ref, wout_ref, sems, ret_v = rest
     n_rows, width = x_ref.shape
     slots = n_rows // BLOCK
     head_dim = width // HEADS
@@ -137,13 +138,13 @@
         inv_ref[pl.ds(j * BLOCK, BLOCK), :] = jnp.broadcast_to(inv, (BLOCK, LANES))
         nrm_ref[pl.ds(j * BLOCK, BLOCK), :] = (x * inv * gain).astype(BF16)
     scale = head_dim ** (-0.5)
+    assert math.frexp(scale)[0] == 0.5
     for at in range(2):
         loads[at].wait()
         weight = wqkv_ref[:, (at + 1) * width:(at + 2) * width]
         kv_ref[:, pl.ds(at * width, width)] = nn(nrm_ref[...], weight).astype(BF16)
     loads[2].wait()
     q_ref[...] = nn(nrm_ref[pl.ds(0, BLOCK), :], wqkv_ref[:, :width]).astype(BF16)
-    loads[-1].wait()
     count = count_ref[0]
     first = iota((BLOCK, LANES), 1) < head_dim
 
@@ -162,28 +163,31 @@
         dom = both(do_ref[:, cols])
         k = kv_ref[:, cols]
         v = kv_ref[:, vcols]
-        s = nt(k, qm) * scale
+        qs = qm * jnp.asarray(scale, BF16)
+        s = nt(k, qs)
         s = jnp.concatenate(
             [jnp.where(j < count, s[j * BLOCK:(j + 1) * BLOCK], FAR) for j in range(slots)], axis=0
         )
         e = jnp.exp(s - jnp.max(s, axis=0, keepdims=True))
-        p = e / jnp.sum(e, axis=0, keepdims=True)
+        p = e * (1.0 / jnp.sum(e, axis=0, keepdims=True))
         pb = p.astype(BF16)
         dp = nt(v, dom)
         dots = jnp.sum(dp * p, axis=0, keepdims=True)
-        ds = (p * (dp - dots) * scale).astype(BF16)
+        ds = (p * (dp - dots)).astype(BF16)
         attt_ref[cols, :] = own(tn(v, pb)).astype(BF16)
-        dq_ref[:, cols] = jnp.transpose(own(tn(k, ds))).astype(BF16)
-        dkv_ref[:, cols] = nn(ds, qm).astype(BF16)
+        dq_ref[:, cols] = jnp.transpose(own(tn(k, ds)) * scale).astype(BF16)
+        dkv_ref[:, cols] = nn(ds, qs).astype(BF16)
         dkv_ref[:, vcols] = nn(pb, dom).astype(BF16)
         return carry
 
-    lax.fori_loop(0, width // LANES, pair_step, 0, unroll=2)
+    lax.fori_loop(0, width // LANES, pair_step, 0, unroll=8)
+    loads[3].wait()
     layer = (x_ref[pl.ds(0, BLOCK), :] + tn(attt_ref[...], wout_ref[...])).astype(BF16)
     layer_ref[...] = nn(to_order, layer).astype(BF16)
     att = nt(attt_ref[...], to_order).astype(BF16)
     lane_blocks = width // LANES
     gains = jnp.zeros((1, width), F32)
+    stores = []
     dn_ref[...] = nt(dkv_ref[...], wqkv_ref[:, width:])
     for j in range(slots):
         rows = pl.ds(j * BLOCK, BLOCK)
@@ -201,7 +205,10 @@
             n_dev = ret_ref.shape[0]
             for lb in range(lane_blocks):
                 piece = out[:, lb * LANES:(lb + 1) * LANES].reshape(n_dev, 8, LANES)
-                ret_ref[:, pl.ds((j * lane_blocks + lb) * 8, 8), :] = piece.astype(BF16)
+                ret_v[:, pl.ds((j * lane_blocks + lb) * 8, 8), :] = piece.astype(BF16)
+            region = pl.ds(j * lane_blocks * 8, lane_blocks * 8)
+            stores.append(pltpu.make_async_copy(ret_v.at[:, region], ret_ref.at[:, region], sems.at[4 + j]))
+            stores[-1].start()
         else:
             ret_ref[j] = out.astype(BF16)
     if not fits:
@@ -210,7 +217,7 @@
         return
     base = slots * lane_blocks * 8
     feats = width // n_dev
-    ret_ref[:, pl.ds(base, feats), :] = att.reshape(n_dev, feats, LANES)
+    ret_v[:, pl.ds(base, feats), :] = att.reshape(n_dev, feats, LANES)
     high = gains.astype(BF16).astype(F32)
     low = gains - high
     row = iota((8, LANES), 0)
@@ -219,7 +226,12 @@
         for lb in range(lane_blocks):
             tile = jnp.where(row == lb, value[:, lb * LANES:(lb + 1) * LANES], tile)
         tile = jnp.broadcast_to(tile.astype(BF16)[None], (n_dev, 8, LANES))
-        ret_ref[:, pl.ds(base + feats + part * 8, 8), :] = tile
+        ret_v[:, pl.ds(base + feats + part * 8, 8), :] = tile
+    region = pl.ds(base, feats + 16)
+    stores.append(pltpu.make_async_copy(ret_v.at[:, region], ret_ref.at[:, region], sems.at[4 + slots]))
+    stores[-1].start()
+    for store in stores:
+        store.wait()
 
 
 def finish_kernel(
@@ -257,9 +269,8 @@
     acc = jnp.zeros((feats, width), F32)
     for group, ref, load in zip(masks, cots, loads):
         load.wait()
-        for at, mask in enumerate(group):
-            att = back_ref[me ^ mask, pl.ds(base, feats), :]
-            acc = acc + nn(att, ref[pl.ds(at * rows, rows), :])
+        att = jnp.concatenate([back_ref[me ^ mask, pl.ds(base, feats), :] for mask in group], axis=1)
+        acc = acc + nn(att, ref[...])
     gw_ref[...] = acc * norm_scale
     tile = jnp.zeros((8, LANES), F32)
     for dest in range(n_dev):
@@ -304,20 +315,20 @@
     note = lax.all_to_all(note, "ctx", 0, 0, tiled=True)
     msg_shape = (half, 2, slots, per_peer, width) if fits else (8, LANES)
     sort_shape = (2, n_dev, per_peer, width) if fits else (2, rows, width)
-    msg, one, in_order = pl.pallas_call(
+    msg, one, *in_order = pl.pallas_call(
         functools.partial(pack_kernel, n_dev, slots, per_peer),
         out_shape=(
             jax.ShapeDtypeStruct(msg_shape, BF16),
             jax.ShapeDtypeStruct((2, rows, rows), BF16),
-            jax.ShapeDtypeStruct(sort_shape, BF16),
-        ),
+        ) + (() if fits else (jax.ShapeDtypeStruct(sort_shape, BF16),)),
         in_specs=[SM, SM] + [VM] * 3,
-        out_specs=(VM,) * 3,
+        out_specs=(VM,) * (2 if fits else 3),
+        scratch_shapes=[pltpu.VMEM(sort_shape, BF16)] if fits else [],
     )(place, note, near_core(note), raster_tokens, near_core(mirror))
     table = note[:, 0, rows:rows + slots]
     if not fits:
         mine = lax.dynamic_slice_in_dim(table, place[0] * half, half, 0)
-        msg = in_order.reshape(2, n_dev, per_peer, width)[:, mine].transpose(1, 0, 2, 3, 4)
+        msg = in_order[0].reshape(2, n_dev, per_peer, width)[:, mine].transpose(1, 0, 2, 3, 4)
     halves = [list(range(half)), list(range(half, n_dev))]
     arrived = lax.all_to_all(msg, "ctx", 0, 0, tiled=True, axis_index_groups=halves)
     held, cots, d_att, order = pl.pallas_call(
@@ -357,7 +368,7 @@
             jax.ShapeDtypeStruct(ret_shape, BF16),
         ) + extra_shapes,
         in_specs=[SM] + [VM] * 5 + [HB] * 2,
-        out_specs=(VM,) * (2 + len(extra_shapes)),
+        out_specs=(VM, HB if fits else VM) + (VM,) * len(extra_shapes),
         scratch_shapes=[
             pltpu.VMEM((n_rows, width), F32),
             pltpu.VMEM((n_rows, LANES), F32),
@@ -370,7 +381,8 @@
             pltpu.VMEM((n_rows, width), F32),
             pltpu.VMEM(w_qkv.shape, BF16),
             pltpu.VMEM(w_out.shape, BF16),
-            pltpu.SemaphoreType.DMA((4,)),
+            pltpu.SemaphoreType.DMA((5 + slots,)),
+            pltpu.VMEM(ret_shape if fits else (8, LANES), BF16),
         ],
         cost_estimate=pl.CostEstimate(
             flops=14 * n_rows * width * width, bytes_accessed=16 * width * width, transcendentals=0

time: 158 us -> 158 us (level)
  no operation moved by 1% of the time
where the time goes in v5:
time: 158 us
  waiting for transfers between devices  96.3 us (61%)
  Pallas kernels  30.6 us (19%)
  starting transfers between devices  25.2 us (16%)
  local copies, waits for them, and re-layouts  2.52 us (2%)
  between operations  1.58 us (1%)
    ppermute x9, waiting for transfers between devices, swap(): return lax.ppermute(block, 'ctx', [(i, i ^ mask) for i in range(n_dev)])  88.8 us
    pallas_call x1, Pallas kernels, per_device(): pl.pallas_call(functools.partial(main_kernel, fits), out_shape=(jax.Shape...  19.8 us
    ppermute x9, starting transfers between devices, swap(): return lax.ppermute(block, 'ctx', [(i, i ^ mask) for i in range(n_dev)])  12.6 us
    all_to_all x1, waiting for transfers between devices, per_device(): note = lax.all_to_all(note, 'ctx', 0, 0, tiled=True)  7.55 us
    all_to_all x1, starting transfers between devices, per_device(): back = lax.all_to_all(ret, 'ctx', 0, 0, tiled=True)  5.07 us
    pallas_call x1, Pallas kernels, per_device(): pl.pallas_call(functools.partial(finish_kernel, n_dev, slots, masks, norm...  4.07 us
    all_to_all x1, starting transfers between devices, per_device(): note = lax.all_to_all(note, 'ctx', 0, 0, tiled=True)  3.91 us
    all_to_all x1, starting transfers between devices, per_device(): lax.all_to_all(msg, 'ctx', 0, 0, tiled=True, axis_index_groups=halves)  3.57 us
  transfers between devices with their start and end apart: 12, of which 5 were waited for; matrix products, arithmetic and copies ran while one was open for 1% of the time, Pallas kernels for 2%

profile of v5, /device:TPU:0, one launch (start us, length us, event | category | flops | bytes accessed | tf_op | source)
XLA Modules:
  0.0 157.5 jit_solution(758287970692376960)
XLA Ops:
  0.6 4.1 %collective-permute-start = (bf16[128,1024]{1,0:T(8,128)(2,1)}, bf16[128,1024]{1,0:T(8,128)(2,1)S(1)}, u32[]{:S(2)}, u32[]{:S(2)}) collective-permute-start(bf16[128,1024]{1,0:T(8,128)(2,1)} %own_ref.1), channel_id=1, source_target_pairs={{0,8},{1,9},{2,10},{3,11},{4,12},{5,13},{6,14},{7,15},{8,0},{9,1},... | collective-permute-start | bytes 786440 | tf_op jit(solution)/shard_map/ppermute | solution.py:293
  4.8 0.7 pad_add_fusion
  5.4 0.0 copy-start.8
  5.4 0.6 broadcast_in_dim.12
  6.1 3.9 %all-to-all-start = ((s32[16,1,256]{2,1,0:T(1,128)}), s32[16,1,256]{2,1,0:T(1,128)S(1)}, u32[]{:S(2)}, u32[]{:S(2)}) async-start(s32[16,1,256]{2,1,0:T(1,128)} %broadcast_in_dim.12), calls=%async_computation | async-start | bytes 32768 | tf_op jit(solution)/shard_map/all_to_all | solution.py:315
  10.0 0.7 pad_add_fusion.1.place_ref
  10.7 7.5 %all-to-all-done.table_ref.note_ref = s32[16,1,256]{2,1,0:T(1,128)S(1)} async-done(((s32[16,1,256]{2,1,0:T(1,128)}), s32[16,1,256]{2,1,0:T(1,128)S(1)}, u32[]{:S(2)}, u32[]{:S(2)}) %all-to-all-start) | async-done | bytes 16416 | tf_op jit(solution)/shard_map/all_to_all | solution.py:315
  18.2 0.0 copy-start
  18.2 0.0 collective-permute-done.mirror_ref
  18.2 3.2 %shard_map.111 = (bf16[8,2,5,8,1024]{4,3,2,1,0:T(8,128)(2,1)}, bf16[2,128,128]{2,1,0:T(8,128)(2,1)}) custom-call(s32[2]{0:T(128)} %pad_add_fusion.1.place_ref, s32[16,1,256]{2,1,0:T(1,128)S(1)} %all-to-all-done.table_ref.note_ref, s32[16,1,256]{2,1,0:T(1,128)S(1)} %all-to-all-done.table_ref.note_ref, bf16[128,1024]{1,0:T(8,128)(2,1)} %own_ref.1, ...), custom_call_target="tpu_custom_call" | custom-call | tf_op jit(solution)/shard_map/pallas_call | solution.py:318
  21.4 3.6 %all-to-all-start.1 = ((bf16[8,2,5,8,1024]{4,3,2,1,0:T(8,128)(2,1)}), bf16[8,2,5,8,1024]{4,3,2,1,0:T(8,128)(2,1)S(1)}, u32[]{:S(2)}, u32[]{:S(2)}) async-start(bf16[8,2,5,8,1024]{4,3,2,1,0:T(8,128)(2,1)} %get-tuple-element.17), calls=%async_computation.1 | async-start | bytes 2621440 | tf_op jit(solution)/shard_map/all_to_all | solution.py:333
  25.0 0.0 copy-done.8
  25.0 1.9 %collective-permute-start.1 = (bf16[128,1024]{1,0:T(8,128)(2,1)S(1)}, bf16[128,1024]{1,0:T(8,128)(2,1)S(1)}, u32[]{:S(2)}, u32[]{:S(2)}) collective-permute-start(bf16[128,1024]{1,0:T(8,128)(2,1)S(1)} %copy-done.8), channel_id=1, source_target_pairs={{0,4},{1,5},{2,6},{3,7},{4,0},{5,1},{6,2},{7,3},{8,12},{9,13},{10,... | collective-permute-start | bytes 786440 | tf_op jit(solution)/shard_map/ppermute | solution.py:293
  27.6 20.2 %collective-permute-done.1.other_ref = bf16[128,1024]{1,0:T(8,128)(2,1)S(1)} collective-permute-done((bf16[128,1024]{1,0:T(8,128)(2,1)S(1)}, bf16[128,1024]{1,0:T(8,128)(2,1)S(1)}, u32[]{:S(2)}, u32[]{:S(2)}) %collective-permute-start.1) | collective-permute-done | bytes 262176 | tf_op jit(solution)/shard_map/ppermute | solution.py:293
  47.8 3.5 %shard_map.112 = (bf16[256,1024]{1,0:T(8,128)(2,1)}, bf16[128,1024]{1,0:T(8,128)(2,1)}, bf16[128,1024]{1,0:T(8,128)(2,1)}, bf16[128,128]{1,0:T(8,128)(2,1)}) custom-call(bf16[128,1024]{1,0:T(8,128)(2,1)} %cot_ref.1, bf16[128,1024]{1,0:T(8,128)(2,1)S(1)} %collective-permute-done.1.other_ref, s32[1,128]{1,0:T(1,128)} %bitcast.6, bf16[1024,1024]{1,0:T(8,128)(2,1)} %wout_hbm.1), custom_call_target="tpu_custom_call" | custom-call | tf_op jit(solution)/shard_map/pallas_call | solution.py:334
  51.3 0.0 copy-done
  51.3 0.0 all-to-all-done.1.arrived_ref
  51.3 19.8 %shard_map.113 = (bf16[128,1024]{1,0:T(8,128)(2,1)}, bf16[16,400,128]{2,1,0:T(8,128)(2,1)}) custom-call(s32[1]{0:T(128)S(6)} %copy.12.count_ref, bf16[8,2,5,8,1024]{4,3,2,1,0:T(8,128)(2,1)S(1)} %all-to-all-done.1.arrived_ref, bf16[128,128]{1,0:T(8,128)(2,1)} %get-tuple-element.20.order_ref, f32[1,1024]{1,0:T(1,128)} %bitcast.8, ...), custom_call_target="tpu_custom_call" | custom-call | flops 9395240960 | bytes 16777216 | tf_op jit(solution)/shard_map/pallas_call | solution.py:364
  71.2 0.0 copy-start.1
  71.2 5.1 %all-to-all-start.2 = ((bf16[16,400,128]{2,1,0:T(8,128)(2,1)}), bf16[16,400,128]{2,1,0:T(8,128)(2,1)S(1)}, u32[]{:S(2)}, u32[]{:S(2)}) async-start(bf16[16,400,128]{2,1,0:T(8,128)(2,1)} %get-tuple-element.24), calls=%async_computation.2 | async-start | bytes 3276800 | tf_op jit(solution)/shard_map/all_to_all | solution.py:395
  76.3 0.0 copy-done.1
  76.3 2.9 %collective-permute-start.2 = (bf16[256,1024]{1,0:T(8,128)(2,1)S(1)}, bf16[256,1024]{1,0:T(8,128)(2,1)S(1)}, u32[]{:S(2)}, u32[]{:S(2)}) collective-permute-start(bf16[256,1024]{1,0:T(8,128)(2,1)S(1)} %copy-done.1), channel_id=1, source_target_pairs={{0,8},{1,9},{2,10},{3,11},{4,12},{5,13},{6,14},{7,15},{8,0},{9,1},... | collective-permute-start | bytes 1572872 | tf_op jit(solution)/shard_map/ppermute | solution.py:293
  79.2 1.5 collective-permute-start.3
  80.6 57.3 %collective-permute-done.2.rest_1_ = bf16[256,1024]{1,0:T(8,128)(2,1)S(1)} collective-permute-done((bf16[256,1024]{1,0:T(8,128)(2,1)S(1)}, bf16[256,1024]{1,0:T(8,128)(2,1)S(1)}, u32[]{:S(2)}, u32[]{:S(2)}) %collective-permute-start.2) | collective-permute-done | bytes 524320 | tf_op jit(solution)/shard_map/ppermute | solution.py:293
  137.9 0.0 copy-start.2
  137.9 1.6 %collective-permute-start.4 = (bf16[256,1024]{1,0:T(8,128)(2,1)S(1)}, bf16[256,1024]{1,0:T(8,128)(2,1)S(1)}, u32[]{:S(2)}, u32[]{:S(2)}) collective-permute-start(bf16[256,1024]{1,0:T(8,128)(2,1)S(1)} %collective-permute-done.2.rest_1_), channel_id=1, source_target_pairs={{0,2},{1,3},{2,0},{3,1},{4,6},{5,7},{6,4},{7,5},{8,10},{9,11},{10,... | collective-permute-start | bytes 1572872 | tf_op jit(solution)/shard_map/ppermute | solution.py:293
  139.5 0.0 collective-permute-start.5
  139.5 0.5 collective-permute-start.6
  140.0 0.0 collective-permute-done.3.rest_2_
  140.0 0.0 copy-start.3
  140.0 0.1 collective-permute-start.7
  140.1 11.2 %collective-permute-done.4.rest_3_ = bf16[256,1024]{1,0:T(8,128)(2,1)S(1)} collective-permute-done((bf16[256,1024]{1,0:T(8,128)(2,1)S(1)}, bf16[256,1024]{1,0:T(8,128)(2,1)S(1)}, u32[]{:S(2)}, u32[]{:S(2)}) %collective-permute-start.4) | collective-permute-done | bytes 524320 | tf_op jit(solution)/shard_map/ppermute | solution.py:293
  151.3 0.0 copy-start.4
  151.3 0.0 collective-permute-start.8
  151.3 0.0 collective-permute-done.5.rest_4_
  151.3 0.0 copy-start.5
  151.3 0.0 collective-permute-done.7.rest_6_
  151.3 0.0 copy-start.7
  151.3 0.0 collective-permute-done.6.rest_5_
  151.3 0.8 copy-done.4
  152.1 0.1 copy-done.5
  152.2 0.2 copy-done.7
  152.4 0.8 copy-done.6
  153.2 0.1 collective-permute-done.8.rest_7_
  153.3 0.0 all-to-all-done.2.back_ref
  153.3 0.0 copy-done.2
  153.3 0.0 copy-done.3
  153.3 4.1 %shard_map.114 = (bf16[128,1024]{1,0:T(8,128)(2,1)}, f32[64,1024]{1,0:T(8,128)}, f32[8,128]{1,0:T(8,128)}) custom-call(s32[2]{0:T(128)} %pad_add_fusion.1.place_ref, s32[16,1,256]{2,1,0:T(1,128)} %copy-done, bf16[16,400,128]{2,1,0:T(8,128)(2,1)S(1)} %all-to-all-done.2.back_ref, bf16[2,128,128]{2,1,0:T(8,128)(2,1)} %get-tuple-element.25.one_ref, ...), custom_call_target="tpu_custom_call" | custom-call | tf_op jit(solution)/shard_map/pallas_call | solution.py:407
  (1 shorter events, 0.0 us)
Async XLA Ops:
  0.6 17.6 %collective-permute-start = (bf16[128,1024]{1,0:T(8,128)(2,1)}, bf16[128,1024]{1,0:T(8,128)(2,1)S(1)}, u32[]{:S(2)}, u32[]{:S(2)}) collective-permute-start(bf16[128,1024]{1,0:T(8,128)(2,1)} %own_ref.1), channel_id=1, source_target_pairs={{0,8},{1,9},{2,10},{3,11},{4,12},{5,13},{6,14},{7,15},{8,0},{9,1},... | collective-permute-start | bytes 786440 | tf_op jit(solution)/shard_map/ppermute | solution.py:293
  5.4 19.5 %copy-start.8 = (bf16[128,1024]{1,0:T(8,128)(2,1)S(1)}, bf16[128,1024]{1,0:T(8,128)(2,1)}, u32[]{:S(2)}) copy-start(bf16[128,1024]{1,0:T(8,128)(2,1)} %cot_ref.1) | copy-start | bytes 786436
  6.1 12.2 %all-to-all-start = ((s32[16,1,256]{2,1,0:T(1,128)}), s32[16,1,256]{2,1,0:T(1,128)S(1)}, u32[]{:S(2)}, u32[]{:S(2)}) async-start(s32[16,1,256]{2,1,0:T(1,128)} %broadcast_in_dim.12), calls=%async_computation | async-start | bytes 32768 | tf_op jit(solution)/shard_map/all_to_all | solution.py:315
  18.2 33.1 %copy-start = (s32[16,1,256]{2,1,0:T(1,128)}, s32[16,1,256]{2,1,0:T(1,128)S(1)}, u32[]{:S(2)}) copy-start(s32[16,1,256]{2,1,0:T(1,128)S(1)} %all-to-all-done.table_ref.note_ref) | copy-start | bytes 49156
  21.4 29.9 %all-to-all-start.1 = ((bf16[8,2,5,8,1024]{4,3,2,1,0:T(8,128)(2,1)}), bf16[8,2,5,8,1024]{4,3,2,1,0:T(8,128)(2,1)S(1)}, u32[]{:S(2)}, u32[]{:S(2)}) async-start(bf16[8,2,5,8,1024]{4,3,2,1,0:T(8,128)(2,1)} %get-tuple-element.17), calls=%async_computation.1 | async-start | bytes 2621440 | tf_op jit(solution)/shard_map/all_to_all | solution.py:333
  25.0 22.8 %collective-permute-start.1 = (bf16[128,1024]{1,0:T(8,128)(2,1)S(1)}, bf16[128,1024]{1,0:T(8,128)(2,1)S(1)}, u32[]{:S(2)}, u32[]{:S(2)}) collective-permute-start(bf16[128,1024]{1,0:T(8,128)(2,1)S(1)} %copy-done.8), channel_id=1, source_target_pairs={{0,4},{1,5},{2,6},{3,7},{4,0},{5,1},{6,2},{7,3},{8,12},{9,13},{10,... | collective-permute-start | bytes 786440 | tf_op jit(solution)/shard_map/ppermute | solution.py:293
  71.2 5.1 %copy-start.1 = (bf16[256,1024]{1,0:T(8,128)(2,1)S(1)}, bf16[256,1024]{1,0:T(8,128)(2,1)}, u32[]{:S(2)}) copy-start(bf16[256,1024]{1,0:T(8,128)(2,1)} %get-tuple-element.26.rest_0_) | copy-start | bytes 1572868
  71.2 82.1 %all-to-all-start.2 = ((bf16[16,400,128]{2,1,0:T(8,128)(2,1)}), bf16[16,400,128]{2,1,0:T(8,128)(2,1)S(1)}, u32[]{:S(2)}, u32[]{:S(2)}) async-start(bf16[16,400,128]{2,1,0:T(8,128)(2,1)} %get-tuple-element.24), calls=%async_computation.2 | async-start | bytes 3276800 | tf_op jit(solution)/shard_map/all_to_all | solution.py:395
  76.3 61.6 %collective-permute-start.2 = (bf16[256,1024]{1,0:T(8,128)(2,1)S(1)}, bf16[256,1024]{1,0:T(8,128)(2,1)S(1)}, u32[]{:S(2)}, u32[]{:S(2)}) collective-permute-start(bf16[256,1024]{1,0:T(8,128)(2,1)S(1)} %copy-done.1), channel_id=1, source_target_pairs={{0,8},{1,9},{2,10},{3,11},{4,12},{5,13},{6,14},{7,15},{8,0},{9,1},... | collective-permute-start | bytes 1572872 | tf_op jit(solution)/shard_map/ppermute | solution.py:293
  79.2 60.8 %collective-permute-start.3 = (bf16[256,1024]{1,0:T(8,128)(2,1)S(1)}, bf16[256,1024]{1,0:T(8,128)(2,1)S(1)}, u32[]{:S(2)}, u32[]{:S(2)}) collective-permute-start(bf16[256,1024]{1,0:T(8,128)(2,1)S(1)} %copy-done.1), channel_id=1, source_target_pairs={{0,2},{1,3},{2,0},{3,1},{4,6},{5,7},{6,4},{7,5},{8,10},{9,11},{10,... | collective-permute-start | bytes 1572872 | tf_op jit(solution)/shard_map/ppermute | solution.py:293
  137.9 15.4 %copy-start.2 = (bf16[256,1024]{1,0:T(8,128)(2,1)}, bf16[256,1024]{1,0:T(8,128)(2,1)S(1)}, u32[]{:S(2)}) copy-start(bf16[256,1024]{1,0:T(8,128)(2,1)S(1)} %collective-permute-done.2.rest_1_) | copy-start | bytes 1572868
  137.9 13.4 %collective-permute-start.4 = (bf16[256,1024]{1,0:T(8,128)(2,1)S(1)}, bf16[256,1024]{1,0:T(8,128)(2,1)S(1)}, u32[]{:S(2)}, u32[]{:S(2)}) collective-permute-start(bf16[256,1024]{1,0:T(8,128)(2,1)S(1)} %collective-permute-done.2.rest_1_), channel_id=1, source_target_pairs={{0,2},{1,3},{2,0},{3,1},{4,6},{5,7},{6,4},{7,5},{8,10},{9,11},{10,... | collective-permute-start | bytes 1572872 | tf_op jit(solution)/shard_map/ppermute | solution.py:293
  139.5 11.8 %collective-permute-start.5 = (bf16[256,1024]{1,0:T(8,128)(2,1)S(1)}, bf16[256,1024]{1,0:T(8,128)(2,1)S(1)}, u32[]{:S(2)}, u32[]{:S(2)}) collective-permute-start(bf16[256,1024]{1,0:T(8,128)(2,1)S(1)} %copy-done.1), channel_id=1, source_target_pairs={{0,1},{1,0},{2,3},{3,2},{4,5},{5,4},{6,7},{7,6},{8,9},{9,8},{10,11... | collective-permute-start | bytes 1572872 | tf_op jit(solution)/shard_map/ppermute | solution.py:293
  139.5 11.8 %collective-permute-start.6 = (bf16[256,1024]{1,0:T(8,128)(2,1)S(1)}, bf16[256,1024]{1,0:T(8,128)(2,1)S(1)}, u32[]{:S(2)}, u32[]{:S(2)}) collective-permute-start(bf16[256,1024]{1,0:T(8,128)(2,1)S(1)} %collective-permute-done.2.rest_1_), channel_id=1, source_target_pairs={{0,1},{1,0},{2,3},{3,2},{4,5},{5,4},{6,7},{7,6},{8,9},{9,8},{10,11... | collective-permute-start | bytes 1572872 | tf_op jit(solution)/shard_map/ppermute | solution.py:293
  140.0 13.3 %copy-start.3 = (bf16[256,1024]{1,0:T(8,128)(2,1)}, bf16[256,1024]{1,0:T(8,128)(2,1)S(1)}, u32[]{:S(2)}) copy-start(bf16[256,1024]{1,0:T(8,128)(2,1)S(1)} %collective-permute-done.3.rest_2_) | copy-start | bytes 1572868
  140.0 11.3 %collective-permute-start.7 = (bf16[256,1024]{1,0:T(8,128)(2,1)S(1)}, bf16[256,1024]{1,0:T(8,128)(2,1)S(1)}, u32[]{:S(2)}, u32[]{:S(2)}) collective-permute-start(bf16[256,1024]{1,0:T(8,128)(2,1)S(1)} %collective-permute-done.3.rest_2_), channel_id=1, source_target_pairs={{0,1},{1,0},{2,3},{3,2},{4,5},{5,4},{6,7},{7,6},{8,9},{9,8},{10,11... | collective-permute-start | bytes 1572872 | tf_op jit(solution)/shard_map/ppermute | solution.py:293
  151.3 0.8 copy-start.4
  151.3 2.0 %collective-permute-start.8 = (bf16[256,1024]{1,0:T(8,128)(2,1)S(1)}, bf16[256,1024]{1,0:T(8,128)(2,1)}, u32[]{:S(2)}, u32[]{:S(2)}) collective-permute-start(bf16[256,1024]{1,0:T(8,128)(2,1)S(1)} %collective-permute-done.4.rest_3_), channel_id=1, source_target_pairs={{0,1},{1,0},{2,3},{3,2},{4,5},{5,4},{6,7},{7,6},{8,9},{9,8},{10,11... | collective-permute-start | bytes 1572872 | tf_op jit(solution)/shard_map/ppermute | solution.py:293
  151.3 0.9 copy-start.5
  151.3 1.1 copy-start.7
  152.4 0.8 copy-start.6

commit v6 on v5

--- a/solution.py
+++ b/solution.py
@@ -50,6 +50,16 @@
     n = col.shape[0]
     wide = jnp.broadcast_to(col.astype(F32), (n, n))
     return jnp.transpose(wide)[:1, :].astype(jnp.int32)
+
+
+def note_kernel(list_ref, perm_ref, out_ref):
+    n_dev, rows = out_ref.shape[0], perm_ref.shape[1]
+    lane = iota((1, rows), 1)
+    listed = jnp.zeros((1, rows), jnp.int32)
+    for slot in range(list_ref.shape[1]):
+        listed = jnp.where(lane == slot, list_ref[0, slot], listed)
+    both = jnp.concatenate([perm_ref[...], listed], axis=1)
+    out_ref[...] = jnp.broadcast_to(both[None], (n_dev, 1, 2 * rows))
 
 
 def pack_kernel(n_dev, slots, per_peer, place_ref, table_ref, note_ref, own_ref, mirror_ref, msg_ref, one_ref, sorted_ref):
@@ -308,8 +318,12 @@
     lane_blocks = width // LANES
     feats = width // n_dev
     place = jnp.stack([me // half, me % half]).astype(jnp.int32)
-    note = jnp.concatenate([hilbert_perm, jnp.pad(neighbors[0], (0, rows - slots))])
-    note = jnp.broadcast_to(note[None, None], (n_dev, 1, 2 * rows))
+    note = pl.pallas_call(
+        note_kernel,
+        out_shape=jax.ShapeDtypeStruct((n_dev, 1, 2 * rows), jnp.int32),
+        in_specs=[SM, VM],
+        out_specs=VM,
+    )(neighbors, hilbert_perm[None])
     mirror = swap(raster_tokens, half)
     other = swap(cotangent, half // 2)
     note = lax.all_to_all(note, "ctx", 0, 0, tiled=True)

time: 158 us -> 158 us (level)
  transfers between devices with their start and end apart: 12 -> 12, of which waited for: 5 -> 5; matrix products, arithmetic and copies ran while one was open for 1% -> 0% of each run, Pallas kernels for 2% -> 3%
where the time goes in v6:
time: 158 us
  waiting for transfers between devices  96.2 us (61%)
  Pallas kernels  32 us (20%)
  starting transfers between devices  25.2 us (16%)
  local copies, waits for them, and re-layouts  1.91 us (1%)
  between operations  1.58 us (1%)
    ppermute x9, waiting for transfers between devices, swap(): return lax.ppermute(block, 'ctx', [(i, i ^ mask) for i in range(n_dev)])  88.8 us
    pallas_call x1, Pallas kernels, per_device(): pl.pallas_call(functools.partial(main_kernel, fits), out_shape=(jax.Shape...  19.8 us
    ppermute x9, starting transfers between devices, swap(): return lax.ppermute(block, 'ctx', [(i, i ^ mask) for i in range(n_dev)])  12.6 us
    all_to_all x1, waiting for transfers between devices, per_device(): note = lax.all_to_all(note, 'ctx', 0, 0, tiled=True)  7.42 us
    all_to_all x1, starting transfers between devices, per_device(): back = lax.all_to_all(ret, 'ctx', 0, 0, tiled=True)  5.07 us
    pallas_call x1, Pallas kernels, per_device(): pl.pallas_call(functools.partial(finish_kernel, n_dev, slots, masks, norm...  4.07 us
    all_to_all x1, starting transfers between devices, per_device(): note = lax.all_to_all(note, 'ctx', 0, 0, tiled=True)  3.91 us
    all_to_all x1, starting transfers between devices, per_device(): lax.all_to_all(msg, 'ctx', 0, 0, tiled=True, axis_index_groups=halves)  3.57 us
  transfers between devices with their start and end apart: 12, of which 5 were waited for; matrix products, arithmetic and copies ran while one was open for 0% of the time, Pallas kernels for 3%

profile of v6, /device:TPU:0, one launch (start us, length us, event | category | flops | bytes accessed | tf_op | source)
XLA Modules:
  0.0 157.5 jit_solution(12991873373886697645)
XLA Ops:
  0.6 4.1 %collective-permute-start = (bf16[128,1024]{1,0:T(8,128)(2,1)}, bf16[128,1024]{1,0:T(8,128)(2,1)S(1)}, u32[]{:S(2)}, u32[]{:S(2)}) collective-permute-start(bf16[128,1024]{1,0:T(8,128)(2,1)} %own_ref.1), channel_id=1, source_target_pairs={{0,8},{1,9},{2,10},{3,11},{4,12},{5,13},{6,14},{7,15},{8,0},{9,1},... | collective-permute-start | bytes 786440 | tf_op jit(solution)/shard_map/ppermute | solution.py:303
  4.8 0.0 copy-start.8
  4.8 1.4 shard_map.111
  6.2 3.9 %all-to-all-start = ((s32[16,1,256]{2,1,0:T(1,128)}), s32[16,1,256]{2,1,0:T(1,128)S(1)}, u32[]{:S(2)}, u32[]{:S(2)}) async-start(s32[16,1,256]{2,1,0:T(1,128)} %shard_map.111), calls=%async_computation | async-start | bytes 32768 | tf_op jit(solution)/shard_map/all_to_all | solution.py:329
  10.1 0.7 pad_add_fusion.place_ref
  10.8 7.4 %all-to-all-done.table_ref.note_ref = s32[16,1,256]{2,1,0:T(1,128)S(1)} async-done(((s32[16,1,256]{2,1,0:T(1,128)}), s32[16,1,256]{2,1,0:T(1,128)S(1)}, u32[]{:S(2)}, u32[]{:S(2)}) %all-to-all-start) | async-done | bytes 16416 | tf_op jit(solution)/shard_map/all_to_all | solution.py:329
  18.2 0.0 copy-start
  18.2 0.0 collective-permute-done.mirror_ref
  18.2 3.2 %shard_map.112 = (bf16[8,2,5,8,1024]{4,3,2,1,0:T(8,128)(2,1)}, bf16[2,128,128]{2,1,0:T(8,128)(2,1)}) custom-call(s32[2]{0:T(128)} %pad_add_fusion.place_ref, s32[16,1,256]{2,1,0:T(1,128)S(1)} %all-to-all-done.table_ref.note_ref, s32[16,1,256]{2,1,0:T(1,128)S(1)} %all-to-all-done.table_ref.note_ref, bf16[128,1024]{1,0:T(8,128)(2,1)} %own_ref.1, ...), custom_call_target="tpu_custom_call" | custom-call | tf_op jit(solution)/shard_map/pallas_call | solution.py:332
  21.4 3.6 %all-to-all-start.1 = ((bf16[8,2,5,8,1024]{4,3,2,1,0:T(8,128)(2,1)}), bf16[8,2,5,8,1024]{4,3,2,1,0:T(8,128)(2,1)S(1)}, u32[]{:S(2)}, u32[]{:S(2)}) async-start(bf16[8,2,5,8,1024]{4,3,2,1,0:T(8,128)(2,1)} %get-tuple-element.17), calls=%async_computation.1 | async-start | bytes 2621440 | tf_op jit(solution)/shard_map/all_to_all | solution.py:347
  25.0 0.0 copy-done.8
  25.0 1.9 %collective-permute-start.1 = (bf16[128,1024]{1,0:T(8,128)(2,1)S(1)}, bf16[128,1024]{1,0:T(8,128)(2,1)S(1)}, u32[]{:S(2)}, u32[]{:S(2)}) collective-permute-start(bf16[128,1024]{1,0:T(8,128)(2,1)S(1)} %copy-done.8), channel_id=1, source_target_pairs={{0,4},{1,5},{2,6},{3,7},{4,0},{5,1},{6,2},{7,3},{8,12},{9,13},{10,... | collective-permute-start | bytes 786440 | tf_op jit(solution)/shard_map/ppermute | solution.py:303
  27.6 20.2 %collective-permute-done.1.other_ref = bf16[128,1024]{1,0:T(8,128)(2,1)S(1)} collective-permute-done((bf16[128,1024]{1,0:T(8,128)(2,1)S(1)}, bf16[128,1024]{1,0:T(8,128)(2,1)S(1)}, u32[]{:S(2)}, u32[]{:S(2)}) %collective-permute-start.1) | collective-permute-done | bytes 262176 | tf_op jit(solution)/shard_map/ppermute | solution.py:303
  47.8 3.5 %shard_map.113 = (bf16[256,1024]{1,0:T(8,128)(2,1)}, bf16[128,1024]{1,0:T(8,128)(2,1)}, bf16[128,1024]{1,0:T(8,128)(2,1)}, bf16[128,128]{1,0:T(8,128)(2,1)}) custom-call(bf16[128,1024]{1,0:T(8,128)(2,1)} %cot_ref.1, bf16[128,1024]{1,0:T(8,128)(2,1)S(1)} %collective-permute-done.1.other_ref, s32[1,128]{1,0:T(1,128)} %bitcast.6, bf16[1024,1024]{1,0:T(8,128)(2,1)} %wout_hbm.1), custom_call_target="tpu_custom_call" | custom-call | tf_op jit(solution)/shard_map/pallas_call | solution.py:348
  51.3 0.0 copy-done
  51.3 0.0 all-to-all-done.1.arrived_ref
  51.3 19.8 %shard_map.114 = (bf16[128,1024]{1,0:T(8,128)(2,1)}, bf16[16,400,128]{2,1,0:T(8,128)(2,1)}) custom-call(s32[1]{0:T(128)S(6)} %copy.12.count_ref, bf16[8,2,5,8,1024]{4,3,2,1,0:T(8,128)(2,1)S(1)} %all-to-all-done.1.arrived_ref, bf16[128,128]{1,0:T(8,128)(2,1)} %get-tuple-element.20.order_ref, f32[1,1024]{1,0:T(1,128)} %bitcast.7, ...), custom_call_target="tpu_custom_call" | custom-call | flops 9395240960 | bytes 16777216 | tf_op jit(solution)/shard_map/pallas_call | solution.py:378
  71.2 0.0 copy-start.1
  71.2 5.1 %all-to-all-start.2 = ((bf16[16,400,128]{2,1,0:T(8,128)(2,1)}), bf16[16,400,128]{2,1,0:T(8,128)(2,1)S(1)}, u32[]{:S(2)}, u32[]{:S(2)}) async-start(bf16[16,400,128]{2,1,0:T(8,128)(2,1)} %get-tuple-element.24), calls=%async_computation.2 | async-start | bytes 3276800 | tf_op jit(solution)/shard_map/all_to_all | solution.py:409
  76.3 0.0 copy-done.1
  76.3 2.9 %collective-permute-start.2 = (bf16[256,1024]{1,0:T(8,128)(2,1)S(1)}, bf16[256,1024]{1,0:T(8,128)(2,1)S(1)}, u32[]{:S(2)}, u32[]{:S(2)}) collective-permute-start(bf16[256,1024]{1,0:T(8,128)(2,1)S(1)} %copy-done.1), channel_id=1, source_target_pairs={{0,8},{1,9},{2,10},{3,11},{4,12},{5,13},{6,14},{7,15},{8,0},{9,1},... | collective-permute-start | bytes 1572872 | tf_op jit(solution)/shard_map/ppermute | solution.py:303
  79.2 1.5 collective-permute-start.3
  80.6 57.3 %collective-permute-done.2.rest_1_ = bf16[256,1024]{1,0:T(8,128)(2,1)S(1)} collective-permute-done((bf16[256,1024]{1,0:T(8,128)(2,1)S(1)}, bf16[256,1024]{1,0:T(8,128)(2,1)S(1)}, u32[]{:S(2)}, u32[]{:S(2)}) %collective-permute-start.2) | collective-permute-done | bytes 524320 | tf_op jit(solution)/shard_map/ppermute | solution.py:303
  137.9 0.0 copy-start.2
  137.9 1.6 %collective-permute-start.4 = (bf16[256,1024]{1,0:T(8,128)(2,1)S(1)}, bf16[256,1024]{1,0:T(8,128)(2,1)S(1)}, u32[]{:S(2)}, u32[]{:S(2)}) collective-permute-start(bf16[256,1024]{1,0:T(8,128)(2,1)S(1)} %collective-permute-done.2.rest_1_), channel_id=1, source_target_pairs={{0,2},{1,3},{2,0},{3,1},{4,6},{5,7},{6,4},{7,5},{8,10},{9,11},{10,... | collective-permute-start | bytes 1572872 | tf_op jit(solution)/shard_map/ppermute | solution.py:303
  139.5 0.0 collective-permute-start.5
  139.5 0.5 collective-permute-start.6
  140.0 0.0 collective-permute-done.3.rest_2_
  140.0 0.0 copy-start.3
  140.0 0.1 collective-permute-start.7
  140.1 11.2 %collective-permute-done.4.rest_3_ = bf16[256,1024]{1,0:T(8,128)(2,1)S(1)} collective-permute-done((bf16[256,1024]{1,0:T(8,128)(2,1)S(1)}, bf16[256,1024]{1,0:T(8,128)(2,1)S(1)}, u32[]{:S(2)}, u32[]{:S(2)}) %collective-permute-start.4) | collective-permute-done | bytes 524320 | tf_op jit(solution)/shard_map/ppermute | solution.py:303
  151.3 0.0 copy-start.4
  151.3 0.0 collective-permute-start.8
  151.3 0.0 collective-permute-done.5.rest_4_
  151.3 0.0 copy-start.5
  151.3 0.0 collective-permute-done.7.rest_6_
  151.3 0.0 copy-start.7
  151.3 0.0 collective-permute-done.6.rest_5_
  151.3 0.8 copy-done.4
  152.1 0.1 copy-done.5
  152.2 0.2 copy-done.7
  152.4 0.0 copy-start.6
  152.4 0.8 copy-done.6
  153.2 0.1 collective-permute-done.8.rest_7_
  153.3 0.0 all-to-all-done.2.back_ref
  153.3 0.0 copy-done.2
  153.3 0.0 copy-done.3
  153.3 4.1 %shard_map.115 = (bf16[128,1024]{1,0:T(8,128)(2,1)}, f32[64,1024]{1,0:T(8,128)}, f32[8,128]{1,0:T(8,128)}) custom-call(s32[2]{0:T(128)} %pad_add_fusion.place_ref, s32[16,1,256]{2,1,0:T(1,128)} %copy-done, bf16[16,400,128]{2,1,0:T(8,128)(2,1)S(1)} %all-to-all-done.2.back_ref, bf16[2,128,128]{2,1,0:T(8,128)(2,1)} %get-tuple-element.25.one_ref, ...), custom_call_target="tpu_custom_call" | custom-call | tf_op jit(solution)/shard_map/pallas_call | solution.py:421
Async XLA Ops:
  0.6 17.6 %collective-permute-start = (bf16[128,1024]{1,0:T(8,128)(2,1)}, bf16[128,1024]{1,0:T(8,128)(2,1)S(1)}, u32[]{:S(2)}, u32[]{:S(2)}) collective-permute-start(bf16[128,1024]{1,0:T(8,128)(2,1)} %own_ref.1), channel_id=1, source_target_pairs={{0,8},{1,9},{2,10},{3,11},{4,12},{5,13},{6,14},{7,15},{8,0},{9,1},... | collective-permute-start | bytes 786440 | tf_op jit(solution)/shard_map/ppermute | solution.py:303
  4.8 20.2 %copy-start.8 = (bf16[128,1024]{1,0:T(8,128)(2,1)S(1)}, bf16[128,1024]{1,0:T(8,128)(2,1)}, u32[]{:S(2)}) copy-start(bf16[128,1024]{1,0:T(8,128)(2,1)} %cot_ref.1) | copy-start | bytes 786436
  6.2 12.0 %all-to-all-start = ((s32[16,1,256]{2,1,0:T(1,128)}), s32[16,1,256]{2,1,0:T(1,128)S(1)}, u32[]{:S(2)}, u32[]{:S(2)}) async-start(s32[16,1,256]{2,1,0:T(1,128)} %shard_map.111), calls=%async_computation | async-start | bytes 32768 | tf_op jit(solution)/shard_map/all_to_all | solution.py:329
  18.2 33.1 %copy-start = (s32[16,1,256]{2,1,0:T(1,128)}, s32[16,1,256]{2,1,0:T(1,128)S(1)}, u32[]{:S(2)}) copy-start(s32[16,1,256]{2,1,0:T(1,128)S(1)} %all-to-all-done.table_ref.note_ref) | copy-start | bytes 49156
  21.4 29.9 %all-to-all-start.1 = ((bf16[8,2,5,8,1024]{4,3,2,1,0:T(8,128)(2,1)}), bf16[8,2,5,8,1024]{4,3,2,1,0:T(8,128)(2,1)S(1)}, u32[]{:S(2)}, u32[]{:S(2)}) async-start(bf16[8,2,5,8,1024]{4,3,2,1,0:T(8,128)(2,1)} %get-tuple-element.17), calls=%async_computation.1 | async-start | bytes 2621440 | tf_op jit(solution)/shard_map/all_to_all | solution.py:347
  25.0 22.8 %collective-permute-start.1 = (bf16[128,1024]{1,0:T(8,128)(2,1)S(1)}, bf16[128,1024]{1,0:T(8,128)(2,1)S(1)}, u32[]{:S(2)}, u32[]{:S(2)}) collective-permute-start(bf16[128,1024]{1,0:T(8,128)(2,1)S(1)} %copy-done.8), channel_id=1, source_target_pairs={{0,4},{1,5},{2,6},{3,7},{4,0},{5,1},{6,2},{7,3},{8,12},{9,13},{10,... | collective-permute-start | bytes 786440 | tf_op jit(solution)/shard_map/ppermute | solution.py:303
  71.2 5.1 %copy-start.1 = (bf16[256,1024]{1,0:T(8,128)(2,1)S(1)}, bf16[256,1024]{1,0:T(8,128)(2,1)}, u32[]{:S(2)}) copy-start(bf16[256,1024]{1,0:T(8,128)(2,1)} %get-tuple-element.26.rest_0_) | copy-start | bytes 1572868
  71.2 82.1 %all-to-all-start.2 = ((bf16[16,400,128]{2,1,0:T(8,128)(2,1)}), bf16[16,400,128]{2,1,0:T(8,128)(2,1)S(1)}, u32[]{:S(2)}, u32[]{:S(2)}) async-start(bf16[16,400,128]{2,1,0:T(8,128)(2,1)} %get-tuple-element.24), calls=%async_computation.2 | async-start | bytes 3276800 | tf_op jit(solution)/shard_map/all_to_all | solution.py:409
  76.3 61.6 %collective-permute-start.2 = (bf16[256,1024]{1,0:T(8,128)(2,1)S(1)}, bf16[256,1024]{1,0:T(8,128)(2,1)S(1)}, u32[]{:S(2)}, u32[]{:S(2)}) collective-permute-start(bf16[256,1024]{1,0:T(8,128)(2,1)S(1)} %copy-done.1), channel_id=1, source_target_pairs={{0,8},{1,9},{2,10},{3,11},{4,12},{5,13},{6,14},{7,15},{8,0},{9,1},... | collective-permute-start | bytes 1572872 | tf_op jit(solution)/shard_map/ppermute | solution.py:303
  79.2 60.8 %collective-permute-start.3 = (bf16[256,1024]{1,0:T(8,128)(2,1)S(1)}, bf16[256,1024]{1,0:T(8,128)(2,1)S(1)}, u32[]{:S(2)}, u32[]{:S(2)}) collective-permute-start(bf16[256,1024]{1,0:T(8,128)(2,1)S(1)} %copy-done.1), channel_id=1, source_target_pairs={{0,2},{1,3},{2,0},{3,1},{4,6},{5,7},{6,4},{7,5},{8,10},{9,11},{10,... | collective-permute-start | bytes 1572872 | tf_op jit(solution)/shard_map/ppermute | solution.py:303
  137.9 15.4 %copy-start.2 = (bf16[256,1024]{1,0:T(8,128)(2,1)}, bf16[256,1024]{1,0:T(8,128)(2,1)S(1)}, u32[]{:S(2)}) copy-start(bf16[256,1024]{1,0:T(8,128)(2,1)S(1)} %collective-permute-done.2.rest_1_) | copy-start | bytes 1572868
  137.9 13.4 %collective-permute-start.4 = (bf16[256,1024]{1,0:T(8,128)(2,1)S(1)}, bf16[256,1024]{1,0:T(8,128)(2,1)S(1)}, u32[]{:S(2)}, u32[]{:S(2)}) collective-permute-start(bf16[256,1024]{1,0:T(8,128)(2,1)S(1)} %collective-permute-done.2.rest_1_), channel_id=1, source_target_pairs={{0,2},{1,3},{2,0},{3,1},{4,6},{5,7},{6,4},{7,5},{8,10},{9,11},{10,... | collective-permute-start | bytes 1572872 | tf_op jit(solution)/shard_map/ppermute | solution.py:303
  139.5 11.8 %collective-permute-start.5 = (bf16[256,1024]{1,0:T(8,128)(2,1)S(1)}, bf16[256,1024]{1,0:T(8,128)(2,1)S(1)}, u32[]{:S(2)}, u32[]{:S(2)}) collective-permute-start(bf16[256,1024]{1,0:T(8,128)(2,1)S(1)} %copy-done.1), channel_id=1, source_target_pairs={{0,1},{1,0},{2,3},{3,2},{4,5},{5,4},{6,7},{7,6},{8,9},{9,8},{10,11... | collective-permute-start | bytes 1572872 | tf_op jit(solution)/shard_map/ppermute | solution.py:303
  139.5 11.8 %collective-permute-start.6 = (bf16[256,1024]{1,0:T(8,128)(2,1)S(1)}, bf16[256,1024]{1,0:T(8,128)(2,1)S(1)}, u32[]{:S(2)}, u32[]{:S(2)}) collective-permute-start(bf16[256,1024]{1,0:T(8,128)(2,1)S(1)} %collective-permute-done.2.rest_1_), channel_id=1, source_target_pairs={{0,1},{1,0},{2,3},{3,2},{4,5},{5,4},{6,7},{7,6},{8,9},{9,8},{10,11... | collective-permute-start | bytes 1572872 | tf_op jit(solution)/shard_map/ppermute | solution.py:303
  140.0 13.3 %copy-start.3 = (bf16[256,1024]{1,0:T(8,128)(2,1)}, bf16[256,1024]{1,0:T(8,128)(2,1)S(1)}, u32[]{:S(2)}) copy-start(bf16[256,1024]{1,0:T(8,128)(2,1)S(1)} %collective-permute-done.3.rest_2_) | copy-start | bytes 1572868
  140.0 11.3 %collective-permute-start.7 = (bf16[256,1024]{1,0:T(8,128)(2,1)S(1)}, bf16[256,1024]{1,0:T(8,128)(2,1)S(1)}, u32[]{:S(2)}, u32[]{:S(2)}) collective-permute-start(bf16[256,1024]{1,0:T(8,128)(2,1)S(1)} %collective-permute-done.3.rest_2_), channel_id=1, source_target_pairs={{0,1},{1,0},{2,3},{3,2},{4,5},{5,4},{6,7},{7,6},{8,9},{9,8},{10,11... | collective-permute-start | bytes 1572872 | tf_op jit(solution)/shard_map/ppermute | solution.py:303
  151.3 0.8 copy-start.4
  151.3 2.0 %collective-permute-start.8 = (bf16[256,1024]{1,0:T(8,128)(2,1)S(1)}, bf16[256,1024]{1,0:T(8,128)(2,1)}, u32[]{:S(2)}, u32[]{:S(2)}) collective-permute-start(bf16[256,1024]{1,0:T(8,128)(2,1)S(1)} %collective-permute-done.4.rest_3_), channel_id=1, source_target_pairs={{0,1},{1,0},{2,3},{3,2},{4,5},{5,4},{6,7},{7,6},{8,9},{9,8},{10,11... | collective-permute-start | bytes 1572872 | tf_op jit(solution)/shard_map/ppermute | solution.py:303
  151.3 0.9 copy-start.5
  151.3 1.1 copy-start.7
  152.4 0.8 copy-start.6
